TPU v7x, 32 devices: a whole 2x2x4 slice. The times are simulated.
32 devices in a mesh: groups: 2 (over y), gx: 16 (over z, x, core).
Axes of the slice: x: 2, y: 2, z: 4, core: 2. Of those that a mesh axis runs over, the one named last changes fastest.
Arguments:
- states: float32 [2, 4, 128, 512], P(None, 'groups', 'gx'), parts along dimension 1, may hold values from -5 to 5
- pre_acts: bfloat16 [2, 3, 256, 48, 512], P(None, None, ('groups', 'gx')), parts along dimension 2, may hold values from -6 to 6
- cotangent: float32 [4, 128, 512], P('groups', 'gx'), parts along dimension 0, may hold values from -12 to 12
- weight_in: bfloat16 [9, 48, 2], replicated, may hold values from -1.5 to 1.5
- weight_second: bfloat16 [9, 48, 48], replicated, may hold values from -0.3125 to 0.3125
- weight_third: bfloat16 [9, 48, 48], replicated, may hold values from -0.3125 to 0.3125
- weight_out: bfloat16 [9, 2, 48], replicated, may hold values from -0.3125 to 0.3125
Outputs:
- state_adjoint: float32 [4, 128, 512], P('groups', 'gx'), parts along dimension 0
- grad_in: float32 [18, 48, 2], P('groups'), parts along dimension 0
- grad_second: float32 [18, 48, 48], P('groups'), parts along dimension 0
- grad_third: float32 [18, 48, 48], P('groups'), parts along dimension 0
- grad_out: float32 [18, 2, 48], P('groups'), parts along dimension 0
There are 2 independent parts, one for each index of `groups`. A program takes and returns all parts, laid end to end along the dimension named above; an argument that names none is the same for every part. Nothing has to cross between parts.
All inputs are finite; a program needn't handle non-finite values.
Results may differ from a plain program's by a relative error of at most 0.0065.
Values may be sent and summed in bfloat16 or wider, within the bound.
No kernel may reach another device: no remote copies, remote signals or barrier semaphores. Data moves between devices by JAX's collectives and lax.ppermute only.
A program may use at most 64 MiB of HBM per device.

v0:
```python
import math

import jax
import jax.numpy as jnp
from jax import lax
from jax.sharding import PartitionSpec as P

step_factor = 0.25
viscosity = 0.4


def extended(cells, sides, width):
    for axis, dim in sides:
        count = lax.axis_size(axis)
        head = lax.slice_in_dim(cells, 0, width, axis=dim)
        tail = lax.slice_in_dim(cells, cells.shape[dim] - width, cells.shape[dim], axis=dim)
        cells = jnp.concatenate(
            [
                lax.ppermute(tail, axis, [(i, (i + 1) % count) for i in range(count)]),
                cells,
                lax.ppermute(head, axis, [((i + 1) % count, i) for i in range(count)]),
            ],
            axis=dim,
        )
    return cells


def trim_rows(values, rim_width):
    return values[:, rim_width : values.shape[1] - rim_width]


def trim_lead(values, rim_width):
    return values[rim_width : values.shape[0] - rim_width]


def half_valid(state_ext):
    row_count = state_ext.shape[1] - 2
    row_speed = state_ext[0]
    col_speed = state_ext[1][1 : row_count + 1]
    face_speed = 0.25 * (row_speed[:-1] + row_speed[1:])
    side_speed = 0.25 * (col_speed + jnp.roll(col_speed, -1, axis=-1))
    outputs = []
    for component in range(2):
        values = state_ext[component]
        middle = values[1 : row_count + 1]
        row_flux = face_speed * (values[:-1] + values[1:])
        col_flux = side_speed * (middle + jnp.roll(middle, -1, axis=-1))
        divergence = row_flux[1:] - row_flux[:-1] + (col_flux - jnp.roll(col_flux, 1, axis=-1))
        laplacian = (
            values[2:]
            + values[:-2]
            + jnp.roll(middle, -1, axis=-1)
            + jnp.roll(middle, 1, axis=-1)
            - 4.0 * middle
        )
        outputs.append(middle + step_factor * (viscosity * laplacian - divergence))
    return jnp.stack(outputs)


def relu_value(preact):
    return jnp.maximum(preact.astype(jnp.float32), jnp.float32(0.0))


def relu_slope(preact):
    return jnp.where(preact > 0, jnp.float32(1.0), jnp.float32(0.0))


def col_shifts(values):
    return [jnp.roll(values, 1, axis=-1), values, jnp.roll(values, -1, axis=-1)]


def weight_terms(gradient, source_ext):
    row_count = gradient.shape[0]
    shifted = col_shifts(source_ext)
    products = []
    for row_tap in range(3):
        for col_tap in range(3):
            section = shifted[col_tap][row_tap : row_tap + row_count]
            products.append(
                jnp.einsum("roy,rky->ok", gradient, section, preferred_element_type=jnp.float32)
            )
    return jnp.stack(products)


def back_conv(grad_ext, kernel):
    row_count = grad_ext.shape[0] - 2
    shifted = col_shifts(grad_ext)
    summed = None
    for row_tap in range(3):
        for col_tap in range(3):
            section = shifted[2 - col_tap][2 - row_tap : 2 - row_tap + row_count]
            product = jnp.einsum(
                "ok,roy->rky",
                kernel[3 * row_tap + col_tap],
                section,
                preferred_element_type=jnp.float32,
            )
            summed = product if summed is None else summed + product
    return summed


def gradient_rim(gradient):
    return extended(gradient, (("gx", 0),), 1)


def layer_step(state, preacts, adjoint, kernels, grad_totals):
    channels = preacts.shape[2]
    state_ext = extended(state, (("gx", 1),), 2)
    half_ext, pullback = jax.vjp(half_valid, state_ext)
    source_first = jnp.swapaxes(half_ext, 0, 1).astype(jnp.bfloat16)
    gradient = jnp.swapaxes(adjoint, 0, 1).astype(jnp.bfloat16)
    backward = None
    for layer_index in (3, 2, 1, 0):
        if layer_index > 0:
            joined = extended(
                jnp.concatenate([preacts[layer_index - 1], gradient], axis=1), (("gx", 0),), 1
            )
            preact_ext = joined[:, :channels]
            grad_ext = joined[:, channels:]
            source = relu_value(preact_ext).astype(jnp.bfloat16)
        else:
            grad_ext = gradient_rim(gradient)
            source = source_first
        grad_totals[layer_index] = grad_totals[layer_index] + weight_terms(gradient, source)
        backward = back_conv(grad_ext, kernels[layer_index])
        if layer_index > 0:
            gradient = (backward * relu_slope(trim_lead(preact_ext, 1))).astype(jnp.bfloat16)
    combined = adjoint + jnp.swapaxes(backward, 0, 1)
    combined_ext = extended(combined, (("gx", 1),), 1)
    return (trim_rows(pullback(combined_ext)[0], 2), grad_totals)


def on_device(states, pre_acts, cotangent, weight_in, weight_second, weight_third, weight_out):
    kernels = (weight_in, weight_second, weight_third, weight_out)
    grad_totals = [jnp.zeros(kernel.shape, jnp.float32) for kernel in kernels]
    adjoint = cotangent
    for step_index in (1, 0):
        adjoint, grad_totals = layer_step(
            states[step_index], pre_acts[step_index], adjoint, kernels, grad_totals
        )
    summed = lax.psum((grad_totals[0], grad_totals[1], grad_totals[2], grad_totals[3]), "gx")
    factor = 1.0 / math.sqrt(cotangent.shape[1] * lax.axis_size("gx") * cotangent.shape[2])
    return (adjoint, summed[0] * factor, summed[1] * factor, summed[2] * factor, summed[3] * factor)


def solution(mesh):
    return jax.shard_map(
        on_device,
        mesh=mesh,
        in_specs=(
            P(None, "groups", "gx", None),
            P(None, None, ("groups", "gx"), None, None),
            P("groups", "gx", None),
            P(),
            P(),
            P(),
            P(),
        ),
        out_specs=(
            P("groups", "gx", None),
            P("groups", None, None),
            P("groups", None, None),
            P("groups", None, None),
            P("groups", None, None),
        ),
        check_vma=False,
    )
```

profile of v0, /device:TPU:0, one launch (start us, length us, event | category | flops | bytes accessed | tf_op | source)
XLA Modules:
  0.0 230.3 jit_solution(16800260987941374135)
XLA Ops:
  7.2 0.8 convert_element_type.98
  8.0 1.9 slice_bitcast_fusion.2
  9.9 0.5 collective-permute-start
  10.5 5.0 %collective-permute-start.1 = (bf16[1,50,512]{2,1,0:T(8,128)(2,1)S(1)}, bf16[1,50,512]{2,1,0:T(8,128)(2,1)S(1)}, u32[]{:S(2)}, u32[]{:S(2)}) collective-permute-start(bf16[1,50,512]{2,1,0:T(8,128)(2,1)S(1)} %get-tuple-element.86), channel_id=1, source_target_pairs={{1,0},{2,1},{3,2},{4,3},{5,4},{6,5},{7,6},{8,7},{9,8},{10,9},{11,1... | collective-permute-start | bytes 153608 | tf_op jit(solution)/shard_map/ppermute | solution.py:21
  15.6 4.4 %collective-permute-start.11 = (f32[2,2,512]{2,1,0:T(2,128)S(1)}, f32[2,2,512]{2,1,0:T(2,128)S(1)}, u32[]{:S(2)}, u32[]{:S(2)}) collective-permute-start(f32[2,2,512]{2,1,0:T(2,128)S(1)} %get-tuple-element.187), channel_id=1, source_target_pairs={{1,0},{2,1},{3,2},{4,3},{5,4},{6,5},{7,6},{8,7},{9,8},{10,9},{11,1... | collective-permute-start | bytes 24584 | tf_op jit(solution)/shard_map/ppermute | solution.py:21
  20.3 1.0 collective-permute-done.10
  21.3 3.5 %collective-permute-start.23 = (f32[2,2,512]{2,1,0:T(2,128)S(1)}, f32[2,2,512]{2,1,0:T(2,128)S(1)}, u32[]{:S(2)}, u32[]{:S(2)}) collective-permute-start(f32[2,2,512]{2,1,0:T(2,128)S(1)} %get-tuple-element.189), channel_id=1, source_target_pairs={{1,0},{2,1},{3,2},{4,3},{5,4},{6,5},{7,6},{8,7},{9,8},{10,9},{11,1... | collective-permute-start | bytes 24584 | tf_op jit(solution)/shard_map/ppermute | solution.py:21
  25.2 0.6 collective-permute-done.22
  25.8 0.4 collective-permute-done.23
  29.3 0.5 fusion.15
  30.1 1.6 fusion.28
  31.8 4.5 %collective-permute-start.3 = (bf16[1,96,512]{2,1,0:T(8,128)(2,1)S(1)}, bf16[1,96,512]{2,1,0:T(8,128)(2,1)S(1)}, u32[]{:S(2)}, u32[]{:S(2)}) collective-permute-start(bf16[1,96,512]{2,1,0:T(8,128)(2,1)S(1)} %get-tuple-element.46), channel_id=1, source_target_pairs={{1,0},{2,1},{3,2},{4,3},{5,4},{6,5},{7,6},{8,7},{9,8},{10,9},{11,1... | collective-permute-start | bytes 294920 | tf_op jit(solution)/shard_map/ppermute | solution.py:21
  38.6 4.3 %collective-permute-done.2 = bf16[1,96,512]{2,1,0:T(8,128)(2,1)S(1)} collective-permute-done((bf16[1,96,512]{2,1,0:T(8,128)(2,1)S(1)}, bf16[1,96,512]{2,1,0:T(8,128)(2,1)S(1)}, u32[]{:S(2)}, u32[]{:S(2)}) %collective-permute-start.2) | collective-permute-done | bytes 98336 | tf_op jit(solution)/shard_map/ppermute | solution.py:19
  43.7 0.4 fusion.117
  44.1 0.4 copy-done
  47.4 0.4 collective-permute-start.4
  47.8 0.3 fusion.55
  48.4 0.3 fusion.53
  48.7 0.3 fusion.52
  49.6 0.3 fusion.49
  50.2 0.3 fusion.47
  50.5 3.7 %collective-permute-done.4 = bf16[1,96,512]{2,1,0:T(8,128)(2,1)S(1)} collective-permute-done((bf16[1,96,512]{2,1,0:T(8,128)(2,1)S(1)}, bf16[1,96,512]{2,1,0:T(8,128)(2,1)S(1)}, u32[]{:S(2)}, u32[]{:S(2)}) %collective-permute-start.4) | collective-permute-done | bytes 98336 | tf_op jit(solution)/shard_map/ppermute | solution.py:19
  55.0 0.4 fusion.115
  55.4 0.4 copy-done.1
  58.6 4.4 %collective-permute-start.7 = (bf16[1,48,512]{2,1,0:T(8,128)(2,1)S(1)}, bf16[1,48,512]{2,1,0:T(8,128)(2,1)S(1)}, u32[]{:S(2)}, u32[]{:S(2)}) collective-permute-start(bf16[1,48,512]{2,1,0:T(8,128)(2,1)S(1)} %get-tuple-element.90), channel_id=1, source_target_pairs={{1,0},{2,1},{3,2},{4,3},{5,4},{6,5},{7,6},{8,7},{9,8},{10,9},{11,1... | collective-permute-start | bytes 147464 | tf_op jit(solution)/shard_map/ppermute | solution.py:21
  63.0 0.3 fusion.73
  63.9 0.3 fusion.70
  64.9 0.3 fusion.67
  68.2 4.4 %collective-permute-start.9 = (f32[2,1,512]{2,1,0:T(1,128)S(1)}, f32[2,1,512]{2,1,0:T(1,128)S(1)}, u32[]{:S(2)}, u32[]{:S(2)}) collective-permute-start(f32[2,1,512]{2,1,0:T(1,128)S(1)} %get-tuple-element.185), channel_id=1, source_target_pairs={{1,0},{2,1},{3,2},{4,3},{5,4},{6,5},{7,6},{8,7},{9,8},{10,9},{11,1... | collective-permute-start | bytes 12296 | tf_op jit(solution)/shard_map/ppermute | solution.py:21
  72.9 1.0 collective-permute-done.8
  75.8 4.5 %collective-permute-start.13 = (bf16[1,50,512]{2,1,0:T(8,128)(2,1)S(1)}, bf16[1,50,512]{2,1,0:T(8,128)(2,1)S(1)}, u32[]{:S(2)}, u32[]{:S(2)}) collective-permute-start(bf16[1,50,512]{2,1,0:T(8,128)(2,1)S(1)} %get-tuple-element.84), channel_id=1, source_target_pairs={{1,0},{2,1},{3,2},{4,3},{5,4},{6,5},{7,6},{8,7},{9,8},{10,9},{11,1... | collective-permute-start | bytes 153608 | tf_op jit(solution)/shard_map/ppermute | solution.py:21
  82.3 4.2 %collective-permute-done.12 = bf16[1,50,512]{2,1,0:T(8,128)(2,1)S(1)} collective-permute-done((bf16[1,50,512]{2,1,0:T(8,128)(2,1)S(1)}, bf16[1,50,512]{2,1,0:T(8,128)(2,1)S(1)}, u32[]{:S(2)}, u32[]{:S(2)}) %collective-permute-start.12) | collective-permute-done | bytes 51232 | tf_op jit(solution)/shard_map/ppermute | solution.py:19
  88.7 0.5 fusion.7
  89.5 1.6 fusion.29
  91.2 4.4 %collective-permute-start.15 = (bf16[1,96,512]{2,1,0:T(8,128)(2,1)S(1)}, bf16[1,96,512]{2,1,0:T(8,128)(2,1)S(1)}, u32[]{:S(2)}, u32[]{:S(2)}) collective-permute-start(bf16[1,96,512]{2,1,0:T(8,128)(2,1)S(1)} %get-tuple-element.42), channel_id=1, source_target_pairs={{1,0},{2,1},{3,2},{4,3},{5,4},{6,5},{7,6},{8,7},{9,8},{10,9},{11,1... | collective-permute-start | bytes 294920 | tf_op jit(solution)/shard_map/ppermute | solution.py:21
  98.9 0.3 fusion.46
  99.5 0.3 fusion.44
  99.8 0.3 fusion.43
  100.4 0.3 fusion.41
  100.7 0.3 fusion.40
  101.3 0.4 fusion.113
  104.0 0.3 fusion.32
  104.4 4.4 %collective-permute-start.17 = (bf16[1,96,512]{2,1,0:T(8,128)(2,1)S(1)}, bf16[1,96,512]{2,1,0:T(8,128)(2,1)S(1)}, u32[]{:S(2)}, u32[]{:S(2)}) collective-permute-start(bf16[1,96,512]{2,1,0:T(8,128)(2,1)S(1)} %get-tuple-element.40), channel_id=1, source_target_pairs={{1,0},{2,1},{3,2},{4,3},{5,4},{6,5},{7,6},{8,7},{9,8},{10,9},{11,1... | collective-permute-start | bytes 294920 | tf_op jit(solution)/shard_map/ppermute | solution.py:21
  109.2 0.7 add.662
  109.9 1.3 collective-permute-done.16
  112.0 0.3 fusion.64
  112.5 0.3 fusion.62
  112.9 0.3 fusion.61
  113.8 0.3 fusion.58
  114.4 0.4 fusion.111
  117.5 4.5 %collective-permute-start.19 = (bf16[1,48,512]{2,1,0:T(8,128)(2,1)S(1)}, bf16[1,48,512]{2,1,0:T(8,128)(2,1)S(1)}, u32[]{:S(2)}, u32[]{:S(2)}) collective-permute-start(bf16[1,48,512]{2,1,0:T(8,128)(2,1)S(1)} %get-tuple-element.88), channel_id=1, source_target_pairs={{1,0},{2,1},{3,2},{4,3},{5,4},{6,5},{7,6},{8,7},{9,8},{10,9},{11,1... | collective-permute-start | bytes 147464 | tf_op jit(solution)/shard_map/ppermute | solution.py:21
  122.2 1.5 collective-permute-done.18
  124.4 0.3 fusion.312
  124.9 0.3 convolution_add_fusion.36
  125.4 0.3 convolution_add_fusion.34
  126.2 4.5 %collective-permute-start.21 = (f32[2,1,512]{2,0,1:T(2,128)S(1)}, f32[2,1,512]{2,0,1:T(2,128)S(1)}, u32[]{:S(2)}, u32[]{:S(2)}) collective-permute-start(f32[2,1,512]{2,0,1:T(2,128)S(1)} %get-tuple-element.175), channel_id=1, source_target_pairs={{1,0},{2,1},{3,2},{4,3},{5,4},{6,5},{7,6},{8,7},{9,8},{10,9},{11,1... | collective-permute-start | bytes 12296 | tf_op jit(solution)/shard_map/ppermute | solution.py:21
  131.1 0.7 add.661
  135.4 62.0 %all-reduce.78 = (f32[9,48,2]{1,2,0:T(2,128)S(1)}, f32[9,2,48]{2,1,0:T(2,128)S(1)}) all-reduce(f32[9,48,2]{1,2,0:T(2,128)S(1)} %add.660, f32[9,2,48]{2,1,0:T(2,128)S(1)} %add.663), channel_id=1, replica_groups=mesh['groups'=2,'gx'=16] {'gx'}, use_global_device_ids=true, to_apply=%region_0.1 | all-reduce | flops 1728 | bytes 13824 | tf_op jit(solution)/shard_map/psum | solution.py:141
  197.4 0.6 broadcast_multiply_fusion.2
  198.0 0.6 broadcast_multiply_fusion.3
  199.0 0.6 pad_add_fusion
  199.6 20.6 %all-reduce.82.cloned.1.call-done = (f32[9,48,48]{2,1,0:T(8,128)}, f32[9,48,48]{2,1,0:T(8,128)}) async-done(((f32[9,48,48]{2,1,0:T(8,128)}, f32[9,48,48]{2,1,0:T(8,128)}), (f32[9,48,48]{2,1,0:T(8,128)}, f32[9,48,48]{2,1,0:T(8,128)})) %all-reduce.82.cloned.1.call-update) | async-done | bytes 165904 | tf_op jit(solution)/shard_map/psum | solution.py:141
  220.2 1.6 broadcast_multiply_fusion
  221.8 1.6 broadcast_multiply_fusion.1
  (288 shorter events, 42.2 us)
Async XLA Ops:
  7.2 213.0 %all-reduce.82.cloned.1.call-start = ((), (), s32[]{:S(2)}) async-start(), calls=%async_computation | async-start | bytes 884736 | tf_op jit(solution)/shard_map/psum | solution.py:141
  8.0 7.5 %copy-start.3 = (f32[2,2,8,512]{3,2,1,0:T(8,128)S(1)}, f32[2,2,8,512]{3,2,1,0:T(8,128)}, u32[]{:S(2)}) copy-start(f32[2,2,8,512]{3,2,1,0:T(8,128)} %param.7) | copy-start | bytes 196612
  8.0 12.0 %copy-start.4 = (bf16[9,2,48]{2,1,0:T(2,128)(2,1)S(1)}, bf16[9,2,48]{2,1,0:T(2,128)(2,1)}, u32[]{:S(2)}) copy-start(bf16[9,2,48]{2,1,0:T(2,128)(2,1)} %param.13) | copy-start | bytes 5188
  9.9 17.2 %collective-permute-start = (bf16[1,50,512]{2,1,0:T(8,128)(2,1)S(1)}, bf16[1,50,512]{2,1,0:T(8,128)(2,1)S(1)}, u32[]{:S(2)}, u32[]{:S(2)}) collective-permute-start(bf16[1,50,512]{2,1,0:T(8,128)(2,1)S(1)} %get-tuple-element.85), channel_id=1, source_target_pairs={{0,1},{1,2},{2,3},{3,4},{4,5},{5,6},{6,7},{7,8},{8,9},{9,10},{10,1... | collective-permute-start | bytes 153608 | tf_op jit(solution)/shard_map/ppermute | solution.py:19
  10.5 16.7 %collective-permute-start.1 = (bf16[1,50,512]{2,1,0:T(8,128)(2,1)S(1)}, bf16[1,50,512]{2,1,0:T(8,128)(2,1)S(1)}, u32[]{:S(2)}, u32[]{:S(2)}) collective-permute-start(bf16[1,50,512]{2,1,0:T(8,128)(2,1)S(1)} %get-tuple-element.86), channel_id=1, source_target_pairs={{1,0},{2,1},{3,2},{4,3},{5,4},{6,5},{7,6},{8,7},{9,8},{10,9},{11,1... | collective-permute-start | bytes 153608 | tf_op jit(solution)/shard_map/ppermute | solution.py:21
  15.5 5.8 %collective-permute-start.10 = (f32[2,2,512]{2,1,0:T(2,128)S(1)}, f32[2,2,512]{2,1,0:T(2,128)S(1)}, u32[]{:S(2)}, u32[]{:S(2)}) collective-permute-start(f32[2,2,512]{2,1,0:T(2,128)S(1)} %get-tuple-element.186), channel_id=1, source_target_pairs={{0,1},{1,2},{2,3},{3,4},{4,5},{5,6},{6,7},{7,8},{8,9},{9,10},{10,1... | collective-permute-start | bytes 24584 | tf_op jit(solution)/shard_map/ppermute | solution.py:19
  15.6 9.3 %collective-permute-start.11 = (f32[2,2,512]{2,1,0:T(2,128)S(1)}, f32[2,2,512]{2,1,0:T(2,128)S(1)}, u32[]{:S(2)}, u32[]{:S(2)}) collective-permute-start(f32[2,2,512]{2,1,0:T(2,128)S(1)} %get-tuple-element.187), channel_id=1, source_target_pairs={{1,0},{2,1},{3,2},{4,3},{5,4},{6,5},{7,6},{8,7},{9,8},{10,9},{11,1... | collective-permute-start | bytes 24584 | tf_op jit(solution)/shard_map/ppermute | solution.py:21
  20.0 5.8 %collective-permute-start.22 = (f32[2,2,512]{2,1,0:T(2,128)S(1)}, f32[2,2,512]{2,1,0:T(2,128)S(1)}, u32[]{:S(2)}, u32[]{:S(2)}) collective-permute-start(f32[2,2,512]{2,1,0:T(2,128)S(1)} %get-tuple-element.188), channel_id=1, source_target_pairs={{0,1},{1,2},{2,3},{3,4},{4,5},{5,6},{6,7},{7,8},{8,9},{9,10},{10,1... | collective-permute-start | bytes 24584 | tf_op jit(solution)/shard_map/ppermute | solution.py:19
  21.3 4.9 %collective-permute-start.23 = (f32[2,2,512]{2,1,0:T(2,128)S(1)}, f32[2,2,512]{2,1,0:T(2,128)S(1)}, u32[]{:S(2)}, u32[]{:S(2)}) collective-permute-start(f32[2,2,512]{2,1,0:T(2,128)S(1)} %get-tuple-element.189), channel_id=1, source_target_pairs={{1,0},{2,1},{3,2},{4,3},{5,4},{6,5},{7,6},{8,7},{9,8},{10,9},{11,1... | collective-permute-start | bytes 24584 | tf_op jit(solution)/shard_map/ppermute | solution.py:21
  31.8 6.9 %collective-permute-start.3 = (bf16[1,96,512]{2,1,0:T(8,128)(2,1)S(1)}, bf16[1,96,512]{2,1,0:T(8,128)(2,1)S(1)}, u32[]{:S(2)}, u32[]{:S(2)}) collective-permute-start(bf16[1,96,512]{2,1,0:T(8,128)(2,1)S(1)} %get-tuple-element.46), channel_id=1, source_target_pairs={{1,0},{2,1},{3,2},{4,3},{5,4},{6,5},{7,6},{8,7},{9,8},{10,9},{11,1... | collective-permute-start | bytes 294920 | tf_op jit(solution)/shard_map/ppermute | solution.py:21
  36.2 6.7 %collective-permute-start.2 = (bf16[1,96,512]{2,1,0:T(8,128)(2,1)S(1)}, bf16[1,96,512]{2,1,0:T(8,128)(2,1)S(1)}, u32[]{:S(2)}, u32[]{:S(2)}) collective-permute-start(bf16[1,96,512]{2,1,0:T(8,128)(2,1)S(1)} %get-tuple-element.45), channel_id=1, source_target_pairs={{0,1},{1,2},{2,3},{3,4},{4,5},{5,6},{6,7},{7,8},{8,9},{9,10},{10,1... | collective-permute-start | bytes 294920 | tf_op jit(solution)/shard_map/ppermute | solution.py:19
  43.6 0.9 copy-start
  47.2 3.3 %collective-permute-start.5 = (bf16[1,96,512]{2,1,0:T(8,128)(2,1)S(1)}, bf16[1,96,512]{2,1,0:T(8,128)(2,1)S(1)}, u32[]{:S(2)}, u32[]{:S(2)}) collective-permute-start(bf16[1,96,512]{2,1,0:T(8,128)(2,1)S(1)} %get-tuple-element.44), channel_id=1, source_target_pairs={{1,0},{2,1},{3,2},{4,3},{5,4},{6,5},{7,6},{8,7},{9,8},{10,9},{11,1... | collective-permute-start | bytes 294920 | tf_op jit(solution)/shard_map/ppermute | solution.py:21
  47.4 6.8 %collective-permute-start.4 = (bf16[1,96,512]{2,1,0:T(8,128)(2,1)S(1)}, bf16[1,96,512]{2,1,0:T(8,128)(2,1)S(1)}, u32[]{:S(2)}, u32[]{:S(2)}) collective-permute-start(bf16[1,96,512]{2,1,0:T(8,128)(2,1)S(1)} %get-tuple-element.43), channel_id=1, source_target_pairs={{0,1},{1,2},{2,3},{3,4},{4,5},{5,6},{6,7},{7,8},{8,9},{9,10},{10,1... | collective-permute-start | bytes 294920 | tf_op jit(solution)/shard_map/ppermute | solution.py:19
  54.9 0.9 copy-start.1
  58.5 7.1 %collective-permute-start.6 = (bf16[1,48,512]{2,1,0:T(8,128)(2,1)S(1)}, bf16[1,48,512]{2,1,0:T(8,128)(2,1)S(1)}, u32[]{:S(2)}, u32[]{:S(2)}) collective-permute-start(bf16[1,48,512]{2,1,0:T(8,128)(2,1)S(1)} %get-tuple-element.89), channel_id=1, source_target_pairs={{0,1},{1,2},{2,3},{3,4},{4,5},{5,6},{6,7},{7,8},{8,9},{9,10},{10,1... | collective-permute-start | bytes 147464 | tf_op jit(solution)/shard_map/ppermute | solution.py:19
  58.6 7.1 %collective-permute-start.7 = (bf16[1,48,512]{2,1,0:T(8,128)(2,1)S(1)}, bf16[1,48,512]{2,1,0:T(8,128)(2,1)S(1)}, u32[]{:S(2)}, u32[]{:S(2)}) collective-permute-start(bf16[1,48,512]{2,1,0:T(8,128)(2,1)S(1)} %get-tuple-element.90), channel_id=1, source_target_pairs={{1,0},{2,1},{3,2},{4,3},{5,4},{6,5},{7,6},{8,7},{9,8},{10,9},{11,1... | collective-permute-start | bytes 147464 | tf_op jit(solution)/shard_map/ppermute | solution.py:21
  64.3 1.2 copy-start.5
  66.8 1.2 copy-start.2
  68.1 5.8 %collective-permute-start.8 = (f32[2,1,512]{2,1,0:T(1,128)S(1)}, f32[2,1,512]{2,1,0:T(1,128)S(1)}, u32[]{:S(2)}, u32[]{:S(2)}) collective-permute-start(f32[2,1,512]{2,1,0:T(1,128)S(1)} %get-tuple-element.184), channel_id=1, source_target_pairs={{0,1},{1,2},{2,3},{3,4},{4,5},{5,6},{6,7},{7,8},{8,9},{9,10},{10,1... | collective-permute-start | bytes 12296 | tf_op jit(solution)/shard_map/ppermute | solution.py:19
  68.2 5.8 %collective-permute-start.9 = (f32[2,1,512]{2,1,0:T(1,128)S(1)}, f32[2,1,512]{2,1,0:T(1,128)S(1)}, u32[]{:S(2)}, u32[]{:S(2)}) collective-permute-start(f32[2,1,512]{2,1,0:T(1,128)S(1)} %get-tuple-element.185), channel_id=1, source_target_pairs={{1,0},{2,1},{3,2},{4,3},{5,4},{6,5},{7,6},{8,7},{9,8},{10,9},{11,1... | collective-permute-start | bytes 12296 | tf_op jit(solution)/shard_map/ppermute | solution.py:21
  75.8 6.5 %collective-permute-start.13 = (bf16[1,50,512]{2,1,0:T(8,128)(2,1)S(1)}, bf16[1,50,512]{2,1,0:T(8,128)(2,1)S(1)}, u32[]{:S(2)}, u32[]{:S(2)}) collective-permute-start(bf16[1,50,512]{2,1,0:T(8,128)(2,1)S(1)} %get-tuple-element.84), channel_id=1, source_target_pairs={{1,0},{2,1},{3,2},{4,3},{5,4},{6,5},{7,6},{8,7},{9,8},{10,9},{11,1... | collective-permute-start | bytes 153608 | tf_op jit(solution)/shard_map/ppermute | solution.py:21
  80.2 6.3 %collective-permute-start.12 = (bf16[1,50,512]{2,1,0:T(8,128)(2,1)S(1)}, bf16[1,50,512]{2,1,0:T(8,128)(2,1)S(1)}, u32[]{:S(2)}, u32[]{:S(2)}) collective-permute-start(bf16[1,50,512]{2,1,0:T(8,128)(2,1)S(1)} %get-tuple-element.83), channel_id=1, source_target_pairs={{0,1},{1,2},{2,3},{3,4},{4,5},{5,6},{6,7},{7,8},{8,9},{9,10},{10,1... | collective-permute-start | bytes 153608 | tf_op jit(solution)/shard_map/ppermute | solution.py:19
  91.2 7.0 %collective-permute-start.14 = (bf16[1,96,512]{2,1,0:T(8,128)(2,1)S(1)}, bf16[1,96,512]{2,1,0:T(8,128)(2,1)S(1)}, u32[]{:S(2)}, u32[]{:S(2)}) collective-permute-start(bf16[1,96,512]{2,1,0:T(8,128)(2,1)S(1)} %get-tuple-element.41), channel_id=1, source_target_pairs={{0,1},{1,2},{2,3},{3,4},{4,5},{5,6},{6,7},{7,8},{8,9},{9,10},{10,1... | collective-permute-start | bytes 294920 | tf_op jit(solution)/shard_map/ppermute | solution.py:19
  91.2 6.9 %collective-permute-start.15 = (bf16[1,96,512]{2,1,0:T(8,128)(2,1)S(1)}, bf16[1,96,512]{2,1,0:T(8,128)(2,1)S(1)}, u32[]{:S(2)}, u32[]{:S(2)}) collective-permute-start(bf16[1,96,512]{2,1,0:T(8,128)(2,1)S(1)} %get-tuple-element.42), channel_id=1, source_target_pairs={{1,0},{2,1},{3,2},{4,3},{5,4},{6,5},{7,6},{8,7},{9,8},{10,9},{11,1... | collective-permute-start | bytes 294920 | tf_op jit(solution)/shard_map/ppermute | solution.py:21
  104.4 6.8 %collective-permute-start.16 = (bf16[1,96,512]{2,1,0:T(8,128)(2,1)S(1)}, bf16[1,96,512]{2,1,0:T(8,128)(2,1)S(1)}, u32[]{:S(2)}, u32[]{:S(2)}) collective-permute-start(bf16[1,96,512]{2,1,0:T(8,128)(2,1)S(1)} %get-tuple-element.39), channel_id=1, source_target_pairs={{0,1},{1,2},{2,3},{3,4},{4,5},{5,6},{6,7},{7,8},{8,9},{9,10},{10,1... | collective-permute-start | bytes 294920 | tf_op jit(solution)/shard_map/ppermute | solution.py:19
  104.4 6.7 %collective-permute-start.17 = (bf16[1,96,512]{2,1,0:T(8,128)(2,1)S(1)}, bf16[1,96,512]{2,1,0:T(8,128)(2,1)S(1)}, u32[]{:S(2)}, u32[]{:S(2)}) collective-permute-start(bf16[1,96,512]{2,1,0:T(8,128)(2,1)S(1)} %get-tuple-element.40), channel_id=1, source_target_pairs={{1,0},{2,1},{3,2},{4,3},{5,4},{6,5},{7,6},{8,7},{9,8},{10,9},{11,1... | collective-permute-start | bytes 294920 | tf_op jit(solution)/shard_map/ppermute | solution.py:21
  117.5 6.3 %collective-permute-start.18 = (bf16[1,48,512]{2,1,0:T(8,128)(2,1)S(1)}, bf16[1,48,512]{2,1,0:T(8,128)(2,1)S(1)}, u32[]{:S(2)}, u32[]{:S(2)}) collective-permute-start(bf16[1,48,512]{2,1,0:T(8,128)(2,1)S(1)} %get-tuple-element.87), channel_id=1, source_target_pairs={{0,1},{1,2},{2,3},{3,4},{4,5},{5,6},{6,7},{7,8},{8,9},{9,10},{10,1... | collective-permute-start | bytes 147464 | tf_op jit(solution)/shard_map/ppermute | solution.py:19
  117.5 6.2 %collective-permute-start.19 = (bf16[1,48,512]{2,1,0:T(8,128)(2,1)S(1)}, bf16[1,48,512]{2,1,0:T(8,128)(2,1)S(1)}, u32[]{:S(2)}, u32[]{:S(2)}) collective-permute-start(bf16[1,48,512]{2,1,0:T(8,128)(2,1)S(1)} %get-tuple-element.88), channel_id=1, source_target_pairs={{1,0},{2,1},{3,2},{4,3},{5,4},{6,5},{7,6},{8,7},{9,8},{10,9},{11,1... | collective-permute-start | bytes 147464 | tf_op jit(solution)/shard_map/ppermute | solution.py:21
  126.2 5.8 %collective-permute-start.20 = (f32[2,1,512]{2,0,1:T(2,128)S(1)}, f32[2,1,512]{2,0,1:T(2,128)S(1)}, u32[]{:S(2)}, u32[]{:S(2)}) collective-permute-start(f32[2,1,512]{2,0,1:T(2,128)S(1)} %get-tuple-element.174), channel_id=1, source_target_pairs={{0,1},{1,2},{2,3},{3,4},{4,5},{5,6},{6,7},{7,8},{8,9},{9,10},{10,1... | collective-permute-start | bytes 12296 | tf_op jit(solution)/shard_map/ppermute | solution.py:19
  126.2 5.8 %collective-permute-start.21 = (f32[2,1,512]{2,0,1:T(2,128)S(1)}, f32[2,1,512]{2,0,1:T(2,128)S(1)}, u32[]{:S(2)}, u32[]{:S(2)}) collective-permute-start(f32[2,1,512]{2,0,1:T(2,128)S(1)} %get-tuple-element.175), channel_id=1, source_target_pairs={{1,0},{2,1},{3,2},{4,3},{5,4},{6,5},{7,6},{8,7},{9,8},{10,9},{11,1... | collective-permute-start | bytes 12296 | tf_op jit(solution)/shard_map/ppermute | solution.py:21
Sparse Core Ops, SparseCore 0:
  131.9 88.2 all-reduce.81
where the time goes:
time: 231 us; the launch traced here: 230 us
  blocking collectives  62 us (27%)
  starting transfers between devices  50.1 us (22%)
  matrix products  42.7 us (18%)
  waiting for transfers between devices  39.1 us (17%)
  between operations  15.4 us (7%)
  other arithmetic  11.9 us (5%)
  local copies, waits for them, and re-layouts  9.14 us (4%)
    psum x1, blocking collectives, on_device(): lax.psum((grad_totals[0], grad_totals[1], grad_totals[2], grad_totals[3])...  62 us
    ppermute x12, starting transfers between devices, extended(): lax.ppermute(head, axis, [((i + 1) % count, i) for i in range(count)])  48.8 us
    dot_general x72, matrix products, back_conv(): jnp.einsum('ok,roy->rky', kernel[3 * row_tap + col_tap], section, preferr...  23.3 us
    psum x1, waiting for transfers between devices, on_device(): lax.psum((grad_totals[0], grad_totals[1], grad_totals[2], grad_totals[3])...  20.6 us
    dot_general x72, matrix products, weight_terms(): jnp.einsum('roy,rky->ok', gradient, section, preferred_element_type=jnp.f...  19.4 us
    ppermute x12, waiting for transfers between devices, extended(): lax.ppermute(tail, axis, [(i, (i + 1) % count) for i in range(count)])  17.8 us
  transfers between devices with their start and end apart: 25, of which 12 were waited for; matrix products, arithmetic and copies ran while one was open for 9% of the time, Pallas kernels for 0%

commit v1 on v0

v1 whole, which is shorter than its diff:
```python
import functools
import math

import jax
import jax.numpy as jnp
from jax import lax
from jax.experimental import pallas as pl
from jax.experimental.pallas import tpu as pltpu
from jax.sharding import PartitionSpec as P

STEP = 0.25
VISC = 0.4
LANES = 128
BLOCK = 3
BLOCK4 = 4
SMALL = 8

F32 = jnp.float32
BF16 = jnp.bfloat16


def lane_roll(x, shift):
    width = x.shape[-1]
    return pltpu.roll(x, shift % width, x.ndim - 1)


def row_roll(x, shift):
    return pltpu.roll(x, shift % x.shape[0], 0)


def half_step(r, c):
    face = 0.25 * (r + row_roll(r, -1))
    side = 0.25 * (c + lane_roll(c, -1))
    outs = []
    for f in (r, c):
        down, right = row_roll(f, -1), lane_roll(f, -1)
        p = face * (f + down)
        q = side * (f + right)
        div = p - row_roll(p, 1) + (q - lane_roll(q, 1))
        lap = down + row_roll(f, 1) + right + lane_roll(f, 1) - 4.0 * f
        outs.append(f + STEP * (VISC * lap - div))
    return outs


def half_step_transpose(r, c, lr, lc):
    face = 0.25 * (r + row_roll(r, -1))
    side = 0.25 * (c + lane_roll(c, -1))
    outs = []
    extra_r = None
    extra_c = None
    for f, l in ((r, lr), (c, lc)):
        l_down, l_right = row_roll(l, -1), lane_roll(l, -1)
        a = STEP * (l_down - l)
        b = STEP * (l_right - l)
        ap, bq = a * face, b * side
        lap = l_down + row_roll(l, 1) + l_right + lane_roll(l, 1) - 4.0 * l
        outs.append(
            l + (STEP * VISC) * lap + (ap + row_roll(ap, 1)) + (bq + lane_roll(bq, 1))
        )
        af = a * (0.25 * (f + row_roll(f, -1)))
        bf = b * (0.25 * (f + lane_roll(f, -1)))
        extra_r = af if extra_r is None else extra_r + af
        extra_c = bf if extra_c is None else extra_c + bf
    return [
        outs[0] + (extra_r + row_roll(extra_r, 1)),
        outs[1] + (extra_c + lane_roll(extra_c, 1)),
    ]


def joined(first, own, second, even, comp):
    a, b = first[comp], second[comp]
    top = jnp.where(even, b, a)
    bottom = jnp.where(even, a, b)
    return jnp.concatenate([top, own[comp], bottom], axis=0)


def fill_small(dst, planes, rows, row0, sign):
    width = planes[0].shape[-1]
    dst[...] = jnp.zeros(dst.shape, F32)
    for comp, plane in enumerate(planes):
        value = plane.astype(BF16).astype(F32)
        for q in range(3):
            moved = value if q == 1 else lane_roll(value, sign * (q - 1))
            for i in range(rows):
                dst[SMALL * i + 2 * q + comp : SMALL * i + 2 * q + comp + 1, :] = moved[
                    row0 + i : row0 + i + 1, :
                ]


def row_conv(w_ref, src, src0, lo, hi, ch, emit):
    row = lo
    while row < hi:
        count = min(BLOCK, hi - row)
        rhs = src[(row - 1 - src0) * ch : (row + count + 1 - src0) * ch, :]
        lhs = w_ref[: count * 3 * ch, : (count + 2) * ch]
        y = jnp.dot(lhs, rhs, preferred_element_type=F32)
        for k in range(count):
            base = 3 * ch * k
            e = (
                y[base + ch : base + 2 * ch]
                + lane_roll(y[base : base + ch], -1)
                + lane_roll(y[base + 2 * ch : base + 3 * ch], 1)
            )
            emit(row + k, e)
        row += count


def chain(x4, pre, m_a, m_b, even, w4, w3, w2, d3, d2, d1, rows, ch, extra):
    e3, e2, e1 = extra
    starts = (0, e3, e3 + e2)

    def mask_rows(layer, border, row):
        if rows <= row < 2 * rows:
            return pre[layer, row - rows]
        start = starts[2 - layer]
        if row < rows:
            k = row - (rows - border)
            return jnp.where(even, m_b[start + k], m_a[start + k])
        k = row - 2 * rows
        return jnp.where(even, m_a[start + k], m_b[start + k])

    def store(dst, layer, border):
        first = rows - border

        def emit(row, e):
            a = mask_rows(layer, border, row).astype(F32)
            dst[(row - first) * ch : (row - first + 1) * ch, :] = jnp.where(
                a > 0, e, 0.0
            ).astype(BF16)

        return emit

    row, emit = rows - e3, store(d3, 2, e3)
    while row < 2 * rows + e3:
        count = min(BLOCK4, 2 * rows + e3 - row)
        rhs = x4[SMALL * (row - 1) : SMALL * (row + count + 1), :].astype(BF16)
        y = jnp.dot(
            w4[: count * ch, : SMALL * (count + 2)], rhs, preferred_element_type=F32
        )
        for k in range(count):
            emit(row + k, y[k * ch : (k + 1) * ch])
        row += count
    row_conv(w3, d3, rows - e3, rows - e2, 2 * rows + e2, ch, store(d2, 1, e2))
    row_conv(w2, d2, rows - e2, rows - e1, 2 * rows + e1, ch, store(d1, 0, e1))


def first_conv(w1, d1, src0, lo, hi, ch, emit):
    row = lo
    while row < hi:
        start = min(row, hi - BLOCK)
        rhs = d1[(start - 1 - src0) * ch : (start + BLOCK + 1 - src0) * ch, :]
        y = jnp.dot(w1[...], rhs, preferred_element_type=F32)
        e = (
            y[SMALL : 2 * SMALL]
            + lane_roll(y[:SMALL], -1)
            + lane_roll(y[2 * SMALL : 3 * SMALL], 1)
        )
        for k in range(row - start, BLOCK):
            emit(start + k, [e[2 * k + comp : 2 * k + comp + 1, :] for comp in range(2)])
        row = start + BLOCK


def weight_terms(x4, d3, d2, d1, firsts, pre, x0s, rows, ch):
    dims = (((1,), (1,)), ((), ()))

    def product(a, b):
        return lax.dot_general(a, b, dims, preferred_element_type=F32)

    def three(ref, first, row):
        return ref[(row - 1 - first) * ch : (row + 2 - first) * ch, :]

    g1 = g2 = g3 = g4 = None

    def add(total, term):
        return term if total is None else total + term

    for i in range(rows):
        row = rows + i
        source = [jnp.maximum(pre[layer, i].astype(F32), 0.0) for layer in range(3)]
        moved = [
            jnp.concatenate([lane_roll(s, 1), s, lane_roll(s, -1)], axis=0).astype(BF16)
            for s in source[:2]
        ]
        g4 = add(
            g4,
            product(
                x4[SMALL * (row - 1) : SMALL * (row + 2), :].astype(BF16),
                source[2].astype(BF16),
            ),
        )
        g3 = add(g3, product(three(d3, firsts[0], row), moved[1]))
        g2 = add(g2, product(three(d2, firsts[1], row), moved[0]))
        g1 = add(
            g1,
            product(
                three(d1, firsts[2], row),
                x0s[SMALL * i : SMALL * (i + 1), :].astype(BF16),
            ),
        )
    return g1, g2, g3, g4


def pack_rows(ch):
    return 2 * 3 * ch + 3 * ch // 2 + 3 * SMALL


def pack_terms(t_ref, terms, ch, before=None):
    g1, g2, g3, g4 = terms
    n = 3 * ch
    rest = n - LANES
    tail = jnp.concatenate([g2[:, LANES:], g3[:, LANES:], g1], axis=1)
    wide = tail.shape[1]
    half = n // 2
    parts = (
        (0, n, 0, LANES, g2[:, :LANES]),
        (n, 2 * n, 0, LANES, g3[:, :LANES]),
        (2 * n, 2 * n + half, 0, wide, tail[:half]),
        (2 * n, 2 * n + half, wide, 2 * wide, tail[half:]),
        (2 * n + half, 2 * n + half + 3 * SMALL, 0, ch, g4),
    )
    if before is None:
        t_ref[2 * n :, :] = jnp.zeros((t_ref.shape[0] - 2 * n, LANES), F32)
    else:
        t_ref[2 * n :, :] = before[2 * n :, :]
    for r0, r1, c0, c1, value in parts:
        if before is not None:
            value = value + before[r0:r1, c0:c1]
        t_ref[r0:r1, c0:c1] = value


def gather_kernel(axis, takes, rows, pre_hbm, out_a, out_b, sems):
    even = lax.rem(lax.axis_index(axis), 2) == 0
    copies = []
    for step, layer, count, dst in takes:
        low, high = 0, rows - count
        for out, start in (
            (out_a, jnp.where(even, high, low)),
            (out_b, jnp.where(even, low, high)),
        ):
            copy = pltpu.make_async_copy(
                pre_hbm.at[step, layer, pl.ds(start, count)],
                out.at[pl.ds(dst, count)],
                sems.at[len(copies)],
            )
            copy.start()
            copies.append(copy)
    for copy in copies:
        copy.wait()


def back_kernel(
    axis, rows, ch, extra,
    cot, cot_a, cot_b, pre, m_a, m_b, w4, w3, w2, w1,
    gh, x4, d3, d2, d1,
):
    even = lax.rem(lax.axis_index(axis), 2) == 0
    planes = [joined(cot_a, cot, cot_b, even, comp) for comp in range(2)]
    fill_small(x4, planes, 3 * rows, 0, 1)
    chain(x4, pre.at[0], m_a, m_b, even, w4, w3, w2, d3, d2, d1, rows, ch, extra)

    def emit(row, values):
        for comp in range(2):
            i = row - rows
            gh[comp, i : i + 1, :] = cot[comp, i : i + 1, :] + values[comp]

    first_conv(w1, d1, rows - extra[2], rows, 2 * rows, ch, emit)


def term_kernel(axis, rows, ch, extra, x4, d3, d2, d1, pre, u, u_a, u_b, t_out, x0s):
    even = lax.rem(lax.axis_index(axis), 2) == 0
    planes = [joined(u_a, u, u_b, even, comp) for comp in range(2)]
    fill_small(x0s, half_step(*planes), rows, rows, -1)
    firsts = [rows - e for e in extra]
    pack_terms(t_out, weight_terms(x4, d3, d2, d1, firsts, pre.at[0], x0s, rows, ch), ch)


def front_kernel(
    axis, rows, ch, extra,
    gh, gh_a, gh_b, u1, u1_a, u1_b, u0, u0_a, u0_b, pre, m_a, m_b, w4, w3, w2, before,
    t_out, g_out, d1, x4, d3, d2, x0s,
):
    even = lax.rem(lax.axis_index(axis), 2) == 0
    lam = [joined(gh_a, gh, gh_b, even, comp) for comp in range(2)]
    u = [joined(u1_a, u1, u1_b, even, comp) for comp in range(2)]
    planes = half_step_transpose(*u, *lam)
    for comp in range(2):
        g_out[comp] = planes[comp]
    fill_small(x4, planes, 3 * rows, 0, 1)
    u = [joined(u0_a, u0, u0_b, even, comp) for comp in range(2)]
    fill_small(x0s, half_step(*u), rows, rows, -1)
    chain(x4, pre.at[0], m_a, m_b, even, w4, w3, w2, d3, d2, d1, rows, ch, extra)
    firsts = [rows - e for e in extra]
    pack_terms(
        t_out, weight_terms(x4, d3, d2, d1, firsts, pre.at[0], x0s, rows, ch), ch, before
    )


def last_kernel(axis, rows, ch, extra, g, d1, u0, u0_a, u0_b, w1, out, gh):
    even = lax.rem(lax.axis_index(axis), 2) == 0
    for comp in range(2):
        gh[comp] = g[comp]

    def emit(row, values):
        for comp in range(2):
            gh[comp, row : row + 1, :] = g[comp, row : row + 1, :] + values[comp]

    first_conv(w1, d1, rows - extra[2], rows - 1, 2 * rows + 1, ch, emit)
    u = [joined(u0_a, u0, u0_b, even, comp) for comp in range(2)]
    planes = half_step_transpose(*u, gh[0], gh[1])
    for comp in range(2):
        out[comp] = planes[comp][rows : 2 * rows]


def unpack_kernel(axis, ch, factor, mine, other, o1, o2, o3, o4):
    even = lax.rem(lax.axis_index(axis), 2) == 0
    a, b = mine[...].astype(F32), other[...].astype(F32)
    t = factor * jnp.concatenate([jnp.where(even, a, b), jnp.where(even, b, a)], axis=0)
    n = 3 * ch
    rest = n - LANES
    half = n // 2
    wide = 2 * rest + SMALL
    low = t[2 * n : 2 * n + half]
    tail = jnp.concatenate([low[:, :wide], low[:, wide : 2 * wide]], axis=0)
    g2 = jnp.concatenate([t[:n], tail[:, :rest]], axis=1)
    g3 = jnp.concatenate([t[n : 2 * n], tail[:, rest : 2 * rest]], axis=1)
    g1 = tail[:, 2 * rest : 2 * rest + SMALL]
    g4 = t[2 * n + half : 2 * n + half + 3 * SMALL, :ch]
    for m in range(3):
        for q in range(3):
            tap = 3 * (2 - m) + q
            o2[tap] = g2[m * ch : (m + 1) * ch, q * ch : (q + 1) * ch]
            o3[tap] = g3[m * ch : (m + 1) * ch, q * ch : (q + 1) * ch]
            o1[tap] = g1[m * ch : (m + 1) * ch, 2 * q : 2 * q + 2]
            o4[tap] = g4[m * SMALL + 2 * q : m * SMALL + 2 * q + 2, :]


def band(weight, count):
    taps, o, k = weight.shape
    w = weight.reshape(3, 3, o, k)[::-1]
    w = jnp.transpose(w, (1, 3, 0, 2)).reshape(3 * k, 3 * o)
    return jnp.concatenate(
        [jnp.pad(w, ((0, 0), (b * o, (count - 1 - b) * o))) for b in range(count)], axis=0
    )


def band_last(weight, count):
    taps, o, k = weight.shape
    w = weight.reshape(3, 3, o, k)[::-1]
    w = jnp.transpose(w, (3, 0, 1, 2)).reshape(k, 3, 3 * o)
    w = jnp.pad(w, ((0, 0), (0, 0), (0, SMALL - 3 * o))).reshape(k, 3 * SMALL)
    return jnp.concatenate(
        [jnp.pad(w, ((0, 0), (b * SMALL, (count - 1 - b) * SMALL))) for b in range(count)],
        axis=0,
    )


def band_first(weight, count):
    taps, o, k = weight.shape
    w = weight.reshape(3, 3, o, k)[::-1]
    w = jnp.transpose(w, (1, 3, 0, 2)).reshape(3, k, 3 * o)
    w = jnp.concatenate(
        [
            jnp.pad(w, ((0, 0), (0, 0), (b * o, (count - 1 - b) * o)))
            for b in range(count)
        ],
        axis=1,
    )
    w = jnp.pad(w, ((0, 0), (0, SMALL - count * k), (0, 0)))
    return w.reshape(3 * SMALL, (count + 2) * o)


VMEM = pl.BlockSpec(memory_space=pltpu.VMEM)


def call(kernel, outs, scratch, args, specs=None, limit=24 << 20, flops=10**8):
    specs = specs or {}
    return pl.pallas_call(
        kernel,
        out_shape=outs,
        grid=(1,) if specs else (),
        in_specs=[specs.get(i, VMEM) for i in range(len(args))],
        out_specs=jax.tree.map(lambda _: VMEM, outs),
        scratch_shapes=scratch,
        compiler_params=pltpu.CompilerParams(vmem_limit_bytes=limit),
        cost_estimate=pl.CostEstimate(
            flops=flops, bytes_accessed=2 * 10**6, transcendentals=0
        ),
    )(*args)


def on_device(states, pre_acts, cotangent, weight_in, weight_second, weight_third, weight_out):
    axis = "gx"
    count = lax.axis_size(axis)
    _, _, rows, width = states.shape
    ch = pre_acts.shape[3]

    pair_a = [(i, i ^ 1) for i in range(count)]
    pair_b = [(i, (i + 1) % count if i % 2 else (i - 1) % count) for i in range(count)]

    def swap(for_a, for_b):
        return lax.ppermute(for_a, axis, pair_a), lax.ppermute(for_b, axis, pair_b)

    def shape(*dims, dtype=F32):
        return jax.ShapeDtypeStruct(dims, dtype)

    back_extra, front_extra = (3, 2, 1), (4, 3, 2)

    def borders(step, extra):
        takes, total = [], 0
        for layer, border in zip((2, 1, 0), extra):
            takes.append((step, layer, border, total))
            total += border
        out = shape(total, ch, width, dtype=BF16)
        return pl.pallas_call(
            functools.partial(gather_kernel, axis, takes, rows),
            out_shape=[out, out],
            in_specs=[pl.BlockSpec(memory_space=pl.ANY)],
            out_specs=[VMEM, VMEM],
            scratch_shapes=[pltpu.SemaphoreType.DMA((2 * len(takes),))],
            compiler_params=pltpu.CompilerParams(vmem_limit_bytes=8 << 20),
        )(pre_acts)

    cot_a, cot_b = swap(cotangent, cotangent)
    m1_a, m1_b = swap(*borders(1, back_extra))
    u_all = states.reshape((-1,) + states.shape[2:])
    u_a, u_b = swap(u_all, u_all)
    m0_a, m0_b = swap(*borders(0, front_extra))
    u1, u1_a, u1_b = states[1], u_a[2:], u_b[2:]
    u0, u0_a, u0_b = states[0], u_a[:2], u_b[:2]

    w4 = band_last(weight_out, BLOCK4)
    w3 = band(weight_third, BLOCK)
    w2 = band(weight_second, BLOCK)
    w1 = band_first(weight_in, BLOCK)

    def pre_spec(step):
        return pl.BlockSpec(
            (1,) + pre_acts.shape[1:], lambda *_: (step, 0, 0, 0, 0)
        )

    def d_shapes(extra):
        return [shape((rows + 2 * e) * ch, width, dtype=BF16) for e in extra]

    x4_shape = shape(3 * rows * SMALL, width)
    gh, x4, d3, d2, d1 = call(
        functools.partial(back_kernel, axis, rows, ch, back_extra),
        [shape(2, rows, width), x4_shape] + d_shapes(back_extra),
        [],
        (cotangent, cot_a, cot_b, pre_acts, m1_a, m1_b, w4, w3, w2, w1),
        {3: pre_spec(1)},
    )
    gh_a, gh_b = swap(gh, gh)
    x0s = pltpu.VMEM((rows * SMALL, width), F32)
    before = call(
        functools.partial(term_kernel, axis, rows, ch, back_extra),
        shape(pack_rows(ch), LANES),
        [x0s],
        (x4, d3, d2, d1, pre_acts, u1, u1_a, u1_b),
        {4: pre_spec(1)},
    )
    front_d = d_shapes(front_extra)
    total, g, d1 = call(
        functools.partial(front_kernel, axis, rows, ch, front_extra),
        [shape(pack_rows(ch), LANES), shape(2, 3 * rows, width), front_d[2]],
        [pltpu.VMEM(x4_shape.shape, F32)]
        + [pltpu.VMEM(s.shape, s.dtype) for s in front_d[:2]]
        + [x0s],
        (gh, gh_a, gh_b, u1, u1_a, u1_b, u0, u0_a, u0_b, pre_acts, m0_a, m0_b, w4, w3, w2, before),
        {9: pre_spec(0)},
    )
    adjoint = call(
        functools.partial(last_kernel, axis, rows, ch, front_extra),
        shape(2, rows, width),
        [pltpu.VMEM((2, 3 * rows, width), F32)],
        (g, d1, u0, u0_a, u0_b, w1),
    )

    side = lax.rem(lax.axis_index(axis), 2)
    half = total.shape[0] // 2
    keep = lax.dynamic_slice_in_dim(total, side * half, half, 0)
    give = lax.dynamic_slice_in_dim(total, (1 - side) * half, half, 0)
    mine = keep + lax.ppermute(give, axis, pair_a)
    bit = 2
    while bit < count:
        others = [bit] if bit == 2 or 2 * bit >= count else [bit, 2 * bit, 3 * bit]
        got = [
            lax.ppermute(mine, axis, [(i, i ^ b) for i in range(count)]) for b in others
        ]
        if len(others) == 1:
            mine = mine + got[0]
            bit *= 2
        else:
            mine = (mine + got[0]) + (got[1] + got[2])
            bit *= 4
    other = lax.ppermute(mine, axis, pair_a)
    factor = 1.0 / math.sqrt(rows * count * width)
    g1, g2, g3, g4 = call(
        functools.partial(unpack_kernel, axis, ch, factor),
        [shape(*w.shape) for w in (weight_in, weight_second, weight_third, weight_out)],
        [],
        (mine, other),
    )
    return adjoint, g1, g2, g3, g4


def solution(mesh):
    return jax.shard_map(
        on_device,
        mesh=mesh,
        in_specs=(
            P(None, "groups", "gx", None),
            P(None, None, ("groups", "gx"), None, None),
            P("groups", "gx", None),
            P(),
            P(),
            P(),
            P(),
        ),
        out_specs=(
            P("groups", "gx", None),
            P("groups", None, None),
            P("groups", None, None),
            P("groups", None, None),
            P("groups", None, None),
        ),
        check_vma=False,
    )
```

time: 231 us -> 66.9 us (0.29)
  blocking collectives: 62 us -> 0 us
  matrix products: 42.7 us -> 0 us
  starting transfers between devices: 50.1 us -> 21.9 us
  waiting for transfers between devices: 39.1 us -> 12.6 us
  between operations: 15.4 us -> 0.88 us
  Pallas kernels: 0 us -> 13.9 us
  other arithmetic: 11.9 us -> 2.33 us
  local copies, waits for them, and re-layouts: 9.14 us -> 14.6 us
    psum x1 -> x0, blocking collectives: 62 us -> none  [on_device(): lax.psum((grad_totals[0], grad_totals[1], grad_totals[2], grad_totals[3])...]
    dot_general x144 -> x0, matrix products: 42.7 us -> none  [the longest x72 23.3 us: back_conv(): jnp.einsum('ok,roy->rky', kernel[3 * row_tap + col_tap], section, preferr...]
    ppermute x24 -> x16, starting transfers between devices: 50.1 us -> 21.9 us  [the longest x5 14.6 us: swap(): lax.ppermute(for_b, axis, pair_b)]
    psum x1 -> x0, waiting for transfers between devices: 20.6 us -> none  [on_device(): lax.psum((grad_totals[0], grad_totals[1], grad_totals[2], grad_totals[3])...]
    pallas_call x0 -> x7, Pallas kernels: none -> 13.9 us  [the longest x5 11 us: call(): pl.pallas_call(kernel, out_shape=outs, grid=(1,) if specs else (), in_spe...]
    unnamed x14 -> x31, local copies, waits for them, and re-layouts: 0.91 us -> 8.36 us
    ppermute x24 -> x16, waiting for transfers between devices: 18.4 us -> 12.6 us  [the longest x4 11.1 us: on_device(): lax.ppermute(mine, axis, [(i, i ^ b) for i in range(count)])]
    mul x15 -> x0, other arithmetic: 4.93 us -> none  [the longest x1 1.64 us: on_device(): summed[2] * factor]
  transfers between devices with their start and end apart: 25 -> 16, of which waited for: 12 -> 5; matrix products, arithmetic and copies ran while one was open for 9% -> 10% of each run, Pallas kernels for 0% -> 13%
where the time goes in v1:
time: 66.9 us; the launch traced here: 66.2 us
  starting transfers between devices  21.9 us (33%)
  local copies, waits for them, and re-layouts  14.6 us (22%)
  Pallas kernels  13.9 us (21%)
  waiting for transfers between devices  12.6 us (19%)
  other arithmetic  2.33 us (3%)
  between operations  0.88 us (1%)
    ppermute x5, starting transfers between devices, swap(): lax.ppermute(for_b, axis, pair_b)  14.6 us
    ppermute x4, waiting for transfers between devices, on_device(): lax.ppermute(mine, axis, [(i, i ^ b) for i in range(count)])  11.1 us
    pallas_call x5, Pallas kernels, call(): pl.pallas_call(kernel, out_shape=outs, grid=(1,) if specs else (), in_spe...  11 us
    unnamed x31, local copies, waits for them, and re-layouts  8.36 us
    ppermute x4, starting transfers between devices, on_device(): lax.ppermute(mine, axis, [(i, i ^ b) for i in range(count)])  4.59 us
    pallas_call x2, Pallas kernels, borders(): pl.pallas_call(functools.partial(gather_kernel, axis, takes, rows), out_s...  2.89 us
    rev x2, local copies, waits for them, and re-layouts, band(): w = weight.reshape(3, 3, o, k)[::-1]  1.66 us
    reshape x2, local copies, waits for them, and re-layouts, band(): w = jnp.transpose(w, (1, 3, 0, 2)).reshape(3 * k, 3 * o)  1.52 us
  transfers between devices with their start and end apart: 16, of which 5 were waited for; matrix products, arithmetic and copies ran while one was open for 10% of the time, Pallas kernels for 13%

profile of v1, /device:TPU:0, one launch (start us, length us, event | category | flops | bytes accessed | tf_op | source)
XLA Modules:
  0.0 66.2 jit_solution(5270003321405262653)
XLA Ops:
  0.6 0.6 collective-permute-start
  1.2 5.6 %collective-permute-start.1 = (f32[2,8,512]{2,1,0:T(8,128)}, f32[2,8,512]{2,1,0:T(8,128)}, u32[]{:S(2)}, u32[]{:S(2)}) collective-permute-start(f32[2,8,512]{2,1,0:T(8,128)} %cot.1), channel_id=1, source_target_pairs={{0,15},{1,2},{2,1},{3,4},{4,3},{5,6},{6,5},{7,8},{8,7},{9,10},{10,... | collective-permute-start | bytes 98312 | tf_op jit(solution)/shard_map/ppermute | solution.py:401
  6.8 1.7 %copy-done = bf16[2,3,8,48,512]{4,3,2,1,0:T(8,128)(2,1)S(1)} copy-done((bf16[2,3,8,48,512]{4,3,2,1,0:T(8,128)(2,1)S(1)}, bf16[2,3,8,48,512]{4,3,2,1,0:T(8,128)(2,1)}, u32[]{:S(2)}) %copy-start) | copy-done | bytes 2359320
  8.5 1.7 %shard_map.110 = (bf16[6,48,512]{2,1,0:T(8,128)(2,1)}, bf16[6,48,512]{2,1,0:T(8,128)(2,1)}) custom-call(bf16[2,3,8,48,512]{4,3,2,1,0:T(8,128)(2,1)S(1)} %copy-done), custom_call_target="tpu_custom_call" | custom-call | tf_op jit(solution)/shard_map/pallas_call | solution.py:414
  10.2 0.1 collective-permute-start.2
  10.3 0.6 collective-permute-start.3
  10.9 3.9 %collective-permute-start.7 = (f32[4,8,512]{2,1,0:T(8,128)}, f32[4,8,512]{2,1,0:T(8,128)}, u32[]{:S(2)}, u32[]{:S(2)}) collective-permute-start(f32[4,8,512]{2,1,0:T(8,128)} %bitcast.24), channel_id=1, source_target_pairs={{0,15},{1,2},{2,1},{3,4},{4,3},{5,6},{6,5},{7,8},{8,7},{9,10},{10,... | collective-permute-start | bytes 196616 | tf_op jit(solution)/shard_map/ppermute | solution.py:401
  14.8 0.8 %slice_bitcast_fusion = (f32[2,8,512]{2,1,0:T(8,128)S(1)}, f32[2,8,512]{2,1,0:T(8,128)S(1)}) fusion(f32[2,2,8,512]{3,2,1,0:T(8,128)} %param.7), kind=kLoop, calls=%fused_computation.34 | loop fusion | bytes 131072 | tf_op jit(solution)/shard_map/squeeze | solution.py:429
  15.6 0.1 copy.21
  15.7 0.8 %rev.13 = bf16[3,3,48,48]{2,0,3,1:T(4,128)(2,1)S(1)} reverse(bf16[3,3,48,48]{2,0,3,1:T(4,128)(2,1)S(1)} %copy.21), dimensions={0} | reverse | bytes 82944 | tf_op jit(solution)/shard_map/rev | solution.py:339
  16.6 0.8 %reshape.47 = bf16[144,144]{1,0:T(8,128)(2,1)} reshape(bf16[3,48,3,48]{3,2,1,0:T(4,128)(2,1)S(1)} %bitcast.20) | data formatting | bytes 82944 | tf_op jit(solution)/shard_map/reshape | solution.py:340
  17.3 0.1 copy.22
  17.5 0.8 %rev.14 = bf16[3,3,48,48]{2,0,3,1:T(4,128)(2,1)S(1)} reverse(bf16[3,3,48,48]{2,0,3,1:T(4,128)(2,1)S(1)} %copy.22), dimensions={0} | reverse | bytes 82944 | tf_op jit(solution)/shard_map/rev | solution.py:339
  18.3 0.8 %reshape.49 = bf16[144,144]{1,0:T(8,128)(2,1)} reshape(bf16[3,48,3,48]{3,2,1,0:T(4,128)(2,1)S(1)} %bitcast.21) | data formatting | bytes 82944 | tf_op jit(solution)/shard_map/reshape | solution.py:340
  19.1 0.1 copy.17
  19.2 0.1 fusion.18.w4
  19.4 0.1 reshape.51
  19.5 0.1 fusion.25
  19.5 1.2 %fusion.8 = (bf16[432,240]{1,0:T(8,128)(2,1)S(1)}, bf16[432,240]{1,0:T(8,128)(2,1)S(1)}) fusion(bf16[144,144]{1,0:T(8,128)(2,1)} %reshape.47, bf16[144,144]{1,0:T(8,128)(2,1)} %reshape.49), kind=kLoop, calls=%fused_computation.12 | loop fusion | flops 2384640 | bytes 497664 | tf_op jit(solution)/shard_map/concatenate | solution.py:341
  20.8 1.2 %shard_map.112 = (bf16[9,48,512]{2,1,0:T(8,128)(2,1)S(1)}, bf16[9,48,512]{2,1,0:T(8,128)(2,1)S(1)}) custom-call(bf16[2,3,8,48,512]{4,3,2,1,0:T(8,128)(2,1)S(1)} %copy-done.1), custom_call_target="tpu_custom_call" | custom-call | tf_op jit(solution)/shard_map/pallas_call | solution.py:414
  22.0 0.8 %copy-done.9 = bf16[9,48,512]{2,1,0:T(8,128)(2,1)} copy-done((bf16[9,48,512]{2,1,0:T(8,128)(2,1)}, bf16[9,48,512]{2,1,0:T(8,128)(2,1)S(1)}, u32[]{:S(2)}) %copy-start.9) | copy-done | bytes 442392
  22.8 0.8 %copy-done.10 = bf16[9,48,512]{2,1,0:T(8,128)(2,1)} copy-done((bf16[9,48,512]{2,1,0:T(8,128)(2,1)}, bf16[9,48,512]{2,1,0:T(8,128)(2,1)S(1)}, u32[]{:S(2)}) %copy-start.10) | copy-done | bytes 442392
  23.6 0.0 collective-permute-done.cot_a
  23.6 0.6 copy-done.7
  24.2 0.0 collective-permute-start.6
  24.2 0.0 collective-permute-done.1.cot_b
  24.2 0.5 collective-permute-start.8
  24.7 0.0 collective-permute-done.7
  24.7 0.6 collective-permute-start.9
  25.3 0.8 %fusion.26 = (f32[2,8,512]{2,1,0:T(8,128)S(1)}, f32[2,8,512]{2,1,0:T(8,128)S(1)}) fusion(f32[4,8,512]{2,1,0:T(8,128)} %collective-permute-done.7), kind=kLoop, calls=%fused_computation.48 | loop fusion | bytes 131072 | tf_op jit(solution)/shard_map/slice | solution.py:429
  26.1 0.0 collective-permute-done.2.m_a
  26.1 0.0 copy-start.6
  26.1 0.7 %copy-done.6 = f32[2,8,512]{2,1,0:T(8,128)S(1)} copy-done((f32[2,8,512]{2,1,0:T(8,128)S(1)}, f32[2,8,512]{2,1,0:T(8,128)}, u32[]{:S(2)}) %copy-start.6) | copy-done | bytes 32792
  26.8 0.8 %copy-done.8 = f32[2,8,512]{2,1,0:T(8,128)S(1)} copy-done((f32[2,8,512]{2,1,0:T(8,128)S(1)}, f32[2,8,512]{2,1,0:T(8,128)}, u32[]{:S(2)}) %copy-start.8) | copy-done | bytes 32792
  27.6 2.8 %shard_map.111 = (f32[2,8,512]{2,1,0:T(8,128)S(1)}, f32[192,512]{1,0:T(8,128)S(1)}, bf16[672,512]{1,0:T(8,128)(2,1)S(1)}, bf16[576,512]{1,0:T(8,128)(2,1)S(1)}, bf16[480,512]{1,0:T(8,128)(2,1)S(1)}) custom-call(f32[2,8,512]{2,1,0:T(8,128)S(1)} %copy-done.6, f32[2,8,512]{2,1,0:T(8,128)S(1)} %copy-done.8, f32[2,8,512]{2,1,0:T(8,128)} %collective-permute-done.1.cot_b, ...), custom_call_target="tpu_custom_call" | custom-call | flops 100000000 | bytes 2000000 | tf_op jit(solution)/shard_map/pallas_call | solution.py:377
  30.5 0.1 collective-permute-start.4
  30.5 3.9 %collective-permute-start.5 = (f32[2,8,512]{2,1,0:T(8,128)S(1)}, f32[2,8,512]{2,1,0:T(8,128)S(1)}, u32[]{:S(2)}, u32[]{:S(2)}) collective-permute-start(f32[2,8,512]{2,1,0:T(8,128)S(1)} %get-tuple-element.23.gh), channel_id=1, source_target_pairs={{0,15},{1,2},{2,1},{3,4},{4,3},{5,6},{6,5},{7,8},{8,7},{9,10},{10,... | collective-permute-start | bytes 98312 | tf_op jit(solution)/shard_map/ppermute | solution.py:401
  34.5 0.0 copy-start.2
  34.5 1.7 %shard_map.113.before = f32[384,128]{1,0:T(8,128)S(1)} custom-call(f32[192,512]{1,0:T(8,128)S(1)} %get-tuple-element.26.x4, bf16[672,512]{1,0:T(8,128)(2,1)S(1)} %get-tuple-element.27.d3, bf16[576,512]{1,0:T(8,128)(2,1)S(1)} %get-tuple-element.28.d2, bf16[480,512]{1,0:T(8,128)(2,1)S(1)} %get-tuple-element.29.d1, bf16[2,3,8,48,512]{4,3,2,1,0:T(8,128)(2,1)S(1)} %copy-done.1, ...), custom_call_target="tpu_custom_call" | custom-call | flops 100000000 | bytes 2000000 | tf_op jit(solution)/shard_map/pallas_call | solution.py:377
  36.2 0.0 collective-permute-done.4.gh_a
  36.2 0.6 collective-permute-done.5.gh_b
  36.7 0.0 collective-permute-done.8.m_a
  36.7 0.0 collective-permute-done.9.m_b
  36.7 4.3 %shard_map.114 = (f32[384,128]{1,0:T(8,128)}, f32[2,24,512]{2,1,0:T(8,128)S(1)}, bf16[576,512]{1,0:T(8,128)(2,1)S(1)}) custom-call(f32[2,8,512]{2,1,0:T(8,128)S(1)} %get-tuple-element.23.gh, f32[2,8,512]{2,1,0:T(8,128)S(1)} %collective-permute-done.4.gh_a, f32[2,8,512]{2,1,0:T(8,128)S(1)} %collective-permute-done.5.gh_b, ...), custom_call_target="tpu_custom_call" | custom-call | flops 100000000 | bytes 2000000 | tf_op jit(solution)/shard_map/pallas_call | solution.py:377
  41.1 0.6 copy-done.4
  41.7 0.9 %constant_dynamic-slice_fusion = f32[192,128]{1,0:T(8,128)S(1)} fusion(f32[384,128]{1,0:T(8,128)} %get-tuple-element.32, s32[]{:T(128)S(6)} %select_n.7), kind=kLoop, calls=%fused_computation.47 | loop fusion | bytes 196612 | tf_op jit(solution)/shard_map/dynamic_slice | solution.py:481
  42.6 1.4 %collective-permute-start.10 = (f32[192,128]{1,0:T(8,128)S(1)}, f32[192,128]{1,0:T(8,128)S(1)}, u32[]{:S(2)}, u32[]{:S(2)}) collective-permute-start(f32[192,128]{1,0:T(8,128)S(1)} %constant_dynamic-slice_fusion), channel_id=1, source_target_pairs={{0,1},{1,0},{2,3},{3,2},{4,5},{5,4},{6,7},{7,6},{8,9},{9,8},{10,11... | collective-permute-start | bytes 294920 | tf_op jit(solution)/shard_map/ppermute | solution.py:482
  44.1 0.9 %collective-permute-done.10 = f32[192,128]{1,0:T(8,128)S(1)} collective-permute-done((f32[192,128]{1,0:T(8,128)S(1)}, f32[192,128]{1,0:T(8,128)S(1)}, u32[]{:S(2)}, u32[]{:S(2)}) %collective-permute-start.10) | collective-permute-done | bytes 98336 | tf_op jit(solution)/shard_map/ppermute | solution.py:482
  45.0 0.9 %dynamic-slice_add_fusion = f32[192,128]{1,0:T(8,128)S(1)} fusion(f32[192,128]{1,0:T(8,128)S(1)} %collective-permute-done.10, f32[384,128]{1,0:T(8,128)} %get-tuple-element.32, s32[]{:T(128)S(6)} %select_n.6), kind=kLoop, calls=%fused_computation.22 | loop fusion | flops 24576 | bytes 294916 | tf_op jit(solution)/shard_map/add | solution.py:482
  45.9 0.1 collective-permute-start.11
  46.1 5.0 %collective-permute-done.11 = f32[192,128]{1,0:T(8,128)S(1)} collective-permute-done((f32[192,128]{1,0:T(8,128)S(1)}, f32[192,128]{1,0:T(8,128)S(1)}, u32[]{:S(2)}, u32[]{:S(2)}) %collective-permute-start.11) | collective-permute-done | bytes 98336 | tf_op jit(solution)/shard_map/ppermute | solution.py:487
  51.0 0.1 collective-permute-start.12
  51.1 2.1 %collective-permute-start.13 = (f32[192,128]{1,0:T(8,128)S(1)}, f32[192,128]{1,0:T(8,128)S(1)}, u32[]{:S(2)}, u32[]{:S(2)}) collective-permute-start(f32[192,128]{1,0:T(8,128)S(1)} %add.54), channel_id=1, source_target_pairs={{0,8},{1,9},{2,10},{3,11},{4,12},{5,13},{6,14},{7,15},{8,0},{9,1},... | collective-permute-start | bytes 294920 | tf_op jit(solution)/shard_map/ppermute | solution.py:487
  53.2 2.2 %collective-permute-start.14 = (f32[192,128]{1,0:T(8,128)S(1)}, f32[192,128]{1,0:T(8,128)S(1)}, u32[]{:S(2)}, u32[]{:S(2)}) collective-permute-start(f32[192,128]{1,0:T(8,128)S(1)} %add.54), channel_id=1, source_target_pairs={{0,12},{1,13},{2,14},{3,15},{4,8},{5,9},{6,10},{7,11},{8,4},{9,5},... | collective-permute-start | bytes 294920 | tf_op jit(solution)/shard_map/ppermute | solution.py:487
  55.5 0.9 %collective-permute-done.12 = f32[192,128]{1,0:T(8,128)S(1)} collective-permute-done((f32[192,128]{1,0:T(8,128)S(1)}, f32[192,128]{1,0:T(8,128)S(1)}, u32[]{:S(2)}, u32[]{:S(2)}) %collective-permute-start.12) | collective-permute-done | bytes 98336 | tf_op jit(solution)/shard_map/ppermute | solution.py:487
  56.4 5.2 %collective-permute-done.13 = f32[192,128]{1,0:T(8,128)S(1)} collective-permute-done((f32[192,128]{1,0:T(8,128)S(1)}, f32[192,128]{1,0:T(8,128)S(1)}, u32[]{:S(2)}, u32[]{:S(2)}) %collective-permute-start.13) | collective-permute-done | bytes 98336 | tf_op jit(solution)/shard_map/ppermute | solution.py:487
  61.6 0.0 collective-permute-done.14
  61.6 0.1 collective-permute-start.15
  61.7 0.0 copy-start.3
  61.7 0.7 %copy-done.3 = f32[2,8,512]{2,1,0:T(8,128)S(1)} copy-done((f32[2,8,512]{2,1,0:T(8,128)S(1)}, f32[2,8,512]{2,1,0:T(8,128)}, u32[]{:S(2)}) %copy-start.3) | copy-done | bytes 32792
  62.4 0.9 %copy-done.5 = f32[2,24,512]{2,1,0:T(8,128)S(1)} copy-done((f32[2,24,512]{2,1,0:T(8,128)S(1)}, f32[2,24,512]{2,1,0:T(8,128)}, u32[]{:S(2)}) %copy-start.5) | copy-done | bytes 98328
  63.3 1.1 %shard_map.115 = f32[2,8,512]{2,1,0:T(8,128)} custom-call(f32[2,24,512]{2,1,0:T(8,128)S(1)} %copy-done.5, bf16[576,512]{1,0:T(8,128)(2,1)S(1)} %get-tuple-element.31.d1, f32[2,8,512]{2,1,0:T(8,128)S(1)} %get-tuple-element.51.u0, f32[2,8,512]{2,1,0:T(8,128)S(1)} %copy-done.3, f32[2,8,512]{2,1,0:T(8,128)S(1)} %get-tuple-element.47.u0_b, ...), custom_call_target="tpu_custom_call" | custom-call | flops 100000000 | bytes 2000000 | tf_op jit(solution)/shard_map/pallas_call | solution.py:377
  64.4 1.0 %shard_map.116 = (f32[9,48,2]{2,1,0:T(8,128)S(1)}, f32[9,48,48]{2,1,0:T(8,128)}, f32[9,48,48]{2,1,0:T(8,128)}, f32[9,2,48]{2,1,0:T(2,128)}) custom-call(f32[192,128]{1,0:T(8,128)S(1)} %add_add_fusion.mine, f32[192,128]{1,0:T(8,128)S(1)} %collective-permute-done.15.other), custom_call_target="tpu_custom_call" | custom-call | flops 100000000 | bytes 2000000 | tf_op jit(solution)/shard_map/pallas_call | solution.py:377
  65.5 0.7 %copy.24 = f32[9,48,2]{1,2,0:T(2,128)} copy(f32[9,48,2]{2,1,0:T(8,128)S(1)} %get-tuple-element.43) | data formatting | bytes 6912
  (30 shorter events, 0.2 us)
Async XLA Ops:
  0.6 22.9 %collective-permute-start = (f32[2,8,512]{2,1,0:T(8,128)}, f32[2,8,512]{2,1,0:T(8,128)S(1)}, u32[]{:S(2)}, u32[]{:S(2)}) collective-permute-start(f32[2,8,512]{2,1,0:T(8,128)} %cot.1), channel_id=1, source_target_pairs={{0,1},{1,0},{2,3},{3,2},{4,5},{5,4},{6,7},{7,6},{8,9},{9,8},{10,11... | collective-permute-start | bytes 98312 | tf_op jit(solution)/shard_map/ppermute | solution.py:401
  1.2 23.0 %collective-permute-start.1 = (f32[2,8,512]{2,1,0:T(8,128)}, f32[2,8,512]{2,1,0:T(8,128)}, u32[]{:S(2)}, u32[]{:S(2)}) collective-permute-start(f32[2,8,512]{2,1,0:T(8,128)} %cot.1), channel_id=1, source_target_pairs={{0,15},{1,2},{2,1},{3,4},{4,3},{5,6},{6,5},{7,8},{8,7},{9,10},{10,... | collective-permute-start | bytes 98312 | tf_op jit(solution)/shard_map/ppermute | solution.py:401
  6.8 1.7 %copy-start = (bf16[2,3,8,48,512]{4,3,2,1,0:T(8,128)(2,1)S(1)}, bf16[2,3,8,48,512]{4,3,2,1,0:T(8,128)(2,1)}, u32[]{:S(2)}) copy-start(bf16[2,3,8,48,512]{4,3,2,1,0:T(8,128)(2,1)} %pre.5) | copy-start | bytes 7077892
  8.5 7.1 %copy-start.11 = (bf16[9,48,48]{2,1,0:T(8,128)(2,1)S(1)}, bf16[9,48,48]{2,1,0:T(8,128)(2,1)}, u32[]{:S(2)}) copy-start(bf16[9,48,48]{2,1,0:T(8,128)(2,1)} %param.12) | copy-start | bytes 124420
  8.5 8.8 %copy-start.12 = (bf16[9,48,48]{2,1,0:T(8,128)(2,1)S(1)}, bf16[9,48,48]{2,1,0:T(8,128)(2,1)}, u32[]{:S(2)}) copy-start(bf16[9,48,48]{2,1,0:T(8,128)(2,1)} %param.11) | copy-start | bytes 124420
  8.5 10.6 %copy-start.13 = (bf16[9,2,48]{2,1,0:T(2,128)(2,1)S(1)}, bf16[9,2,48]{2,1,0:T(2,128)(2,1)}, u32[]{:S(2)}) copy-start(bf16[9,2,48]{2,1,0:T(2,128)(2,1)} %param.13) | copy-start | bytes 5188
  8.5 10.8 %copy-start.14 = (bf16[9,48,2]{1,2,0:T(2,128)(2,1)S(1)}, bf16[9,48,2]{1,2,0:T(2,128)(2,1)}, u32[]{:S(2)}) copy-start(bf16[9,48,2]{1,2,0:T(2,128)(2,1)} %param.10) | copy-start | bytes 5188
  8.5 12.3 %copy-start.1 = (bf16[2,3,8,48,512]{4,3,2,1,0:T(8,128)(2,1)S(1)}, bf16[2,3,8,48,512]{4,3,2,1,0:T(8,128)(2,1)}, u32[]{:S(2)}) copy-start(bf16[2,3,8,48,512]{4,3,2,1,0:T(8,128)(2,1)} %pre.5) | copy-start | bytes 7077892
  10.2 15.9 %collective-permute-start.2 = (bf16[6,48,512]{2,1,0:T(8,128)(2,1)}, bf16[6,48,512]{2,1,0:T(8,128)(2,1)S(1)}, u32[]{:S(2)}, u32[]{:S(2)}) collective-permute-start(bf16[6,48,512]{2,1,0:T(8,128)(2,1)} %get-tuple-element.21), channel_id=1, source_target_pairs={{0,1},{1,0},{2,3},{3,2},{4,5},{5,4},{6,7},{7,6},{8,9},{9,8},{10,11... | collective-permute-start | bytes 884744 | tf_op jit(solution)/shard_map/ppermute | solution.py:401
  10.3 15.8 %collective-permute-start.3 = (bf16[6,48,512]{2,1,0:T(8,128)(2,1)}, bf16[6,48,512]{2,1,0:T(8,128)(2,1)S(1)}, u32[]{:S(2)}, u32[]{:S(2)}) collective-permute-start(bf16[6,48,512]{2,1,0:T(8,128)(2,1)} %get-tuple-element.22), channel_id=1, source_target_pairs={{0,15},{1,2},{2,1},{3,4},{4,3},{5,6},{6,5},{7,8},{8,7},{9,10},{10,... | collective-permute-start | bytes 884744 | tf_op jit(solution)/shard_map/ppermute | solution.py:401
  10.9 13.8 %collective-permute-start.7 = (f32[4,8,512]{2,1,0:T(8,128)}, f32[4,8,512]{2,1,0:T(8,128)}, u32[]{:S(2)}, u32[]{:S(2)}) collective-permute-start(f32[4,8,512]{2,1,0:T(8,128)} %bitcast.24), channel_id=1, source_target_pairs={{0,15},{1,2},{2,1},{3,4},{4,3},{5,6},{6,5},{7,8},{8,7},{9,10},{10,... | collective-permute-start | bytes 196616 | tf_op jit(solution)/shard_map/ppermute | solution.py:401
  22.0 0.8 %copy-start.9 = (bf16[9,48,512]{2,1,0:T(8,128)(2,1)}, bf16[9,48,512]{2,1,0:T(8,128)(2,1)S(1)}, u32[]{:S(2)}) copy-start(bf16[9,48,512]{2,1,0:T(8,128)(2,1)S(1)} %get-tuple-element.25) | copy-start | bytes 1327108
  22.8 0.8 %copy-start.10 = (bf16[9,48,512]{2,1,0:T(8,128)(2,1)}, bf16[9,48,512]{2,1,0:T(8,128)(2,1)S(1)}, u32[]{:S(2)}) copy-start(bf16[9,48,512]{2,1,0:T(8,128)(2,1)S(1)} %get-tuple-element.24) | copy-start | bytes 1327108
  23.6 0.6 copy-start.7
  24.2 10.3 %collective-permute-start.6 = (f32[4,8,512]{2,1,0:T(8,128)}, f32[4,8,512]{2,1,0:T(8,128)S(1)}, u32[]{:S(2)}, u32[]{:S(2)}) collective-permute-start(f32[4,8,512]{2,1,0:T(8,128)} %bitcast.25), channel_id=1, source_target_pairs={{0,1},{1,0},{2,3},{3,2},{4,5},{5,4},{6,7},{7,6},{8,9},{9,8},{10,11... | collective-permute-start | bytes 196616 | tf_op jit(solution)/shard_map/ppermute | solution.py:401
  24.2 12.5 %collective-permute-start.8 = (bf16[9,48,512]{2,1,0:T(8,128)(2,1)}, bf16[9,48,512]{2,1,0:T(8,128)(2,1)S(1)}, u32[]{:S(2)}, u32[]{:S(2)}) collective-permute-start(bf16[9,48,512]{2,1,0:T(8,128)(2,1)} %copy-done.10), channel_id=1, source_target_pairs={{0,1},{1,0},{2,3},{3,2},{4,5},{5,4},{6,7},{7,6},{8,9},{9,8},{10,11... | collective-permute-start | bytes 1327112 | tf_op jit(solution)/shard_map/ppermute | solution.py:401
  24.7 12.0 %collective-permute-start.9 = (bf16[9,48,512]{2,1,0:T(8,128)(2,1)}, bf16[9,48,512]{2,1,0:T(8,128)(2,1)S(1)}, u32[]{:S(2)}, u32[]{:S(2)}) collective-permute-start(bf16[9,48,512]{2,1,0:T(8,128)(2,1)} %copy-done.9), channel_id=1, source_target_pairs={{0,15},{1,2},{2,1},{3,4},{4,3},{5,6},{6,5},{7,8},{8,7},{9,10},{10,... | collective-permute-start | bytes 1327112 | tf_op jit(solution)/shard_map/ppermute | solution.py:401
  26.1 0.8 %copy-start.6 = (f32[2,8,512]{2,1,0:T(8,128)S(1)}, f32[2,8,512]{2,1,0:T(8,128)}, u32[]{:S(2)}) copy-start(f32[2,8,512]{2,1,0:T(8,128)} %cot.1) | copy-start | bytes 98308
  26.8 0.8 %copy-start.8 = (f32[2,8,512]{2,1,0:T(8,128)S(1)}, f32[2,8,512]{2,1,0:T(8,128)}, u32[]{:S(2)}) copy-start(f32[2,8,512]{2,1,0:T(8,128)} %copy-done.7) | copy-start | bytes 98308
  30.5 5.7 %collective-permute-start.4 = (f32[2,8,512]{2,1,0:T(8,128)S(1)}, f32[2,8,512]{2,1,0:T(8,128)S(1)}, u32[]{:S(2)}, u32[]{:S(2)}) collective-permute-start(f32[2,8,512]{2,1,0:T(8,128)S(1)} %get-tuple-element.23.gh), channel_id=1, source_target_pairs={{0,1},{1,0},{2,3},{3,2},{4,5},{5,4},{6,7},{7,6},{8,9},{9,8},{10,11... | collective-permute-start | bytes 98312 | tf_op jit(solution)/shard_map/ppermute | solution.py:401
  30.5 6.2 %collective-permute-start.5 = (f32[2,8,512]{2,1,0:T(8,128)S(1)}, f32[2,8,512]{2,1,0:T(8,128)S(1)}, u32[]{:S(2)}, u32[]{:S(2)}) collective-permute-start(f32[2,8,512]{2,1,0:T(8,128)S(1)} %get-tuple-element.23.gh), channel_id=1, source_target_pairs={{0,15},{1,2},{2,1},{3,4},{4,3},{5,6},{6,5},{7,8},{8,7},{9,10},{10,... | collective-permute-start | bytes 98312 | tf_op jit(solution)/shard_map/ppermute | solution.py:401
  34.5 2.3 %copy-start.2 = (f32[2,8,512]{2,1,0:T(8,128)}, f32[2,8,512]{2,1,0:T(8,128)S(1)}, u32[]{:S(2)}) copy-start(f32[2,8,512]{2,1,0:T(8,128)S(1)} %get-tuple-element.49.u0_a) | copy-start | bytes 98308
  41.1 0.6 copy-start.4
  42.6 2.4 %collective-permute-start.10 = (f32[192,128]{1,0:T(8,128)S(1)}, f32[192,128]{1,0:T(8,128)S(1)}, u32[]{:S(2)}, u32[]{:S(2)}) collective-permute-start(f32[192,128]{1,0:T(8,128)S(1)} %constant_dynamic-slice_fusion), channel_id=1, source_target_pairs={{0,1},{1,0},{2,3},{3,2},{4,5},{5,4},{6,7},{7,6},{8,9},{9,8},{10,11... | collective-permute-start | bytes 294920 | tf_op jit(solution)/shard_map/ppermute | solution.py:482
  45.9 5.1 %collective-permute-start.11 = (f32[192,128]{1,0:T(8,128)S(1)}, f32[192,128]{1,0:T(8,128)S(1)}, u32[]{:S(2)}, u32[]{:S(2)}) collective-permute-start(f32[192,128]{1,0:T(8,128)S(1)} %dynamic-slice_add_fusion), channel_id=1, source_target_pairs={{0,2},{1,3},{2,0},{3,1},{4,6},{5,7},{6,4},{7,5},{8,10},{9,11},{10,... | collective-permute-start | bytes 294920 | tf_op jit(solution)/shard_map/ppermute | solution.py:487
  51.0 5.3 %collective-permute-start.12 = (f32[192,128]{1,0:T(8,128)S(1)}, f32[192,128]{1,0:T(8,128)S(1)}, u32[]{:S(2)}, u32[]{:S(2)}) collective-permute-start(f32[192,128]{1,0:T(8,128)S(1)} %add.54), channel_id=1, source_target_pairs={{0,4},{1,5},{2,6},{3,7},{4,0},{5,1},{6,2},{7,3},{8,12},{9,13},{10,... | collective-permute-start | bytes 294920 | tf_op jit(solution)/shard_map/ppermute | solution.py:487
  51.1 10.5 %collective-permute-start.13 = (f32[192,128]{1,0:T(8,128)S(1)}, f32[192,128]{1,0:T(8,128)S(1)}, u32[]{:S(2)}, u32[]{:S(2)}) collective-permute-start(f32[192,128]{1,0:T(8,128)S(1)} %add.54), channel_id=1, source_target_pairs={{0,8},{1,9},{2,10},{3,11},{4,12},{5,13},{6,14},{7,15},{8,0},{9,1},... | collective-permute-start | bytes 294920 | tf_op jit(solution)/shard_map/ppermute | solution.py:487
  53.2 8.3 %collective-permute-start.14 = (f32[192,128]{1,0:T(8,128)S(1)}, f32[192,128]{1,0:T(8,128)S(1)}, u32[]{:S(2)}, u32[]{:S(2)}) collective-permute-start(f32[192,128]{1,0:T(8,128)S(1)} %add.54), channel_id=1, source_target_pairs={{0,12},{1,13},{2,14},{3,15},{4,8},{5,9},{6,10},{7,11},{8,4},{9,5},... | collective-permute-start | bytes 294920 | tf_op jit(solution)/shard_map/ppermute | solution.py:487
  61.6 2.8 %collective-permute-start.15 = (f32[192,128]{1,0:T(8,128)S(1)}, f32[192,128]{1,0:T(8,128)S(1)}, u32[]{:S(2)}, u32[]{:S(2)}) collective-permute-start(f32[192,128]{1,0:T(8,128)S(1)} %add_add_fusion.mine), channel_id=1, source_target_pairs={{0,1},{1,0},{2,3},{3,2},{4,5},{5,4},{6,7},{7,6},{8,9},{9,8},{10,11... | collective-permute-start | bytes 294920 | tf_op jit(solution)/shard_map/ppermute | solution.py:495
  61.7 0.8 %copy-start.3 = (f32[2,8,512]{2,1,0:T(8,128)S(1)}, f32[2,8,512]{2,1,0:T(8,128)}, u32[]{:S(2)}) copy-start(f32[2,8,512]{2,1,0:T(8,128)} %copy-done.2) | copy-start | bytes 98308
  62.4 0.9 %copy-start.5 = (f32[2,24,512]{2,1,0:T(8,128)S(1)}, f32[2,24,512]{2,1,0:T(8,128)}, u32[]{:S(2)}) copy-start(f32[2,24,512]{2,1,0:T(8,128)} %copy-done.4) | copy-start | bytes 294916

commit v2 on v1

v2 whole, which is shorter than its diff:
```python
import functools
import math

import jax
import jax.numpy as jnp
from jax import lax
from jax.experimental import pallas as pl
from jax.experimental.pallas import tpu as pltpu
from jax.sharding import PartitionSpec as P


STEP = 0.25
VISC = 0.4
LANES = 128
BLOCK = 3
BLOCK4 = 4
VMEM_BYTES = 67043328
BORDERS = (2, 1, 0)
EMPTY = 2
SMALL = 8

F32 = jnp.float32
BF16 = jnp.bfloat16


def lane_roll(x, shift):
    width = x.shape[-1]
    return pltpu.roll(x, shift % width, x.ndim - 1)


def row_roll(x, shift):
    return pltpu.roll(x, shift % x.shape[0], 0)


def half_step(r, c):
    face = 0.25 * (r + row_roll(r, -1))
    side = 0.25 * (c + lane_roll(c, -1))
    outs = []
    for f in (r, c):
        down, right = row_roll(f, -1), lane_roll(f, -1)
        p = face * (f + down)
        q = side * (f + right)
        div = p - row_roll(p, 1) + (q - lane_roll(q, 1))
        lap = down + row_roll(f, 1) + right + lane_roll(f, 1) - 4.0 * f
        outs.append(f + STEP * (VISC * lap - div))
    return outs


def half_step_transpose(r, c, lr, lc):
    face = 0.25 * (r + row_roll(r, -1))
    side = 0.25 * (c + lane_roll(c, -1))
    outs = []
    extra_r = None
    extra_c = None
    for f, l in ((r, lr), (c, lc)):
        l_down, l_right = row_roll(l, -1), lane_roll(l, -1)
        a = STEP * (l_down - l)
        b = STEP * (l_right - l)
        ap, bq = a * face, b * side
        lap = l_down + row_roll(l, 1) + l_right + lane_roll(l, 1) - 4.0 * l
        outs.append(
            l + (STEP * VISC) * lap + (ap + row_roll(ap, 1)) + (bq + lane_roll(bq, 1))
        )
        af = a * (0.25 * (f + row_roll(f, -1)))
        bf = b * (0.25 * (f + lane_roll(f, -1)))
        extra_r = af if extra_r is None else extra_r + af
        extra_c = bf if extra_c is None else extra_c + bf
    return [
        outs[0] + (extra_r + row_roll(extra_r, 1)),
        outs[1] + (extra_c + lane_roll(extra_c, 1)),
    ]


def joined(a, own, b, even):
    return jnp.concatenate([jnp.where(even, b, a), own, jnp.where(even, a, b)], axis=0)


def split_terms(x):
    high = x.astype(BF16).astype(F32)
    return jnp.concatenate([high, x - high], axis=0).astype(BF16)


def border_planes(ref, first, rows, count):
    parts = [
        ref[first + 2 * rows * i : first + 2 * rows * (i + 1), :].astype(F32)
        for i in range(count)
    ]
    return [p[:rows] + p[rows:] for p in parts]


def fill_small(dst, planes, rows, row0, sign):
    dst[...] = jnp.zeros(dst.shape, F32)
    for comp, plane in enumerate(planes):
        value = plane.astype(BF16).astype(F32)
        for q in range(3):
            moved = value if q == 1 else lane_roll(value, sign * (q - 1))
            for i in range(rows):
                dst[SMALL * i + 2 * q + comp : SMALL * i + 2 * q + comp + 1, :] = moved[
                    row0 + i : row0 + i + 1, :
                ]


def row_conv(w_ref, src, src0, lo, hi, ch, emit):
    row = lo
    while row < hi:
        count = min(BLOCK, hi - row)
        rhs = src[(row - 1 - src0) * ch : (row + count + 1 - src0) * ch, :]
        lhs = w_ref[: count * 3 * ch, : (count + 2) * ch]
        y = jnp.dot(lhs, rhs, preferred_element_type=F32)
        for k in range(count):
            base = 3 * ch * k
            e = (
                y[base + ch : base + 2 * ch]
                + lane_roll(y[base : base + ch], -1)
                + lane_roll(y[base + 2 * ch : base + 3 * ch], 1)
            )
            emit(row + k, e)
        row += count


def chain(x4, pre, m_a, m_b, even, w4, w3, w2, d3, d2, d1, rows, ch):
    e3, e2, e1 = BORDERS

    def mask_rows(layer, row):
        if rows <= row < 2 * rows:
            return pre[layer, row - rows].astype(F32)
        above = row < rows
        border, start = ((e1, e3 + e2), (e2, e3), (e3, 0))[layer]
        k = start + (row - (rows - border) if above else row - 2 * rows)
        a, b = (m[k * ch : (k + 1) * ch, :].astype(F32) for m in (m_a, m_b))
        return jnp.where(even, b, a) if above else jnp.where(even, a, b)

    def store(dst, layer, first):
        def emit(row, e):
            dst[(row - first) * ch : (row - first + 1) * ch, :] = jnp.where(
                mask_rows(layer, row) > 0, e, 0.0
            ).astype(BF16)

        return emit

    row, emit = rows - e3, store(d3, 2, rows - e3)
    while row < 2 * rows + e3:
        count = min(BLOCK4, 2 * rows + e3 - row)
        rhs = x4[SMALL * (row - 1) : SMALL * (row + count + 1), :].astype(BF16)
        y = jnp.dot(
            w4[: count * ch, : SMALL * (count + 2)], rhs, preferred_element_type=F32
        )
        for k in range(count):
            emit(row + k, y[k * ch : (k + 1) * ch])
        row += count
    row_conv(w3, d3, rows - e3, rows - e2, 2 * rows + e2, ch, store(d2, 1, rows - e2))
    empty = jnp.zeros((EMPTY * ch, d1.shape[-1]), BF16)
    d1[: EMPTY * ch, :] = empty
    d1[(rows + EMPTY) * ch :, :] = empty
    row_conv(w2, d2, rows - e2, rows, 2 * rows, ch, store(d1, 0, rows - EMPTY))


def first_conv(w1, d1, src0, lo, hi, ch, emit):
    row = lo
    while row < hi:
        start = min(row, hi - BLOCK)
        rhs = d1[(start - 1 - src0) * ch : (start + BLOCK + 1 - src0) * ch, :]
        y = jnp.dot(w1[...], rhs, preferred_element_type=F32)
        e = (
            y[SMALL : 2 * SMALL]
            + lane_roll(y[:SMALL], -1)
            + lane_roll(y[2 * SMALL : 3 * SMALL], 1)
        )
        for k in range(row - start, BLOCK):
            emit(start + k, [e[2 * k + comp : 2 * k + comp + 1, :] for comp in range(2)])
        row = start + BLOCK


def weight_terms(x4, d3, d2, d1, pre, x0s, rows, ch):
    dims = (((1,), (1,)), ((), ()))

    def product(a, b):
        return lax.dot_general(a, b, dims, preferred_element_type=F32)

    def three(ref, row, border):
        row -= rows - border
        return ref[(row - 1) * ch : (row + 2) * ch, :]

    totals = [None] * 4
    for i in range(rows):
        row = rows + i
        source = [jnp.maximum(pre[layer, i].astype(F32), 0.0) for layer in range(3)]
        moved = [
            jnp.concatenate([lane_roll(s, 1), s, lane_roll(s, -1)], axis=0).astype(BF16)
            for s in source[:2]
        ]
        terms = (
            product(
                x0s[SMALL * i : SMALL * (i + 3), :].astype(BF16),
                d1[(i + EMPTY) * ch : (i + EMPTY + 1) * ch, :],
            ),
            product(three(d2, row, BORDERS[1]), moved[0]),
            product(three(d3, row, BORDERS[0]), moved[1]),
            product(
                x4[SMALL * (row - 1) : SMALL * (row + 2), :].astype(BF16),
                source[2].astype(BF16),
            ),
        )
        totals = [t if old is None else old + t for old, t in zip(totals, terms)]
    return totals


def pack_rows(ch):
    n = 3 * ch
    return -(-(2 * n + n // 2 + 3 * SMALL) // 32) * 32


def pack_terms(t_ref, terms, ch, before=None):
    g1, g2, g3, g4 = terms
    n = 3 * ch
    low = 2 * n + n // 2
    tail = jnp.concatenate([g2[:, LANES:], g3[:, LANES:]], axis=1)
    wide = tail.shape[1]
    parts = (
        (0, n, 0, LANES, g2[:, :LANES]),
        (n, 2 * n, 0, LANES, g3[:, :LANES]),
        (2 * n, low, 0, wide, tail[: n // 2]),
        (2 * n, low, wide, 2 * wide, tail[n // 2 :]),
        (low, low + 3 * SMALL, 0, 2 * ch, jnp.concatenate([g4, g1], axis=1)),
    )
    t_ref[2 * n :, :] = jnp.zeros((t_ref.shape[0] - 2 * n, LANES), F32)
    for r0, r1, c0, c1, value in parts:
        if before is not None:
            value = value + before[r0:r1, c0:c1]
        t_ref[r0:r1, c0:c1] = value


def border_copies(axis, takes, rows, ch, pre_hbm, out_a, out_b, sems):
    even = lax.rem(lax.axis_index(axis), 2) == 0
    copies = []
    for step, layer, count, dst in takes:
        low, high = 0, (rows - count) * ch
        for out, start in (
            (out_a, jnp.where(even, high, low)),
            (out_b, jnp.where(even, low, high)),
        ):
            copy = pltpu.make_async_copy(
                pre_hbm.at[step, layer, pl.ds(pl.multiple_of(start, ch), count * ch)],
                out.at[pl.ds(dst * ch, count * ch)],
                sems.at[len(copies)],
            )
            copy.start()
            copies.append(copy)
    return copies


def gather_kernel(axis, takes, rows, ch, base, step, with_d4, pre_hbm, states, cot, out_a, out_b, sems):
    copies = border_copies(axis, takes, rows, ch, pre_hbm, out_a, out_b, sems)
    planes = [split_terms(states[step, comp]) for comp in range(2)]
    if with_d4:
        planes.append(jnp.concatenate([cot[0], cot[1]], axis=0).astype(BF16))
    for i, plane in enumerate(planes):
        for out in (out_a, out_b):
            out[base + 2 * rows * i : base + 2 * rows * (i + 1), :] = plane
    for copy in copies:
        copy.wait()


def weights_kernel(ch, w1, w2, w3, w4, o1, o2, o3, o4):
    for w, o in ((w3, o3), (w2, o2)):
        for q in range(3):
            block = jnp.concatenate([w[3 * (2 - m) + q].astype(F32) for m in range(3)], axis=0)
            block = block.T.astype(BF16)
            for b in range(BLOCK):
                r = (3 * b + q) * ch
                o[r : r + ch, :] = placed(block, b * ch, o.shape[1])
    zero = jnp.zeros((SMALL - 6, ch), F32)
    block = jnp.concatenate(
        [
            piece
            for m in range(3)
            for piece in [w4[3 * (2 - m) + q].astype(F32) for q in range(3)] + [zero]
        ],
        axis=0,
    )
    block = block.T.astype(BF16)
    for b in range(BLOCK4):
        o4[b * ch : (b + 1) * ch, :] = placed(block, b * SMALL, o4.shape[1])
    rows = []
    for q in range(3):
        block = jnp.concatenate([w1[3 * (2 - m) + q].astype(F32) for m in range(3)], axis=1)
        for b in range(BLOCK):
            rows.append(placed(block, b * ch, o1.shape[1]))
        rows.append(jnp.zeros((SMALL - 2 * BLOCK, o1.shape[1]), F32))
    o1[...] = jnp.concatenate(rows, axis=0).astype(BF16)


def placed(block, column, width):
    parts = [block]
    if column:
        parts.insert(0, jnp.zeros((block.shape[0], column), block.dtype))
    rest = width - column - block.shape[1]
    if rest:
        parts.append(jnp.zeros((block.shape[0], rest), block.dtype))
    return jnp.concatenate(parts, axis=1)


def partial_input(w1, d1, own, out, rows, ch):
    out[2 * rows :, :] = jnp.zeros((SMALL, out.shape[1]), F32)

    def emit(row, values):
        i = row - rows
        for comp in range(2):
            if 0 <= i < rows:
                k = rows * comp + i
                out[k : k + 1, :] = own(comp, i) + values[comp]
            else:
                k = 2 * rows + 2 * comp + (i > 0)
                out[k : k + 1, :] = values[comp]

    first_conv(w1, d1, rows - EMPTY, rows - 1, 2 * rows + 1, ch, emit)


def whole_input(gh, gh_a, gh_b, lam, rows, even):
    a, b = gh_a[...], gh_b[...]
    above, below = jnp.where(even, b, a), jnp.where(even, a, b)
    for comp in range(2):
        own = slice(rows * comp, rows * (comp + 1))
        lam[comp, :rows, :] = above[own]
        lam[comp, rows : 2 * rows, :] = gh[own, :]
        lam[comp, 2 * rows :, :] = below[own]
        k = 2 * rows + 2 * comp
        for row, part in (
            (rows - 1, gh[k : k + 1, :]),
            (rows, above[k + 1 : k + 2]),
            (2 * rows - 1, below[k : k + 1]),
            (2 * rows, gh[k + 1 : k + 2, :]),
        ):
            lam[comp, row : row + 1, :] += part


def border_states(states, step, m_a, m_b, rows, ch, even):
    a = border_planes(m_a, sum(BORDERS) * ch, rows, 2)
    b = border_planes(m_b, sum(BORDERS) * ch, rows, 2)
    return [joined(a[comp], states[step, comp], b[comp], even) for comp in range(2)]


def back_kernel(axis, rows, ch, cot, pre, m_a, m_b, w4, w3, w2, w1, gh, x4, d3, d2, d1):
    even = lax.rem(lax.axis_index(axis), 2) == 0
    base = sum(BORDERS) * ch + 4 * rows
    a, b = (m[base : base + 2 * rows, :].astype(F32) for m in (m_a, m_b))
    planes = [
        joined(
            a[rows * comp : rows * (comp + 1)], cot[comp], b[rows * comp : rows * (comp + 1)], even
        )
        for comp in range(2)
    ]
    fill_small(x4, planes, 3 * rows, 0, 1)
    chain(x4, pre.at[0], m_a, m_b, even, w4, w3, w2, d3, d2, d1, rows, ch)
    partial_input(w1, d1, lambda comp, i: cot[comp, i : i + 1, :], gh, rows, ch)


def term_kernel(axis, rows, ch, x4, d3, d2, d1, pre, states, m_a, m_b, t_out, u_out, x0s):
    even = lax.rem(lax.axis_index(axis), 2) == 0
    u = border_states(states, 1, m_a, m_b, rows, ch, even)
    for comp in range(2):
        u_out[comp] = u[comp]
    fill_small(x0s, half_step(*u), rows + 2, rows - 1, -1)
    pack_terms(t_out, weight_terms(x4, d3, d2, d1, pre.at[0], x0s, rows, ch), ch)


def front_kernel(
    axis, rows, ch,
    gh, gh_a, gh_b, u1, states, pre, m_a, m_b, w4, w3, w2, before,
    keep, give, g_out, u_out, d1, x4, d3, d2, x0s, total, lam,
):
    even = lax.rem(lax.axis_index(axis), 2) == 0
    whole_input(gh, gh_a, gh_b, lam, rows, even)
    planes = half_step_transpose(u1[0], u1[1], lam[0], lam[1])
    for comp in range(2):
        g_out[comp] = planes[comp][rows : 2 * rows]
    fill_small(x4, planes, 3 * rows, 0, 1)
    u = border_states(states, 0, m_a, m_b, rows, ch, even)
    for comp in range(2):
        u_out[comp] = u[comp]
    fill_small(x0s, half_step(*u), rows + 2, rows - 1, -1)
    chain(x4, pre.at[0], m_a, m_b, even, w4, w3, w2, d3, d2, d1, rows, ch)
    pack_terms(total, weight_terms(x4, d3, d2, d1, pre.at[0], x0s, rows, ch), ch, before)
    half = total.shape[0] // 2
    a, b = total[:half, :], total[half:, :]
    keep[...] = jnp.where(even, a, b)
    give[...] = jnp.where(even, b, a)


def input_kernel(rows, ch, g, d1, w1, gh):
    partial_input(w1, d1, lambda comp, i: g[comp, i : i + 1, :], gh, rows, ch)


def last_kernel(axis, rows, gh, gh_a, gh_b, u, out, lam):
    even = lax.rem(lax.axis_index(axis), 2) == 0
    whole_input(gh, gh_a, gh_b, lam, rows, even)
    planes = half_step_transpose(u[0], u[1], lam[0], lam[1])
    for comp in range(2):
        out[comp] = planes[comp][rows : 2 * rows]


def unpack_kernel(axis, ch, factor, mine, other, o1, o2, o3, o4):
    even = lax.rem(lax.axis_index(axis), 2) == 0
    a, b = mine[...].astype(F32), other[...].astype(F32)
    t = factor * jnp.concatenate([jnp.where(even, a, b), jnp.where(even, b, a)], axis=0)
    n = 3 * ch
    rest = n - LANES
    wide = 2 * rest
    low = 2 * n + n // 2
    tail = t[2 * n : low]
    tail = jnp.concatenate([tail[:, :wide], tail[:, wide : 2 * wide]], axis=0)
    g2 = jnp.concatenate([t[:n], tail[:, :rest]], axis=1)
    g3 = jnp.concatenate([t[n : 2 * n], tail[:, rest:]], axis=1)
    g4 = t[low : low + 3 * SMALL, :ch]
    g1 = t[low : low + 3 * SMALL, ch : 2 * ch]
    for m in range(3):
        for q in range(3):
            tap = 3 * (2 - m) + q
            o2[tap] = g2[m * ch : (m + 1) * ch, q * ch : (q + 1) * ch]
            o3[tap] = g3[m * ch : (m + 1) * ch, q * ch : (q + 1) * ch]
            small = slice(m * SMALL + 2 * q, m * SMALL + 2 * q + 2)
            o4[tap] = g4[small]
            o1[3 * m + q] = g1[small]


VMEM = pl.BlockSpec(memory_space=pltpu.VMEM)


def call(kernel, outs, scratch, args, specs=None, limit=24 << 20, flops=10**8):
    specs = specs or {}
    return pl.pallas_call(
        kernel,
        out_shape=outs,
        grid=(1,) if specs else (),
        in_specs=[specs.get(i, VMEM) for i in range(len(args))],
        out_specs=jax.tree.map(lambda _: VMEM, outs),
        scratch_shapes=scratch,
        compiler_params=pltpu.CompilerParams(vmem_limit_bytes=limit),
        cost_estimate=pl.CostEstimate(
            flops=flops, bytes_accessed=2 * 10**6, transcendentals=0
        ),
    )(*args)


def on_device(states, pre_acts, cotangent, weight_in, weight_second, weight_third, weight_out):
    axis = "gx"
    count = lax.axis_size(axis)
    _, _, rows, width = states.shape
    ch = pre_acts.shape[3]
    flat = pre_acts.reshape(pre_acts.shape[:2] + (rows * ch, width))

    pair_a = [(i, i ^ 1) for i in range(count)]
    pair_b = [(i, (i + 1) % count if i % 2 else (i - 1) % count) for i in range(count)]

    def swap(for_a, for_b):
        b = lax.ppermute(for_b, axis, pair_b)
        a = lax.ppermute(for_a, axis, pair_a)
        return a, b

    def shape(*dims, dtype=F32):
        return jax.ShapeDtypeStruct(dims, dtype)

    def borders(step, with_d4, room):
        takes, total = [], 0
        for layer, border in zip((2, 1, 0), BORDERS):
            if not border:
                continue
            takes.append((step, layer, border, total))
            total += border
        base = total * ch
        out = shape(base + (6 if with_d4 else 4) * rows, width, dtype=BF16)
        pack = pl.pallas_call(
            functools.partial(gather_kernel, axis, takes, rows, ch, base, step, with_d4),
            out_shape=[out, out],
            in_specs=[pl.BlockSpec(memory_space=pltpu.HBM), VMEM, VMEM],
            out_specs=[VMEM, VMEM],
            scratch_shapes=[pltpu.SemaphoreType.DMA((2 * len(takes),))],
            compiler_params=pltpu.CompilerParams(vmem_limit_bytes=VMEM_BYTES - room),
        )
        a, b = pack(flat, states, cotangent)
        return swap(a, b)

    m1_a, m1_b = borders(1, True, 3 << 20)
    m0_a, m0_b = borders(0, False, 56 << 20)

    def bands(n, m):
        return shape(n, m, dtype=BF16)

    w1, w2, w3, w4 = call(
        functools.partial(weights_kernel, ch),
        [
            bands(3 * SMALL, (BLOCK + 2) * ch),
            bands(3 * BLOCK * ch, (BLOCK + 2) * ch),
            bands(3 * BLOCK * ch, (BLOCK + 2) * ch),
            bands(BLOCK4 * ch, (BLOCK4 + 2) * SMALL),
        ],
        [],
        (jnp.swapaxes(weight_in, 1, 2), weight_second, weight_third, weight_out),
    )

    def pre_spec(step):
        return pl.BlockSpec((1,) + pre_acts.shape[1:], lambda *_: (step, 0, 0, 0, 0))

    def d_shape(border):
        return shape((rows + 2 * border) * ch, width, dtype=BF16)

    def scratch(*shapes):
        return [pltpu.VMEM(s.shape, s.dtype) for s in shapes]

    x4_shape = shape(3 * rows * SMALL, width)
    x0_shape = shape((rows + 2) * SMALL, width)
    d_shapes = [d_shape(BORDERS[0]), d_shape(BORDERS[1]), d_shape(EMPTY)]
    planes = shape(2, 3 * rows, width)
    part = shape(2 * rows + SMALL, width)
    total = shape(pack_rows(ch), LANES)
    half = shape(pack_rows(ch) // 2, LANES)
    gh, x4, d3, d2, d1 = call(
        functools.partial(back_kernel, axis, rows, ch),
        [part, x4_shape] + d_shapes,
        [],
        (cotangent, pre_acts, m1_a, m1_b, w4, w3, w2, w1),
        {1: pre_spec(1)},
    )
    gh_a, gh_b = swap(gh, gh)
    before, u1 = call(
        functools.partial(term_kernel, axis, rows, ch),
        [total, planes],
        scratch(x0_shape),
        (x4, d3, d2, d1, pre_acts, states, m1_a, m1_b),
        {4: pre_spec(1)},
    )
    keep, give, g, u0, d1 = call(
        functools.partial(front_kernel, axis, rows, ch),
        [half, half, shape(2, rows, width), planes, d_shapes[2]],
        scratch(x4_shape, d_shapes[0], d_shapes[1], x0_shape, total, planes),
        (gh, gh_a, gh_b, u1, states, pre_acts, m0_a, m0_b, w4, w3, w2, before),
        {5: pre_spec(0)},
    )
    gh0 = call(functools.partial(input_kernel, rows, ch), part, [], (g, d1, w1))
    gh0_a, gh0_b = swap(gh0, gh0)
    adjoint = call(
        functools.partial(last_kernel, axis, rows),
        shape(2, rows, width),
        scratch(planes),
        (gh0, gh0_a, gh0_b, u0),
    )

    mine = keep + lax.ppermute(give, axis, pair_a)
    bit = 2
    while bit < count:
        mine = mine.astype(BF16)
        got = lax.ppermute(mine, axis, [(i, i ^ bit) for i in range(count)])
        if 2 * bit >= count:
            got, adjoint = lax.optimization_barrier((got, adjoint))
        mine = mine.astype(F32) + got.astype(F32)
        bit *= 2
    other = lax.ppermute(mine, axis, pair_a)
    factor = 1.0 / math.sqrt(rows * count * width)
    g1, g2, g3, g4 = call(
        functools.partial(unpack_kernel, axis, ch, factor),
        [
            shape(*w)
            for w in (
                weight_out.shape[:1] + (weight_in.shape[2], ch),
                weight_second.shape,
                weight_third.shape,
                weight_out.shape,
            )
        ],
        [],
        (mine, other),
    )
    return adjoint, jnp.swapaxes(g1, 1, 2), g2, g3, g4


def solution(mesh):
    return jax.shard_map(
        on_device,
        mesh=mesh,
        in_specs=(
            P(None, "groups", "gx", None),
            P(None, None, ("groups", "gx"), None, None),
            P("groups", "gx", None),
            P(),
            P(),
            P(),
            P(),
        ),
        out_specs=(
            P("groups", "gx", None),
            P("groups", None, None),
            P("groups", None, None),
            P("groups", None, None),
            P("groups", None, None),
        ),
        check_vma=False,
    )
```

time: 66.9 us -> 43.3 us (0.65)
  local copies, waits for them, and re-layouts: 14.6 us -> 0.03 us
  starting transfers between devices: 21.9 us -> 18.2 us
  other arithmetic: 2.33 us -> 0.06 us
  Pallas kernels: 13.9 us -> 12.6 us
  waiting for transfers between devices: 12.6 us -> 11.4 us
    unnamed x31 -> x14, local copies, waits for them, and re-layouts: 8.36 us -> 0.03 us
    ppermute x14 -> x11, waiting for transfers between devices: 11.7 us -> 8.87 us  [the longest x3 5.01 us: on_device(): got = lax.ppermute(mine, axis, [(i, i ^ bit) for i in range(count)])]
    ppermute x14 -> x11, starting transfers between devices: 20.4 us -> 18.1 us  [the longest x4 13.8 us: swap(): b = lax.ppermute(for_b, axis, pair_b)]
    reshape x10 -> x0, local copies, waits for them, and re-layouts: 2.03 us -> none  [the longest x2 1.52 us: band(): w = jnp.transpose(w, (1, 3, 0, 2)).reshape(3 * k, 3 * o)]
    rev x3 -> x0, local copies, waits for them, and re-layouts: 1.7 us -> none  [the longest x2 1.66 us: band(): w = weight.reshape(3, 3, o, k)[::-1]]
    pallas_call x5 -> x7, Pallas kernels: 11 us -> 9.44 us  [call(): pl.pallas_call(kernel, out_shape=outs, grid=(1,) if specs else (), in_spe...]
    concatenate x3 -> x0, other arithmetic: 1.39 us -> none  [the longest x1 1.22 us: band(): jnp.concatenate([jnp.pad(w, ((0, 0), (b * o, (count - 1 - b) * o))) for b...]
    ppermute x1, starting transfers between devices: 1.43 us -> 0.07 us  [on_device(): mine = keep + lax.ppermute(give, axis, pair_a)]
  transfers between devices with their start and end apart: 16 -> 13, of which waited for: 5 -> 7; matrix products, arithmetic and copies ran while one was open for 10% -> 0% of each run, Pallas kernels for 13% -> 13%
where the time goes in v2:
time: 43.3 us; the launch traced here: 43.2 us
  starting transfers between devices  18.2 us (42%)
  Pallas kernels  12.6 us (29%)
  waiting for transfers between devices  11.4 us (26%)
  between operations  0.81 us (2%)
    ppermute x4, starting transfers between devices, swap(): b = lax.ppermute(for_b, axis, pair_b)  13.8 us
    pallas_call x7, Pallas kernels, call(): pl.pallas_call(kernel, out_shape=outs, grid=(1,) if specs else (), in_spe...  9.44 us
    ppermute x3, waiting for transfers between devices, on_device(): got = lax.ppermute(mine, axis, [(i, i ^ bit) for i in range(count)])  5.01 us
    ppermute x4, waiting for transfers between devices, swap(): b = lax.ppermute(for_b, axis, pair_b)  3.85 us
    pallas_call x2, Pallas kernels, borders(): a, b = pack(flat, states, cotangent)  3.16 us
    ppermute x3, starting transfers between devices, on_device(): got = lax.ppermute(mine, axis, [(i, i ^ bit) for i in range(count)])  3.07 us
    ppermute x1, waiting for transfers between devices, on_device(): other = lax.ppermute(mine, axis, pair_a)  1.29 us
    ppermute x1, waiting for transfers between devices, on_device(): mine = keep + lax.ppermute(give, axis, pair_a)  1.29 us
  transfers between devices with their start and end apart: 13, of which 7 were waited for; matrix products, arithmetic and copies ran while one was open for 0% of the time, Pallas kernels for 13%

profile of v2, /device:TPU:0, one launch (start us, length us, event | category | flops | bytes accessed | tf_op | source)
XLA Modules:
  0.0 43.2 jit_solution(3300009943556855820)
XLA Ops:
  0.6 0.0 copy-start
  0.6 0.0 copy-start.1
  0.7 0.0 copy-start.2
  0.7 0.0 copy-start.3
  0.7 0.0 copy-start.4
  0.7 0.0 copy-start.5
  0.7 0.0 copy-start.6
  0.7 2.7 %shard_map.110 = (bf16[192,512]{1,0:T(8,128)(2,1)}, bf16[192,512]{1,0:T(8,128)(2,1)}) custom-call(bf16[2,3,384,512]{3,2,1,0:T(8,128)(2,1)} %bitcast.3, f32[2,2,8,512]{3,2,1,0:T(8,128)} %states.7, f32[2,8,512]{2,1,0:T(8,128)} %cot.5), custom_call_target="tpu_custom_call" | custom-call | tf_op jit(solution)/shard_map/pallas_call | solution.py:480
  3.4 0.6 %collective-permute-start = (bf16[192,512]{1,0:T(8,128)(2,1)}, bf16[192,512]{1,0:T(8,128)(2,1)S(1)}, u32[]{:S(2)}, u32[]{:S(2)}) collective-permute-start(bf16[192,512]{1,0:T(8,128)(2,1)} %get-tuple-element.31), channel_id=1, source_target_pairs={{0,1},{1,0},{2,3},{3,2},{4,5},{5,4},{6,7},{7,6},{8,9},{9,8},{10,11... | collective-permute-start | bytes 589832 | tf_op jit(solution)/shard_map/ppermute | solution.py:457
  4.0 5.6 %collective-permute-start.1 = (bf16[192,512]{1,0:T(8,128)(2,1)}, bf16[192,512]{1,0:T(8,128)(2,1)S(1)}, u32[]{:S(2)}, u32[]{:S(2)}) collective-permute-start(bf16[192,512]{1,0:T(8,128)(2,1)} %get-tuple-element.32), channel_id=1, source_target_pairs={{0,15},{1,2},{2,1},{3,4},{4,3},{5,6},{6,5},{7,8},{8,7},{9,10},{10,... | collective-permute-start | bytes 589832 | tf_op jit(solution)/shard_map/ppermute | solution.py:456
  9.6 0.0 copy-done
  9.6 0.0 copy-done.1
  9.6 0.0 copy-done.2
  9.6 0.4 %shard_map.114 = (bf16[176,512]{1,0:T(8,128)(2,1)S(1)}, bf16[176,512]{1,0:T(8,128)(2,1)S(1)}) custom-call(bf16[2,3,384,512]{3,2,1,0:T(8,128)(2,1)S(1)} %bitcast.4, f32[2,2,8,512]{3,2,1,0:T(8,128)S(1)} %copy-done.1, f32[2,8,512]{2,1,0:T(8,128)S(1)} %copy-done.2), custom_call_target="tpu_custom_call" | custom-call | tf_op jit(solution)/shard_map/pallas_call | solution.py:480
  10.1 0.1 collective-permute-start.4
  10.2 0.6 %collective-permute-start.5 = (bf16[176,512]{1,0:T(8,128)(2,1)S(1)}, bf16[176,512]{1,0:T(8,128)(2,1)S(1)}, u32[]{:S(2)}, u32[]{:S(2)}) collective-permute-start(bf16[176,512]{1,0:T(8,128)(2,1)S(1)} %get-tuple-element.44), channel_id=1, source_target_pairs={{0,15},{1,2},{2,1},{3,4},{4,3},{5,6},{6,5},{7,8},{8,7},{9,10},{10,... | collective-permute-start | bytes 540680 | tf_op jit(solution)/shard_map/ppermute | solution.py:456
  10.8 0.0 copy-done.3
  10.8 0.0 copy-done.4
  10.8 0.0 copy-done.5
  10.8 0.0 copy-done.6
  10.8 0.4 shard_map.111
  11.2 0.0 collective-permute-done.m_a
  11.2 2.0 %collective-permute-done.1.m_b = bf16[192,512]{1,0:T(8,128)(2,1)S(1)} collective-permute-done((bf16[192,512]{1,0:T(8,128)(2,1)}, bf16[192,512]{1,0:T(8,128)(2,1)S(1)}, u32[]{:S(2)}, u32[]{:S(2)}) %collective-permute-start.1) | collective-permute-done | bytes 196640 | tf_op jit(solution)/shard_map/ppermute | solution.py:456
  13.2 1.9 %shard_map.112 = (f32[24,512]{1,0:T(8,128)S(1)}, f32[192,512]{1,0:T(8,128)S(1)}, bf16[576,512]{1,0:T(8,128)(2,1)S(1)}, bf16[480,512]{1,0:T(8,128)(2,1)S(1)}, bf16[576,512]{1,0:T(8,128)(2,1)S(1)}) custom-call(f32[2,8,512]{2,1,0:T(8,128)S(1)} %copy-done.2, bf16[2,3,8,48,512]{4,3,2,1,0:T(8,128)(2,1)S(1)} %copy-done, ...), custom_call_target="tpu_custom_call" | custom-call | flops 100000000 | bytes 2000000 | tf_op jit(solution)/shard_map/pallas_call | solution.py:431
  15.1 0.5 %collective-permute-start.2 = (f32[24,512]{1,0:T(8,128)S(1)}, f32[24,512]{1,0:T(8,128)S(1)}, u32[]{:S(2)}, u32[]{:S(2)}) collective-permute-start(f32[24,512]{1,0:T(8,128)S(1)} %get-tuple-element.37.gh), channel_id=1, source_target_pairs={{0,1},{1,0},{2,3},{3,2},{4,5},{5,4},{6,7},{7,6},{8,9},{9,8},{10,11... | collective-permute-start | bytes 147464 | tf_op jit(solution)/shard_map/ppermute | solution.py:457
  15.6 4.2 %collective-permute-start.3 = (f32[24,512]{1,0:T(8,128)S(1)}, f32[24,512]{1,0:T(8,128)S(1)}, u32[]{:S(2)}, u32[]{:S(2)}) collective-permute-start(f32[24,512]{1,0:T(8,128)S(1)} %get-tuple-element.37.gh), channel_id=1, source_target_pairs={{0,15},{1,2},{2,1},{3,4},{4,3},{5,6},{6,5},{7,8},{8,7},{9,10},{10,... | collective-permute-start | bytes 147464 | tf_op jit(solution)/shard_map/ppermute | solution.py:456
  19.8 1.8 %shard_map.113 = (f32[384,128]{1,0:T(8,128)S(1)}, f32[2,24,512]{2,1,0:T(8,128)S(1)}) custom-call(f32[192,512]{1,0:T(8,128)S(1)} %get-tuple-element.38.x4, bf16[576,512]{1,0:T(8,128)(2,1)S(1)} %get-tuple-element.39.d3, bf16[480,512]{1,0:T(8,128)(2,1)S(1)} %get-tuple-element.40.d2, bf16[576,512]{1,0:T(8,128)(2,1)S(1)} %get-tuple-element.41.d1, ...), custom_call_target="tpu_custom_call" | custom-call | flops 100000000 | bytes 2000000 | tf_op jit(solution)/shard_map/pallas_call | solution.py:431
  21.6 0.0 collective-permute-done.4.m_a
  21.6 0.0 collective-permute-done.5.m_b
  21.6 0.0 collective-permute-done.2.gh_a
  21.6 0.2 collective-permute-done.3.gh_b
  21.8 3.3 %shard_map.115 = (f32[192,128]{1,0:T(8,128)S(1)}, f32[192,128]{1,0:T(8,128)S(1)}, f32[2,8,512]{2,1,0:T(8,128)S(1)}, f32[2,24,512]{2,1,0:T(8,128)S(1)}, bf16[576,512]{1,0:T(8,128)(2,1)S(1)}) custom-call(f32[24,512]{1,0:T(8,128)S(1)} %get-tuple-element.37.gh, f32[24,512]{1,0:T(8,128)S(1)} %collective-permute-done.2.gh_a, ...), custom_call_target="tpu_custom_call" | custom-call | flops 100000000 | bytes 2000000 | tf_op jit(solution)/shard_map/pallas_call | solution.py:431
  25.1 0.1 collective-permute-start.6
  25.2 1.3 %collective-permute-done.6 = f32[192,128]{1,0:T(8,128)S(1)} collective-permute-done((f32[192,128]{1,0:T(8,128)S(1)}, f32[192,128]{1,0:T(8,128)S(1)}, u32[]{:S(2)}, u32[]{:S(2)}) %collective-permute-start.6) | collective-permute-done | bytes 98336 | tf_op jit(solution)/shard_map/ppermute | solution.py:548
  26.5 0.7 %collective-permute-start.7 = (bf16[192,128]{1,0:T(8,128)(2,1)S(1)}, bf16[192,128]{1,0:T(8,128)(2,1)S(1)}, u32[]{:S(2)}, u32[]{:S(2)}) collective-permute-start(bf16[192,128]{1,0:T(8,128)(2,1)S(1)} %add_convert_fusion.2), channel_id=1, source_target_pairs={{0,2},{1,3},{2,0},{3,1},{4,6},{5,7},{6,4},{7,5},{8,10},{9,11},{10,... | collective-permute-start | bytes 147464 | tf_op jit(solution)/shard_map/ppermute | solution.py:552
  27.1 3.5 %collective-permute-done.7 = bf16[192,128]{1,0:T(8,128)(2,1)S(1)} collective-permute-done((bf16[192,128]{1,0:T(8,128)(2,1)S(1)}, bf16[192,128]{1,0:T(8,128)(2,1)S(1)}, u32[]{:S(2)}, u32[]{:S(2)}) %collective-permute-start.7) | collective-permute-done | bytes 49184 | tf_op jit(solution)/shard_map/ppermute | solution.py:552
  30.7 1.0 %collective-permute-start.8 = (bf16[192,128]{1,0:T(8,128)(2,1)S(1)}, bf16[192,128]{1,0:T(8,128)(2,1)S(1)}, u32[]{:S(2)}, u32[]{:S(2)}) collective-permute-start(bf16[192,128]{1,0:T(8,128)(2,1)S(1)} %add_convert_fusion.1), channel_id=1, source_target_pairs={{0,4},{1,5},{2,6},{3,7},{4,0},{5,1},{6,2},{7,3},{8,12},{9,13},{10,... | collective-permute-start | bytes 147464 | tf_op jit(solution)/shard_map/ppermute | solution.py:552
  31.7 0.3 shard_map.116.gh
  32.0 0.1 collective-permute-start.10
  32.1 3.4 %collective-permute-start.11 = (f32[24,512]{1,0:T(8,128)S(1)}, f32[24,512]{1,0:T(8,128)S(1)}, u32[]{:S(2)}, u32[]{:S(2)}) collective-permute-start(f32[24,512]{1,0:T(8,128)S(1)} %shard_map.116.gh), channel_id=1, source_target_pairs={{0,15},{1,2},{2,1},{3,4},{4,3},{5,6},{6,5},{7,8},{8,7},{9,10},{10,... | collective-permute-start | bytes 147464 | tf_op jit(solution)/shard_map/ppermute | solution.py:456
  35.5 0.0 collective-permute-done.8
  35.5 1.4 %collective-permute-start.9 = (bf16[192,128]{1,0:T(8,128)(2,1)S(1)}, bf16[192,128]{1,0:T(8,128)(2,1)S(1)}, u32[]{:S(2)}, u32[]{:S(2)}) collective-permute-start(bf16[192,128]{1,0:T(8,128)(2,1)S(1)} %add_convert_fusion), channel_id=1, source_target_pairs={{0,8},{1,9},{2,10},{3,11},{4,12},{5,13},{6,14},{7,15},{8,0},{9,1},... | collective-permute-start | bytes 147464 | tf_op jit(solution)/shard_map/ppermute | solution.py:552
  36.9 0.0 collective-permute-done.10.gh_a
  36.9 1.6 %collective-permute-done.11.gh_b = f32[24,512]{1,0:T(8,128)S(1)} collective-permute-done((f32[24,512]{1,0:T(8,128)S(1)}, f32[24,512]{1,0:T(8,128)S(1)}, u32[]{:S(2)}, u32[]{:S(2)}) %collective-permute-start.11) | collective-permute-done | bytes 49184 | tf_op jit(solution)/shard_map/ppermute | solution.py:456
  38.5 0.8 %shard_map.117 = f32[2,8,512]{2,1,0:T(8,128)} custom-call(f32[24,512]{1,0:T(8,128)S(1)} %shard_map.116.gh, f32[24,512]{1,0:T(8,128)S(1)} %collective-permute-done.10.gh_a, f32[24,512]{1,0:T(8,128)S(1)} %collective-permute-done.11.gh_b, f32[2,24,512]{2,1,0:T(8,128)S(1)} %get-tuple-element.50.u), custom_call_target="tpu_custom_call" | custom-call | flops 100000000 | bytes 2000000 | tf_op jit(solution)/shard_map/pallas_call | solution.py:431
  39.3 1.5 %collective-permute-done.9 = bf16[192,128]{1,0:T(8,128)(2,1)S(1)} collective-permute-done((bf16[192,128]{1,0:T(8,128)(2,1)S(1)}, bf16[192,128]{1,0:T(8,128)(2,1)S(1)}, u32[]{:S(2)}, u32[]{:S(2)}) %collective-permute-start.9) | collective-permute-done | bytes 49184 | tf_op jit(solution)/shard_map/ppermute | solution.py:552
  40.8 0.1 collective-permute-start.12
  40.9 1.3 %collective-permute-done.12.other = f32[192,128]{1,0:T(8,128)S(1)} collective-permute-done((f32[192,128]{1,0:T(8,128)S(1)}, f32[192,128]{1,0:T(8,128)S(1)}, u32[]{:S(2)}, u32[]{:S(2)}) %collective-permute-start.12) | collective-permute-done | bytes 98336 | tf_op jit(solution)/shard_map/ppermute | solution.py:557
  42.2 1.0 %shard_map.118 = (f32[9,2,48]{2,1,0:T(2,128)}, f32[9,48,48]{2,1,0:T(8,128)}, f32[9,48,48]{2,1,0:T(8,128)}, f32[9,2,48]{2,1,0:T(2,128)}) custom-call(f32[192,128]{1,0:T(8,128)S(1)} %convert_add_fusion.mine, f32[192,128]{1,0:T(8,128)S(1)} %collective-permute-done.12.other), custom_call_target="tpu_custom_call" | custom-call | flops 100000000 | bytes 2000000 | tf_op jit(solution)/shard_map/pallas_call | solution.py:431
  (4 shorter events, 0.1 us)
Async XLA Ops:
  0.6 9.0 %copy-start = (bf16[2,3,8,48,512]{4,3,2,1,0:T(8,128)(2,1)S(1)}, bf16[2,3,8,48,512]{4,3,2,1,0:T(8,128)(2,1)}, u32[]{:S(2)}) copy-start(bf16[2,3,8,48,512]{4,3,2,1,0:T(8,128)(2,1)} %pre.5) | copy-start | bytes 7077892
  0.6 9.0 %copy-start.1 = (f32[2,2,8,512]{3,2,1,0:T(8,128)S(1)}, f32[2,2,8,512]{3,2,1,0:T(8,128)}, u32[]{:S(2)}) copy-start(f32[2,2,8,512]{3,2,1,0:T(8,128)} %states.7) | copy-start | bytes 196612
  0.7 9.0 %copy-start.2 = (f32[2,8,512]{2,1,0:T(8,128)S(1)}, f32[2,8,512]{2,1,0:T(8,128)}, u32[]{:S(2)}) copy-start(f32[2,8,512]{2,1,0:T(8,128)} %cot.5) | copy-start | bytes 98308
  0.7 10.1 %copy-start.3 = (bf16[9,48,48]{2,1,0:T(8,128)(2,1)S(1)}, bf16[9,48,48]{2,1,0:T(8,128)(2,1)}, u32[]{:S(2)}) copy-start(bf16[9,48,48]{2,1,0:T(8,128)(2,1)} %w2.1) | copy-start | bytes 124420
  0.7 10.1 %copy-start.4 = (bf16[9,48,48]{2,1,0:T(8,128)(2,1)S(1)}, bf16[9,48,48]{2,1,0:T(8,128)(2,1)}, u32[]{:S(2)}) copy-start(bf16[9,48,48]{2,1,0:T(8,128)(2,1)} %w3.1) | copy-start | bytes 124420
  0.7 10.1 %copy-start.5 = (bf16[9,48,2]{1,2,0:T(2,128)(2,1)S(1)}, bf16[9,48,2]{1,2,0:T(2,128)(2,1)}, u32[]{:S(2)}) copy-start(bf16[9,48,2]{1,2,0:T(2,128)(2,1)} %param.10) | copy-start | bytes 5188
  0.7 10.1 %copy-start.6 = (bf16[9,2,48]{2,1,0:T(2,128)(2,1)S(1)}, bf16[9,2,48]{2,1,0:T(2,128)(2,1)}, u32[]{:S(2)}) copy-start(bf16[9,2,48]{2,1,0:T(2,128)(2,1)} %w4.1) | copy-start | bytes 5188
  3.4 7.7 %collective-permute-start = (bf16[192,512]{1,0:T(8,128)(2,1)}, bf16[192,512]{1,0:T(8,128)(2,1)S(1)}, u32[]{:S(2)}, u32[]{:S(2)}) collective-permute-start(bf16[192,512]{1,0:T(8,128)(2,1)} %get-tuple-element.31), channel_id=1, source_target_pairs={{0,1},{1,0},{2,3},{3,2},{4,5},{5,4},{6,7},{7,6},{8,9},{9,8},{10,11... | collective-permute-start | bytes 589832 | tf_op jit(solution)/shard_map/ppermute | solution.py:457
  4.0 9.2 %collective-permute-start.1 = (bf16[192,512]{1,0:T(8,128)(2,1)}, bf16[192,512]{1,0:T(8,128)(2,1)S(1)}, u32[]{:S(2)}, u32[]{:S(2)}) collective-permute-start(bf16[192,512]{1,0:T(8,128)(2,1)} %get-tuple-element.32), channel_id=1, source_target_pairs={{0,15},{1,2},{2,1},{3,4},{4,3},{5,6},{6,5},{7,8},{8,7},{9,10},{10,... | collective-permute-start | bytes 589832 | tf_op jit(solution)/shard_map/ppermute | solution.py:456
  10.1 11.5 %collective-permute-start.4 = (bf16[176,512]{1,0:T(8,128)(2,1)S(1)}, bf16[176,512]{1,0:T(8,128)(2,1)S(1)}, u32[]{:S(2)}, u32[]{:S(2)}) collective-permute-start(bf16[176,512]{1,0:T(8,128)(2,1)S(1)} %get-tuple-element.43), channel_id=1, source_target_pairs={{0,1},{1,0},{2,3},{3,2},{4,5},{5,4},{6,7},{7,6},{8,9},{9,8},{10,11... | collective-permute-start | bytes 540680 | tf_op jit(solution)/shard_map/ppermute | solution.py:457
  10.2 11.4 %collective-permute-start.5 = (bf16[176,512]{1,0:T(8,128)(2,1)S(1)}, bf16[176,512]{1,0:T(8,128)(2,1)S(1)}, u32[]{:S(2)}, u32[]{:S(2)}) collective-permute-start(bf16[176,512]{1,0:T(8,128)(2,1)S(1)} %get-tuple-element.44), channel_id=1, source_target_pairs={{0,15},{1,2},{2,1},{3,4},{4,3},{5,6},{6,5},{7,8},{8,7},{9,10},{10,... | collective-permute-start | bytes 540680 | tf_op jit(solution)/shard_map/ppermute | solution.py:456
  15.1 6.5 %collective-permute-start.2 = (f32[24,512]{1,0:T(8,128)S(1)}, f32[24,512]{1,0:T(8,128)S(1)}, u32[]{:S(2)}, u32[]{:S(2)}) collective-permute-start(f32[24,512]{1,0:T(8,128)S(1)} %get-tuple-element.37.gh), channel_id=1, source_target_pairs={{0,1},{1,0},{2,3},{3,2},{4,5},{5,4},{6,7},{7,6},{8,9},{9,8},{10,11... | collective-permute-start | bytes 147464 | tf_op jit(solution)/shard_map/ppermute | solution.py:457
  15.6 6.2 %collective-permute-start.3 = (f32[24,512]{1,0:T(8,128)S(1)}, f32[24,512]{1,0:T(8,128)S(1)}, u32[]{:S(2)}, u32[]{:S(2)}) collective-permute-start(f32[24,512]{1,0:T(8,128)S(1)} %get-tuple-element.37.gh), channel_id=1, source_target_pairs={{0,15},{1,2},{2,1},{3,4},{4,3},{5,6},{6,5},{7,8},{8,7},{9,10},{10,... | collective-permute-start | bytes 147464 | tf_op jit(solution)/shard_map/ppermute | solution.py:456
  25.1 1.4 %collective-permute-start.6 = (f32[192,128]{1,0:T(8,128)S(1)}, f32[192,128]{1,0:T(8,128)S(1)}, u32[]{:S(2)}, u32[]{:S(2)}) collective-permute-start(f32[192,128]{1,0:T(8,128)S(1)} %get-tuple-element.47), channel_id=1, source_target_pairs={{0,1},{1,0},{2,3},{3,2},{4,5},{5,4},{6,7},{7,6},{8,9},{9,8},{10,11... | collective-permute-start | bytes 294920 | tf_op jit(solution)/shard_map/ppermute | solution.py:548
  26.5 4.2 %collective-permute-start.7 = (bf16[192,128]{1,0:T(8,128)(2,1)S(1)}, bf16[192,128]{1,0:T(8,128)(2,1)S(1)}, u32[]{:S(2)}, u32[]{:S(2)}) collective-permute-start(bf16[192,128]{1,0:T(8,128)(2,1)S(1)} %add_convert_fusion.2), channel_id=1, source_target_pairs={{0,2},{1,3},{2,0},{3,1},{4,6},{5,7},{6,4},{7,5},{8,10},{9,11},{10,... | collective-permute-start | bytes 147464 | tf_op jit(solution)/shard_map/ppermute | solution.py:552
  30.7 4.8 %collective-permute-start.8 = (bf16[192,128]{1,0:T(8,128)(2,1)S(1)}, bf16[192,128]{1,0:T(8,128)(2,1)S(1)}, u32[]{:S(2)}, u32[]{:S(2)}) collective-permute-start(bf16[192,128]{1,0:T(8,128)(2,1)S(1)} %add_convert_fusion.1), channel_id=1, source_target_pairs={{0,4},{1,5},{2,6},{3,7},{4,0},{5,1},{6,2},{7,3},{8,12},{9,13},{10,... | collective-permute-start | bytes 147464 | tf_op jit(solution)/shard_map/ppermute | solution.py:552
  32.0 4.8 %collective-permute-start.10 = (f32[24,512]{1,0:T(8,128)S(1)}, f32[24,512]{1,0:T(8,128)S(1)}, u32[]{:S(2)}, u32[]{:S(2)}) collective-permute-start(f32[24,512]{1,0:T(8,128)S(1)} %shard_map.116.gh), channel_id=1, source_target_pairs={{0,1},{1,0},{2,3},{3,2},{4,5},{5,4},{6,7},{7,6},{8,9},{9,8},{10,11... | collective-permute-start | bytes 147464 | tf_op jit(solution)/shard_map/ppermute | solution.py:457
  32.1 6.4 %collective-permute-start.11 = (f32[24,512]{1,0:T(8,128)S(1)}, f32[24,512]{1,0:T(8,128)S(1)}, u32[]{:S(2)}, u32[]{:S(2)}) collective-permute-start(f32[24,512]{1,0:T(8,128)S(1)} %shard_map.116.gh), channel_id=1, source_target_pairs={{0,15},{1,2},{2,1},{3,4},{4,3},{5,6},{6,5},{7,8},{8,7},{9,10},{10,... | collective-permute-start | bytes 147464 | tf_op jit(solution)/shard_map/ppermute | solution.py:456
  35.5 5.3 %collective-permute-start.9 = (bf16[192,128]{1,0:T(8,128)(2,1)S(1)}, bf16[192,128]{1,0:T(8,128)(2,1)S(1)}, u32[]{:S(2)}, u32[]{:S(2)}) collective-permute-start(bf16[192,128]{1,0:T(8,128)(2,1)S(1)} %add_convert_fusion), channel_id=1, source_target_pairs={{0,8},{1,9},{2,10},{3,11},{4,12},{5,13},{6,14},{7,15},{8,0},{9,1},... | collective-permute-start | bytes 147464 | tf_op jit(solution)/shard_map/ppermute | solution.py:552
  40.8 1.4 %collective-permute-start.12 = (f32[192,128]{1,0:T(8,128)S(1)}, f32[192,128]{1,0:T(8,128)S(1)}, u32[]{:S(2)}, u32[]{:S(2)}) collective-permute-start(f32[192,128]{1,0:T(8,128)S(1)} %convert_add_fusion.mine), channel_id=1, source_target_pairs={{0,1},{1,0},{2,3},{3,2},{4,5},{5,4},{6,7},{7,6},{8,9},{9,8},{10,11... | collective-permute-start | bytes 294920 | tf_op jit(solution)/shard_map/ppermute | solution.py:557

commit v3 on v2

--- a/solution.py
+++ b/solution.py
@@ -101,21 +101,25 @@
 
 
 def row_conv(w_ref, src, src0, lo, hi, ch, emit):
+    spare = w_ref.shape[1] // 3 - (BLOCK + 2) * ch
     row = lo
     while row < hi:
-        count = min(BLOCK, hi - row)
-        rhs = src[(row - 1 - src0) * ch : (row + count + 1 - src0) * ch, :]
-        lhs = w_ref[: count * 3 * ch, : (count + 2) * ch]
-        y = jnp.dot(lhs, rhs, preferred_element_type=F32)
-        for k in range(count):
-            base = 3 * ch * k
-            e = (
-                y[base + ch : base + 2 * ch]
-                + lane_roll(y[base : base + ch], -1)
-                + lane_roll(y[base + 2 * ch : base + 3 * ch], 1)
-            )
-            emit(row + k, e)
-        row += count
+        start = min(row, hi - BLOCK)
+        skip = row - start
+        first = (start - 1 - src0) * ch
+        parts = []
+        for q in range(3):
+            parts.append(src[q, first : first + (BLOCK + 2) * ch, :])
+            if spare:
+                parts.append(jnp.zeros((spare, src.shape[2]), BF16))
+        y = jnp.dot(
+            w_ref[skip * ch : BLOCK * ch, :],
+            jnp.concatenate(parts, axis=0),
+            preferred_element_type=F32,
+        )
+        for k in range(BLOCK - skip):
+            emit(row + k, y[k * ch : (k + 1) * ch])
+        row = start + BLOCK
 
 
 def chain(x4, pre, m_a, m_b, even, w4, w3, w2, d3, d2, d1, rows, ch):
@@ -123,18 +127,23 @@
 
     def mask_rows(layer, row):
         if rows <= row < 2 * rows:
-            return pre[layer, row - rows].astype(F32)
+            return pre[layer, row - rows]
         above = row < rows
         border, start = ((e1, e3 + e2), (e2, e3), (e3, 0))[layer]
         k = start + (row - (rows - border) if above else row - 2 * rows)
-        a, b = (m[k * ch : (k + 1) * ch, :].astype(F32) for m in (m_a, m_b))
+        a, b = (m[k * ch : (k + 1) * ch, :] for m in (m_a, m_b))
         return jnp.where(even, b, a) if above else jnp.where(even, a, b)
 
     def store(dst, layer, first):
         def emit(row, e):
-            dst[(row - first) * ch : (row - first + 1) * ch, :] = jnp.where(
-                mask_rows(layer, row) > 0, e, 0.0
-            ).astype(BF16)
+            d = e.astype(BF16)
+            d = jnp.where(mask_rows(layer, row) > 0, d, jnp.zeros_like(d))
+            at = slice((row - first) * ch, (row - first + 1) * ch)
+            if len(dst.shape) == 2:
+                dst[at, :] = d
+            else:
+                for q in range(3):
+                    dst[q, at, :] = lane_roll(d, q - 1) if q != 1 else d
 
         return emit
 
@@ -179,30 +188,41 @@
 
     def three(ref, row, border):
         row -= rows - border
-        return ref[(row - 1) * ch : (row + 2) * ch, :]
-
-    totals = [None] * 4
-    for i in range(rows):
-        row = rows + i
-        source = [jnp.maximum(pre[layer, i].astype(F32), 0.0) for layer in range(3)]
-        moved = [
-            jnp.concatenate([lane_roll(s, 1), s, lane_roll(s, -1)], axis=0).astype(BF16)
-            for s in source[:2]
-        ]
-        terms = (
-            product(
-                x0s[SMALL * i : SMALL * (i + 3), :].astype(BF16),
-                d1[(i + EMPTY) * ch : (i + EMPTY + 1) * ch, :],
+        return ref[1, (row - 1) * ch : (row + 2) * ch, :]
+
+    def lanes(values):
+        return jnp.concatenate(list(values), axis=1)
+
+    def source(layer, i):
+        a = pre[layer, i]
+        return jnp.maximum(a, jnp.zeros_like(a))
+
+    def moved(layer, i):
+        h = source(layer, i)
+        return jnp.concatenate([lane_roll(h, 1), h, lane_roll(h, -1)], axis=0)
+
+    each = range(rows)
+    return (
+        product(
+            lanes(x0s[SMALL * i : SMALL * (i + 3), :].astype(BF16) for i in each),
+            lanes(d1[(i + EMPTY) * ch : (i + EMPTY + 1) * ch, :] for i in each),
+        ),
+        product(
+            lanes(three(d2, rows + i, BORDERS[1]) for i in each),
+            lanes(moved(0, i) for i in each),
+        ),
+        product(
+            lanes(three(d3, rows + i, BORDERS[0]) for i in each),
+            lanes(moved(1, i) for i in each),
+        ),
+        product(
+            lanes(
+                x4[SMALL * (rows + i - 1) : SMALL * (rows + i + 2), :].astype(BF16)
+                for i in each
             ),
-            product(three(d2, row, BORDERS[1]), moved[0]),
-            product(three(d3, row, BORDERS[0]), moved[1]),
-            product(
-                x4[SMALL * (row - 1) : SMALL * (row + 2), :].astype(BF16),
-                source[2].astype(BF16),
-            ),
-        )
-        totals = [t if old is None else old + t for old, t in zip(totals, terms)]
-    return totals
+            lanes(source(2, i) for i in each),
+        ),
+    )
 
 
 def pack_rows(ch):
@@ -230,45 +250,50 @@
         t_ref[r0:r1, c0:c1] = value
 
 
-def border_copies(axis, takes, rows, ch, pre_hbm, out_a, out_b, sems):
+def gather_kernel(
+    axis, takes, rows, ch, base, step, with_d4,
+    pre_hbm, states, cot, out_a, out_b, sems, u, g,
+):
     even = lax.rem(lax.axis_index(axis), 2) == 0
-    copies = []
-    for step, layer, count, dst in takes:
+    copies = [pltpu.make_async_copy(states.at[step], u, sems.at[0])]
+    if with_d4:
+        copies.append(pltpu.make_async_copy(cot, g, sems.at[1]))
+    first = len(copies)
+    for layer, count, dst in takes:
         low, high = 0, (rows - count) * ch
         for out, start in (
             (out_a, jnp.where(even, high, low)),
             (out_b, jnp.where(even, low, high)),
         ):
-            copy = pltpu.make_async_copy(
-                pre_hbm.at[step, layer, pl.ds(pl.multiple_of(start, ch), count * ch)],
-                out.at[pl.ds(dst * ch, count * ch)],
-                sems.at[len(copies)],
+            copies.append(
+                pltpu.make_async_copy(
+                    pre_hbm.at[step, layer, pl.ds(pl.multiple_of(start, ch), count * ch)],
+                    out.at[pl.ds(dst * ch, count * ch)],
+                    sems.at[len(copies)],
+                )
             )
-            copy.start()
-            copies.append(copy)
-    return copies
-
-
-def gather_kernel(axis, takes, rows, ch, base, step, with_d4, pre_hbm, states, cot, out_a, out_b, sems):
-    copies = border_copies(axis, takes, rows, ch, pre_hbm, out_a, out_b, sems)
-    planes = [split_terms(states[step, comp]) for comp in range(2)]
+    for copy in copies:
+        copy.start()
+    for copy in copies[:first]:
+        copy.wait()
+    planes = [split_terms(u[comp]) for comp in range(2)]
     if with_d4:
-        planes.append(jnp.concatenate([cot[0], cot[1]], axis=0).astype(BF16))
+        planes.append(jnp.concatenate([g[0], g[1]], axis=0).astype(BF16))
     for i, plane in enumerate(planes):
         for out in (out_a, out_b):
             out[base + 2 * rows * i : base + 2 * rows * (i + 1), :] = plane
-    for copy in copies:
+    for copy in copies[first:]:
         copy.wait()
 
 
 def weights_kernel(ch, w1, w2, w3, w4, o1, o2, o3, o4):
     for w, o in ((w3, o3), (w2, o2)):
+        wide = o.shape[1] // 3
         for q in range(3):
             block = jnp.concatenate([w[3 * (2 - m) + q].astype(F32) for m in range(3)], axis=0)
             block = block.T.astype(BF16)
             for b in range(BLOCK):
-                r = (3 * b + q) * ch
-                o[r : r + ch, :] = placed(block, b * ch, o.shape[1])
+                o[b * ch : (b + 1) * ch, q * wide : (q + 1) * wide] = placed(block, b * ch, wide)
     zero = jnp.zeros((SMALL - 6, ch), F32)
     block = jnp.concatenate(
         [
@@ -465,16 +490,17 @@
         for layer, border in zip((2, 1, 0), BORDERS):
             if not border:
                 continue
-            takes.append((step, layer, border, total))
+            takes.append((layer, border, total))
             total += border
         base = total * ch
         out = shape(base + (6 if with_d4 else 4) * rows, width, dtype=BF16)
         pack = pl.pallas_call(
             functools.partial(gather_kernel, axis, takes, rows, ch, base, step, with_d4),
             out_shape=[out, out],
-            in_specs=[pl.BlockSpec(memory_space=pltpu.HBM), VMEM, VMEM],
+            in_specs=[pl.BlockSpec(memory_space=pltpu.HBM)] * 3,
             out_specs=[VMEM, VMEM],
-            scratch_shapes=[pltpu.SemaphoreType.DMA((2 * len(takes),))],
+            scratch_shapes=[pltpu.SemaphoreType.DMA((2 * len(takes) + 2,))]
+            + [pltpu.VMEM((2, rows, width), F32)] * 2,
             compiler_params=pltpu.CompilerParams(vmem_limit_bytes=VMEM_BYTES - room),
         )
         a, b = pack(flat, states, cotangent)
@@ -486,12 +512,13 @@
     def bands(n, m):
         return shape(n, m, dtype=BF16)
 
+    wide = -(-(BLOCK + 2) * ch // LANES) * LANES
     w1, w2, w3, w4 = call(
         functools.partial(weights_kernel, ch),
         [
             bands(3 * SMALL, (BLOCK + 2) * ch),
-            bands(3 * BLOCK * ch, (BLOCK + 2) * ch),
-            bands(3 * BLOCK * ch, (BLOCK + 2) * ch),
+            bands(BLOCK * ch, 3 * wide),
+            bands(BLOCK * ch, 3 * wide),
             bands(BLOCK4 * ch, (BLOCK4 + 2) * SMALL),
         ],
         [],
@@ -509,7 +536,11 @@
 
     x4_shape = shape(3 * rows * SMALL, width)
     x0_shape = shape((rows + 2) * SMALL, width)
-    d_shapes = [d_shape(BORDERS[0]), d_shape(BORDERS[1]), d_shape(EMPTY)]
+    d_shapes = [
+        shape(3, *d_shape(BORDERS[0]).shape, dtype=BF16),
+        shape(3, *d_shape(BORDERS[1]).shape, dtype=BF16),
+        d_shape(EMPTY),
+    ]
     planes = shape(2, 3 * rows, width)
     part = shape(2 * rows + SMALL, width)
     total = shape(pack_rows(ch), LANES)

time: 43.3 us -> 41.7 us (0.963)
  Pallas kernels: 12.6 us -> 10.7 us
    pallas_call x7, Pallas kernels: 9.44 us -> 8.26 us  [call(): pl.pallas_call(kernel, out_shape=outs, grid=(1,) if specs else (), in_spe...]
    pallas_call x2, Pallas kernels: 3.16 us -> 2.42 us  [borders(): a, b = pack(flat, states, cotangent)]
  transfers between devices with their start and end apart: 13 -> 13, of which waited for: 7 -> 7; matrix products, arithmetic and copies ran while one was open for 0% -> 0% of each run, Pallas kernels for 13% -> 12%
where the time goes in v3:
time: 41.7 us; the launch traced here: 41.6 us
  starting transfers between devices  18.2 us (44%)
  waiting for transfers between devices  11.8 us (28%)
  Pallas kernels  10.7 us (26%)
  between operations  0.81 us (2%)
    ppermute x4, starting transfers between devices, swap(): b = lax.ppermute(for_b, axis, pair_b)  13.8 us
    pallas_call x7, Pallas kernels, call(): pl.pallas_call(kernel, out_shape=outs, grid=(1,) if specs else (), in_spe...  8.26 us
    ppermute x3, waiting for transfers between devices, on_device(): got = lax.ppermute(mine, axis, [(i, i ^ bit) for i in range(count)])  5.03 us
    ppermute x4, waiting for transfers between devices, swap(): b = lax.ppermute(for_b, axis, pair_b)  4.19 us
    ppermute x3, starting transfers between devices, on_device(): got = lax.ppermute(mine, axis, [(i, i ^ bit) for i in range(count)])  3.01 us
    pallas_call x2, Pallas kernels, borders(): a, b = pack(flat, states, cotangent)  2.42 us
    ppermute x1, waiting for transfers between devices, on_device(): mine = keep + lax.ppermute(give, axis, pair_a)  1.29 us
    ppermute x1, waiting for transfers between devices, on_device(): other = lax.ppermute(mine, axis, pair_a)  1.29 us
  transfers between devices with their start and end apart: 13, of which 7 were waited for; matrix products, arithmetic and copies ran while one was open for 0% of the time, Pallas kernels for 12%

profile of v3, /device:TPU:0, one launch (start us, length us, event | category | flops | bytes accessed | tf_op | source)
XLA Modules:
  0.0 41.6 jit_solution(14278925192996214529)
XLA Ops:
  0.6 0.0 copy-start
  0.6 0.0 copy-start.1
  0.7 0.0 copy-start.2
  0.7 1.9 %shard_map.110 = (bf16[192,512]{1,0:T(8,128)(2,1)}, bf16[192,512]{1,0:T(8,128)(2,1)}) custom-call(bf16[2,3,384,512]{3,2,1,0:T(8,128)(2,1)} %bitcast.3, f32[2,2,8,512]{3,2,1,0:T(8,128)} %states.7, f32[2,8,512]{2,1,0:T(8,128)} %cot.5), custom_call_target="tpu_custom_call" | custom-call | tf_op jit(solution)/shard_map/pallas_call | solution.py:506
  2.6 0.0 copy-start.3
  2.6 0.0 copy-start.4
  2.6 0.0 copy-start.5
  2.6 0.0 copy-start.6
  2.6 0.6 %collective-permute-start = (bf16[192,512]{1,0:T(8,128)(2,1)}, bf16[192,512]{1,0:T(8,128)(2,1)S(1)}, u32[]{:S(2)}, u32[]{:S(2)}) collective-permute-start(bf16[192,512]{1,0:T(8,128)(2,1)} %get-tuple-element.31), channel_id=1, source_target_pairs={{0,1},{1,0},{2,3},{3,2},{4,5},{5,4},{6,7},{7,6},{8,9},{9,8},{10,11... | collective-permute-start | bytes 589832 | tf_op jit(solution)/shard_map/ppermute | solution.py:482
  3.2 5.6 %collective-permute-start.1 = (bf16[192,512]{1,0:T(8,128)(2,1)}, bf16[192,512]{1,0:T(8,128)(2,1)S(1)}, u32[]{:S(2)}, u32[]{:S(2)}) collective-permute-start(bf16[192,512]{1,0:T(8,128)(2,1)} %get-tuple-element.32), channel_id=1, source_target_pairs={{0,15},{1,2},{2,1},{3,4},{4,3},{5,6},{6,5},{7,8},{8,7},{9,10},{10,... | collective-permute-start | bytes 589832 | tf_op jit(solution)/shard_map/ppermute | solution.py:481
  8.8 0.0 copy-done
  8.8 0.0 copy-done.1
  8.8 0.0 copy-done.2
  8.8 0.5 %shard_map.114 = (bf16[176,512]{1,0:T(8,128)(2,1)S(1)}, bf16[176,512]{1,0:T(8,128)(2,1)S(1)}) custom-call(bf16[2,3,384,512]{3,2,1,0:T(8,128)(2,1)S(1)} %bitcast.4, f32[2,2,8,512]{3,2,1,0:T(8,128)S(1)} %copy-done.1, f32[2,8,512]{2,1,0:T(8,128)S(1)} %copy-done.2), custom_call_target="tpu_custom_call" | custom-call | tf_op jit(solution)/shard_map/pallas_call | solution.py:506
  9.3 0.1 collective-permute-start.4
  9.4 0.6 %collective-permute-start.5 = (bf16[176,512]{1,0:T(8,128)(2,1)S(1)}, bf16[176,512]{1,0:T(8,128)(2,1)S(1)}, u32[]{:S(2)}, u32[]{:S(2)}) collective-permute-start(bf16[176,512]{1,0:T(8,128)(2,1)S(1)} %get-tuple-element.44), channel_id=1, source_target_pairs={{0,15},{1,2},{2,1},{3,4},{4,3},{5,6},{6,5},{7,8},{8,7},{9,10},{10,... | collective-permute-start | bytes 540680 | tf_op jit(solution)/shard_map/ppermute | solution.py:481
  10.1 0.0 copy-done.3
  10.1 0.0 copy-done.4
  10.1 0.0 copy-done.5
  10.1 0.0 copy-done.6
  10.1 0.4 shard_map.111
  10.4 0.0 collective-permute-done.m_a
  10.4 1.9 %collective-permute-done.1.m_b = bf16[192,512]{1,0:T(8,128)(2,1)S(1)} collective-permute-done((bf16[192,512]{1,0:T(8,128)(2,1)}, bf16[192,512]{1,0:T(8,128)(2,1)S(1)}, u32[]{:S(2)}, u32[]{:S(2)}) %collective-permute-start.1) | collective-permute-done | bytes 196640 | tf_op jit(solution)/shard_map/ppermute | solution.py:481
  12.4 1.7 %shard_map.112 = (f32[24,512]{1,0:T(8,128)S(1)}, f32[192,512]{1,0:T(8,128)S(1)}, bf16[3,576,512]{2,1,0:T(8,128)(2,1)S(1)}, bf16[3,480,512]{2,1,0:T(8,128)(2,1)S(1)}, bf16[576,512]{1,0:T(8,128)(2,1)S(1)}) custom-call(f32[2,8,512]{2,1,0:T(8,128)S(1)} %copy-done.2, bf16[2,3,8,48,512]{4,3,2,1,0:T(8,128)(2,1)S(1)} %copy-done, ...), custom_call_target="tpu_custom_call" | custom-call | flops 100000000 | bytes 2000000 | tf_op jit(solution)/shard_map/pallas_call | solution.py:456
  14.1 0.5 %collective-permute-start.2 = (f32[24,512]{1,0:T(8,128)S(1)}, f32[24,512]{1,0:T(8,128)S(1)}, u32[]{:S(2)}, u32[]{:S(2)}) collective-permute-start(f32[24,512]{1,0:T(8,128)S(1)} %get-tuple-element.37.gh), channel_id=1, source_target_pairs={{0,1},{1,0},{2,3},{3,2},{4,5},{5,4},{6,7},{7,6},{8,9},{9,8},{10,11... | collective-permute-start | bytes 147464 | tf_op jit(solution)/shard_map/ppermute | solution.py:482
  14.6 4.2 %collective-permute-start.3 = (f32[24,512]{1,0:T(8,128)S(1)}, f32[24,512]{1,0:T(8,128)S(1)}, u32[]{:S(2)}, u32[]{:S(2)}) collective-permute-start(f32[24,512]{1,0:T(8,128)S(1)} %get-tuple-element.37.gh), channel_id=1, source_target_pairs={{0,15},{1,2},{2,1},{3,4},{4,3},{5,6},{6,5},{7,8},{8,7},{9,10},{10,... | collective-permute-start | bytes 147464 | tf_op jit(solution)/shard_map/ppermute | solution.py:481
  18.8 1.4 %shard_map.113 = (f32[384,128]{1,0:T(8,128)S(1)}, f32[2,24,512]{2,1,0:T(8,128)S(1)}) custom-call(f32[192,512]{1,0:T(8,128)S(1)} %get-tuple-element.38.x4, bf16[3,576,512]{2,1,0:T(8,128)(2,1)S(1)} %get-tuple-element.39.d3, bf16[3,480,512]{2,1,0:T(8,128)(2,1)S(1)} %get-tuple-element.40.d2, bf16[576,512]{1,0:T(8,128)(2,1)S(1)} %get-tuple-element.41.d1, ...), custom_call_target="tpu_custom_call" | custom-call | flops 100000000 | bytes 2000000 | tf_op jit(solution)/shard_map/pallas_call | solution.py:456
  20.2 0.0 collective-permute-done.4.m_a
  20.2 0.0 collective-permute-done.5.m_b
  20.2 0.0 collective-permute-done.2.gh_a
  20.2 0.6 %collective-permute-done.3.gh_b = f32[24,512]{1,0:T(8,128)S(1)} collective-permute-done((f32[24,512]{1,0:T(8,128)S(1)}, f32[24,512]{1,0:T(8,128)S(1)}, u32[]{:S(2)}, u32[]{:S(2)}) %collective-permute-start.3) | collective-permute-done | bytes 49184 | tf_op jit(solution)/shard_map/ppermute | solution.py:481
  20.8 2.7 %shard_map.115 = (f32[192,128]{1,0:T(8,128)S(1)}, f32[192,128]{1,0:T(8,128)S(1)}, f32[2,8,512]{2,1,0:T(8,128)S(1)}, f32[2,24,512]{2,1,0:T(8,128)S(1)}, bf16[576,512]{1,0:T(8,128)(2,1)S(1)}) custom-call(f32[24,512]{1,0:T(8,128)S(1)} %get-tuple-element.37.gh, f32[24,512]{1,0:T(8,128)S(1)} %collective-permute-done.2.gh_a, ...), custom_call_target="tpu_custom_call" | custom-call | flops 100000000 | bytes 2000000 | tf_op jit(solution)/shard_map/pallas_call | solution.py:456
  23.5 0.1 collective-permute-start.6
  23.6 1.3 %collective-permute-done.6 = f32[192,128]{1,0:T(8,128)S(1)} collective-permute-done((f32[192,128]{1,0:T(8,128)S(1)}, f32[192,128]{1,0:T(8,128)S(1)}, u32[]{:S(2)}, u32[]{:S(2)}) %collective-permute-start.6) | collective-permute-done | bytes 98336 | tf_op jit(solution)/shard_map/ppermute | solution.py:579
  24.9 0.6 %collective-permute-start.7 = (bf16[192,128]{1,0:T(8,128)(2,1)S(1)}, bf16[192,128]{1,0:T(8,128)(2,1)S(1)}, u32[]{:S(2)}, u32[]{:S(2)}) collective-permute-start(bf16[192,128]{1,0:T(8,128)(2,1)S(1)} %add_convert_fusion.2), channel_id=1, source_target_pairs={{0,2},{1,3},{2,0},{3,1},{4,6},{5,7},{6,4},{7,5},{8,10},{9,11},{10,... | collective-permute-start | bytes 147464 | tf_op jit(solution)/shard_map/ppermute | solution.py:583
  25.5 3.5 %collective-permute-done.7 = bf16[192,128]{1,0:T(8,128)(2,1)S(1)} collective-permute-done((bf16[192,128]{1,0:T(8,128)(2,1)S(1)}, bf16[192,128]{1,0:T(8,128)(2,1)S(1)}, u32[]{:S(2)}, u32[]{:S(2)}) %collective-permute-start.7) | collective-permute-done | bytes 49184 | tf_op jit(solution)/shard_map/ppermute | solution.py:583
  29.1 1.0 %collective-permute-start.8 = (bf16[192,128]{1,0:T(8,128)(2,1)S(1)}, bf16[192,128]{1,0:T(8,128)(2,1)S(1)}, u32[]{:S(2)}, u32[]{:S(2)}) collective-permute-start(bf16[192,128]{1,0:T(8,128)(2,1)S(1)} %add_convert_fusion.1), channel_id=1, source_target_pairs={{0,4},{1,5},{2,6},{3,7},{4,0},{5,1},{6,2},{7,3},{8,12},{9,13},{10,... | collective-permute-start | bytes 147464 | tf_op jit(solution)/shard_map/ppermute | solution.py:583
  30.1 0.3 shard_map.116.gh
  30.4 0.1 collective-permute-start.10
  30.5 3.4 %collective-permute-start.11 = (f32[24,512]{1,0:T(8,128)S(1)}, f32[24,512]{1,0:T(8,128)S(1)}, u32[]{:S(2)}, u32[]{:S(2)}) collective-permute-start(f32[24,512]{1,0:T(8,128)S(1)} %shard_map.116.gh), channel_id=1, source_target_pairs={{0,15},{1,2},{2,1},{3,4},{4,3},{5,6},{6,5},{7,8},{8,7},{9,10},{10,... | collective-permute-start | bytes 147464 | tf_op jit(solution)/shard_map/ppermute | solution.py:481
  33.9 0.0 collective-permute-done.8
  33.9 1.4 %collective-permute-start.9 = (bf16[192,128]{1,0:T(8,128)(2,1)S(1)}, bf16[192,128]{1,0:T(8,128)(2,1)S(1)}, u32[]{:S(2)}, u32[]{:S(2)}) collective-permute-start(bf16[192,128]{1,0:T(8,128)(2,1)S(1)} %add_convert_fusion), channel_id=1, source_target_pairs={{0,8},{1,9},{2,10},{3,11},{4,12},{5,13},{6,14},{7,15},{8,0},{9,1},... | collective-permute-start | bytes 147464 | tf_op jit(solution)/shard_map/ppermute | solution.py:583
  35.3 0.0 collective-permute-done.10.gh_a
  35.3 1.6 %collective-permute-done.11.gh_b = f32[24,512]{1,0:T(8,128)S(1)} collective-permute-done((f32[24,512]{1,0:T(8,128)S(1)}, f32[24,512]{1,0:T(8,128)S(1)}, u32[]{:S(2)}, u32[]{:S(2)}) %collective-permute-start.11) | collective-permute-done | bytes 49184 | tf_op jit(solution)/shard_map/ppermute | solution.py:481
  36.9 0.8 %shard_map.117 = f32[2,8,512]{2,1,0:T(8,128)} custom-call(f32[24,512]{1,0:T(8,128)S(1)} %shard_map.116.gh, f32[24,512]{1,0:T(8,128)S(1)} %collective-permute-done.10.gh_a, f32[24,512]{1,0:T(8,128)S(1)} %collective-permute-done.11.gh_b, f32[2,24,512]{2,1,0:T(8,128)S(1)} %get-tuple-element.50.u), custom_call_target="tpu_custom_call" | custom-call | flops 100000000 | bytes 2000000 | tf_op jit(solution)/shard_map/pallas_call | solution.py:456
  37.7 1.5 %collective-permute-done.9 = bf16[192,128]{1,0:T(8,128)(2,1)S(1)} collective-permute-done((bf16[192,128]{1,0:T(8,128)(2,1)S(1)}, bf16[192,128]{1,0:T(8,128)(2,1)S(1)}, u32[]{:S(2)}, u32[]{:S(2)}) %collective-permute-start.9) | collective-permute-done | bytes 49184 | tf_op jit(solution)/shard_map/ppermute | solution.py:583
  39.2 0.1 collective-permute-start.12
  39.3 1.3 %collective-permute-done.12.other = f32[192,128]{1,0:T(8,128)S(1)} collective-permute-done((f32[192,128]{1,0:T(8,128)S(1)}, f32[192,128]{1,0:T(8,128)S(1)}, u32[]{:S(2)}, u32[]{:S(2)}) %collective-permute-start.12) | collective-permute-done | bytes 98336 | tf_op jit(solution)/shard_map/ppermute | solution.py:588
  40.6 1.0 %shard_map.118 = (f32[9,2,48]{2,1,0:T(2,128)}, f32[9,48,48]{2,1,0:T(8,128)}, f32[9,48,48]{2,1,0:T(8,128)}, f32[9,2,48]{2,1,0:T(2,128)}) custom-call(f32[192,128]{1,0:T(8,128)S(1)} %convert_add_fusion.mine, f32[192,128]{1,0:T(8,128)S(1)} %collective-permute-done.12.other), custom_call_target="tpu_custom_call" | custom-call | flops 100000000 | bytes 2000000 | tf_op jit(solution)/shard_map/pallas_call | solution.py:456
  (4 shorter events, 0.1 us)
Async XLA Ops:
  0.6 8.2 %copy-start = (bf16[2,3,8,48,512]{4,3,2,1,0:T(8,128)(2,1)S(1)}, bf16[2,3,8,48,512]{4,3,2,1,0:T(8,128)(2,1)}, u32[]{:S(2)}) copy-start(bf16[2,3,8,48,512]{4,3,2,1,0:T(8,128)(2,1)} %pre.5) | copy-start | bytes 7077892
  0.6 8.2 %copy-start.1 = (f32[2,2,8,512]{3,2,1,0:T(8,128)S(1)}, f32[2,2,8,512]{3,2,1,0:T(8,128)}, u32[]{:S(2)}) copy-start(f32[2,2,8,512]{3,2,1,0:T(8,128)} %states.7) | copy-start | bytes 196612
  0.7 8.2 %copy-start.2 = (f32[2,8,512]{2,1,0:T(8,128)S(1)}, f32[2,8,512]{2,1,0:T(8,128)}, u32[]{:S(2)}) copy-start(f32[2,8,512]{2,1,0:T(8,128)} %cot.5) | copy-start | bytes 98308
  2.6 7.5 %copy-start.3 = (bf16[9,48,48]{2,1,0:T(8,128)(2,1)S(1)}, bf16[9,48,48]{2,1,0:T(8,128)(2,1)}, u32[]{:S(2)}) copy-start(bf16[9,48,48]{2,1,0:T(8,128)(2,1)} %w2.1) | copy-start | bytes 124420
  2.6 7.5 %copy-start.4 = (bf16[9,48,48]{2,1,0:T(8,128)(2,1)S(1)}, bf16[9,48,48]{2,1,0:T(8,128)(2,1)}, u32[]{:S(2)}) copy-start(bf16[9,48,48]{2,1,0:T(8,128)(2,1)} %w3.1) | copy-start | bytes 124420
  2.6 7.5 %copy-start.5 = (bf16[9,48,2]{1,2,0:T(2,128)(2,1)S(1)}, bf16[9,48,2]{1,2,0:T(2,128)(2,1)}, u32[]{:S(2)}) copy-start(bf16[9,48,2]{1,2,0:T(2,128)(2,1)} %param.10) | copy-start | bytes 5188
  2.6 7.4 %copy-start.6 = (bf16[9,2,48]{2,1,0:T(2,128)(2,1)S(1)}, bf16[9,2,48]{2,1,0:T(2,128)(2,1)}, u32[]{:S(2)}) copy-start(bf16[9,2,48]{2,1,0:T(2,128)(2,1)} %w4.1) | copy-start | bytes 5188
  2.6 7.8 %collective-permute-start = (bf16[192,512]{1,0:T(8,128)(2,1)}, bf16[192,512]{1,0:T(8,128)(2,1)S(1)}, u32[]{:S(2)}, u32[]{:S(2)}) collective-permute-start(bf16[192,512]{1,0:T(8,128)(2,1)} %get-tuple-element.31), channel_id=1, source_target_pairs={{0,1},{1,0},{2,3},{3,2},{4,5},{5,4},{6,7},{7,6},{8,9},{9,8},{10,11... | collective-permute-start | bytes 589832 | tf_op jit(solution)/shard_map/ppermute | solution.py:482
  3.2 9.2 %collective-permute-start.1 = (bf16[192,512]{1,0:T(8,128)(2,1)}, bf16[192,512]{1,0:T(8,128)(2,1)S(1)}, u32[]{:S(2)}, u32[]{:S(2)}) collective-permute-start(bf16[192,512]{1,0:T(8,128)(2,1)} %get-tuple-element.32), channel_id=1, source_target_pairs={{0,15},{1,2},{2,1},{3,4},{4,3},{5,6},{6,5},{7,8},{8,7},{9,10},{10,... | collective-permute-start | bytes 589832 | tf_op jit(solution)/shard_map/ppermute | solution.py:481
  9.3 10.8 %collective-permute-start.4 = (bf16[176,512]{1,0:T(8,128)(2,1)S(1)}, bf16[176,512]{1,0:T(8,128)(2,1)S(1)}, u32[]{:S(2)}, u32[]{:S(2)}) collective-permute-start(bf16[176,512]{1,0:T(8,128)(2,1)S(1)} %get-tuple-element.43), channel_id=1, source_target_pairs={{0,1},{1,0},{2,3},{3,2},{4,5},{5,4},{6,7},{7,6},{8,9},{9,8},{10,11... | collective-permute-start | bytes 540680 | tf_op jit(solution)/shard_map/ppermute | solution.py:482
  9.4 10.8 %collective-permute-start.5 = (bf16[176,512]{1,0:T(8,128)(2,1)S(1)}, bf16[176,512]{1,0:T(8,128)(2,1)S(1)}, u32[]{:S(2)}, u32[]{:S(2)}) collective-permute-start(bf16[176,512]{1,0:T(8,128)(2,1)S(1)} %get-tuple-element.44), channel_id=1, source_target_pairs={{0,15},{1,2},{2,1},{3,4},{4,3},{5,6},{6,5},{7,8},{8,7},{9,10},{10,... | collective-permute-start | bytes 540680 | tf_op jit(solution)/shard_map/ppermute | solution.py:481
  14.1 6.1 %collective-permute-start.2 = (f32[24,512]{1,0:T(8,128)S(1)}, f32[24,512]{1,0:T(8,128)S(1)}, u32[]{:S(2)}, u32[]{:S(2)}) collective-permute-start(f32[24,512]{1,0:T(8,128)S(1)} %get-tuple-element.37.gh), channel_id=1, source_target_pairs={{0,1},{1,0},{2,3},{3,2},{4,5},{5,4},{6,7},{7,6},{8,9},{9,8},{10,11... | collective-permute-start | bytes 147464 | tf_op jit(solution)/shard_map/ppermute | solution.py:482
  14.6 6.2 %collective-permute-start.3 = (f32[24,512]{1,0:T(8,128)S(1)}, f32[24,512]{1,0:T(8,128)S(1)}, u32[]{:S(2)}, u32[]{:S(2)}) collective-permute-start(f32[24,512]{1,0:T(8,128)S(1)} %get-tuple-element.37.gh), channel_id=1, source_target_pairs={{0,15},{1,2},{2,1},{3,4},{4,3},{5,6},{6,5},{7,8},{8,7},{9,10},{10,... | collective-permute-start | bytes 147464 | tf_op jit(solution)/shard_map/ppermute | solution.py:481
  23.5 1.4 %collective-permute-start.6 = (f32[192,128]{1,0:T(8,128)S(1)}, f32[192,128]{1,0:T(8,128)S(1)}, u32[]{:S(2)}, u32[]{:S(2)}) collective-permute-start(f32[192,128]{1,0:T(8,128)S(1)} %get-tuple-element.47), channel_id=1, source_target_pairs={{0,1},{1,0},{2,3},{3,2},{4,5},{5,4},{6,7},{7,6},{8,9},{9,8},{10,11... | collective-permute-start | bytes 294920 | tf_op jit(solution)/shard_map/ppermute | solution.py:579
  24.9 4.2 %collective-permute-start.7 = (bf16[192,128]{1,0:T(8,128)(2,1)S(1)}, bf16[192,128]{1,0:T(8,128)(2,1)S(1)}, u32[]{:S(2)}, u32[]{:S(2)}) collective-permute-start(bf16[192,128]{1,0:T(8,128)(2,1)S(1)} %add_convert_fusion.2), channel_id=1, source_target_pairs={{0,2},{1,3},{2,0},{3,1},{4,6},{5,7},{6,4},{7,5},{8,10},{9,11},{10,... | collective-permute-start | bytes 147464 | tf_op jit(solution)/shard_map/ppermute | solution.py:583
  29.1 4.8 %collective-permute-start.8 = (bf16[192,128]{1,0:T(8,128)(2,1)S(1)}, bf16[192,128]{1,0:T(8,128)(2,1)S(1)}, u32[]{:S(2)}, u32[]{:S(2)}) collective-permute-start(bf16[192,128]{1,0:T(8,128)(2,1)S(1)} %add_convert_fusion.1), channel_id=1, source_target_pairs={{0,4},{1,5},{2,6},{3,7},{4,0},{5,1},{6,2},{7,3},{8,12},{9,13},{10,... | collective-permute-start | bytes 147464 | tf_op jit(solution)/shard_map/ppermute | solution.py:583
  30.4 4.8 %collective-permute-start.10 = (f32[24,512]{1,0:T(8,128)S(1)}, f32[24,512]{1,0:T(8,128)S(1)}, u32[]{:S(2)}, u32[]{:S(2)}) collective-permute-start(f32[24,512]{1,0:T(8,128)S(1)} %shard_map.116.gh), channel_id=1, source_target_pairs={{0,1},{1,0},{2,3},{3,2},{4,5},{5,4},{6,7},{7,6},{8,9},{9,8},{10,11... | collective-permute-start | bytes 147464 | tf_op jit(solution)/shard_map/ppermute | solution.py:482
  30.5 6.4 %collective-permute-start.11 = (f32[24,512]{1,0:T(8,128)S(1)}, f32[24,512]{1,0:T(8,128)S(1)}, u32[]{:S(2)}, u32[]{:S(2)}) collective-permute-start(f32[24,512]{1,0:T(8,128)S(1)} %shard_map.116.gh), channel_id=1, source_target_pairs={{0,15},{1,2},{2,1},{3,4},{4,3},{5,6},{6,5},{7,8},{8,7},{9,10},{10,... | collective-permute-start | bytes 147464 | tf_op jit(solution)/shard_map/ppermute | solution.py:481
  33.9 5.3 %collective-permute-start.9 = (bf16[192,128]{1,0:T(8,128)(2,1)S(1)}, bf16[192,128]{1,0:T(8,128)(2,1)S(1)}, u32[]{:S(2)}, u32[]{:S(2)}) collective-permute-start(bf16[192,128]{1,0:T(8,128)(2,1)S(1)} %add_convert_fusion), channel_id=1, source_target_pairs={{0,8},{1,9},{2,10},{3,11},{4,12},{5,13},{6,14},{7,15},{8,0},{9,1},... | collective-permute-start | bytes 147464 | tf_op jit(solution)/shard_map/ppermute | solution.py:583
  39.2 1.4 %collective-permute-start.12 = (f32[192,128]{1,0:T(8,128)S(1)}, f32[192,128]{1,0:T(8,128)S(1)}, u32[]{:S(2)}, u32[]{:S(2)}) collective-permute-start(f32[192,128]{1,0:T(8,128)S(1)} %convert_add_fusion.mine), channel_id=1, source_target_pairs={{0,1},{1,0},{2,3},{3,2},{4,5},{5,4},{6,7},{7,6},{8,9},{9,8},{10,11... | collective-permute-start | bytes 294920 | tf_op jit(solution)/shard_map/ppermute | solution.py:588

commit v4 on v3

--- a/solution.py
+++ b/solution.py
@@ -250,15 +250,9 @@
         t_ref[r0:r1, c0:c1] = value
 
 
-def gather_kernel(
-    axis, takes, rows, ch, base, step, with_d4,
-    pre_hbm, states, cot, out_a, out_b, sems, u, g,
-):
+def gather_kernel(axis, takes, rows, ch, base, step, late, pre_hbm, more, out_a, out_b, sems, buf):
     even = lax.rem(lax.axis_index(axis), 2) == 0
-    copies = [pltpu.make_async_copy(states.at[step], u, sems.at[0])]
-    if with_d4:
-        copies.append(pltpu.make_async_copy(cot, g, sems.at[1]))
-    first = len(copies)
+    copies = [pltpu.make_async_copy(more, buf, sems.at[0])]
     for layer, count, dst in takes:
         low, high = 0, (rows - count) * ch
         for out, start in (
@@ -274,15 +268,15 @@
             )
     for copy in copies:
         copy.start()
-    for copy in copies[:first]:
-        copy.wait()
-    planes = [split_terms(u[comp]) for comp in range(2)]
-    if with_d4:
-        planes.append(jnp.concatenate([g[0], g[1]], axis=0).astype(BF16))
+    copies[0].wait()
+    if late:
+        planes = [split_terms(buf[k, comp]) for k in range(2) for comp in range(2)]
+    else:
+        planes = [jnp.concatenate([buf[0], buf[1]], axis=0).astype(BF16)]
     for i, plane in enumerate(planes):
         for out in (out_a, out_b):
             out[base + 2 * rows * i : base + 2 * rows * (i + 1), :] = plane
-    for copy in copies[first:]:
+    for copy in copies[1:]:
         copy.wait()
 
 
@@ -360,14 +354,15 @@
 
 
 def border_states(states, step, m_a, m_b, rows, ch, even):
-    a = border_planes(m_a, sum(BORDERS) * ch, rows, 2)
-    b = border_planes(m_b, sum(BORDERS) * ch, rows, 2)
+    first = sum(BORDERS) * ch + 4 * rows * step
+    a = border_planes(m_a, first, rows, 2)
+    b = border_planes(m_b, first, rows, 2)
     return [joined(a[comp], states[step, comp], b[comp], even) for comp in range(2)]
 
 
 def back_kernel(axis, rows, ch, cot, pre, m_a, m_b, w4, w3, w2, w1, gh, x4, d3, d2, d1):
     even = lax.rem(lax.axis_index(axis), 2) == 0
-    base = sum(BORDERS) * ch + 4 * rows
+    base = sum(BORDERS) * ch
     a, b = (m[base : base + 2 * rows, :].astype(F32) for m in (m_a, m_b))
     planes = [
         joined(
@@ -380,19 +375,24 @@
     partial_input(w1, d1, lambda comp, i: cot[comp, i : i + 1, :], gh, rows, ch)
 
 
-def term_kernel(axis, rows, ch, x4, d3, d2, d1, pre, states, m_a, m_b, t_out, u_out, x0s):
+def term_kernel(
+    axis, rows, ch,
+    x4, d3, d2, d1, pre, states, m_a, m_b,
+    t_out, u1, u0, x0s, x1s,
+):
     even = lax.rem(lax.axis_index(axis), 2) == 0
-    u = border_states(states, 1, m_a, m_b, rows, ch, even)
-    for comp in range(2):
-        u_out[comp] = u[comp]
-    fill_small(x0s, half_step(*u), rows + 2, rows - 1, -1)
-    pack_terms(t_out, weight_terms(x4, d3, d2, d1, pre.at[0], x0s, rows, ch), ch)
+    for step, out, small in ((1, u1, x1s), (0, u0, x0s)):
+        u = border_states(states, step, m_a, m_b, rows, ch, even)
+        for comp in range(2):
+            out[comp] = u[comp]
+        fill_small(small, half_step(*u), rows + 2, rows - 1, -1)
+    pack_terms(t_out, weight_terms(x4, d3, d2, d1, pre.at[0], x1s, rows, ch), ch)
 
 
 def front_kernel(
     axis, rows, ch,
-    gh, gh_a, gh_b, u1, states, pre, m_a, m_b, w4, w3, w2, before,
-    keep, give, g_out, u_out, d1, x4, d3, d2, x0s, total, lam,
+    gh, gh_a, gh_b, u1, x0s, pre, m_a, m_b, w4, w3, w2, before,
+    keep, give, g_out, d1, x4, d3, d2, total, lam,
 ):
     even = lax.rem(lax.axis_index(axis), 2) == 0
     whole_input(gh, gh_a, gh_b, lam, rows, even)
@@ -400,10 +400,6 @@
     for comp in range(2):
         g_out[comp] = planes[comp][rows : 2 * rows]
     fill_small(x4, planes, 3 * rows, 0, 1)
-    u = border_states(states, 0, m_a, m_b, rows, ch, even)
-    for comp in range(2):
-        u_out[comp] = u[comp]
-    fill_small(x0s, half_step(*u), rows + 2, rows - 1, -1)
     chain(x4, pre.at[0], m_a, m_b, even, w4, w3, w2, d3, d2, d1, rows, ch)
     pack_terms(total, weight_terms(x4, d3, d2, d1, pre.at[0], x0s, rows, ch), ch, before)
     half = total.shape[0] // 2
@@ -485,7 +481,7 @@
     def shape(*dims, dtype=F32):
         return jax.ShapeDtypeStruct(dims, dtype)
 
-    def borders(step, with_d4, room):
+    def borders(step, late, room):
         takes, total = [], 0
         for layer, border in zip((2, 1, 0), BORDERS):
             if not border:
@@ -493,21 +489,24 @@
             takes.append((layer, border, total))
             total += border
         base = total * ch
-        out = shape(base + (6 if with_d4 else 4) * rows, width, dtype=BF16)
+        more = states if late else cotangent
+        out = shape(base + 2 * rows * (4 if late else 1), width, dtype=BF16)
         pack = pl.pallas_call(
-            functools.partial(gather_kernel, axis, takes, rows, ch, base, step, with_d4),
+            functools.partial(gather_kernel, axis, takes, rows, ch, base, step, late),
             out_shape=[out, out],
-            in_specs=[pl.BlockSpec(memory_space=pltpu.HBM)] * 3,
+            in_specs=[pl.BlockSpec(memory_space=pltpu.HBM)] * 2,
             out_specs=[VMEM, VMEM],
-            scratch_shapes=[pltpu.SemaphoreType.DMA((2 * len(takes) + 2,))]
-            + [pltpu.VMEM((2, rows, width), F32)] * 2,
+            scratch_shapes=[
+                pltpu.SemaphoreType.DMA((2 * len(takes) + 1,)),
+                pltpu.VMEM(more.shape, F32),
+            ],
             compiler_params=pltpu.CompilerParams(vmem_limit_bytes=VMEM_BYTES - room),
         )
-        a, b = pack(flat, states, cotangent)
+        a, b = pack(flat, more)
         return swap(a, b)
 
-    m1_a, m1_b = borders(1, True, 3 << 20)
-    m0_a, m0_b = borders(0, False, 56 << 20)
+    m1_a, m1_b = borders(1, False, 3 << 20)
+    m0_a, m0_b = borders(0, True, 56 << 20)
 
     def bands(n, m):
         return shape(n, m, dtype=BF16)
@@ -553,18 +552,18 @@
         {1: pre_spec(1)},
     )
     gh_a, gh_b = swap(gh, gh)
-    before, u1 = call(
+    before, u1, u0, x0s = call(
         functools.partial(term_kernel, axis, rows, ch),
-        [total, planes],
+        [total, planes, planes, x0_shape],
         scratch(x0_shape),
-        (x4, d3, d2, d1, pre_acts, states, m1_a, m1_b),
+        (x4, d3, d2, d1, pre_acts, states, m0_a, m0_b),
         {4: pre_spec(1)},
     )
-    keep, give, g, u0, d1 = call(
+    keep, give, g, d1 = call(
         functools.partial(front_kernel, axis, rows, ch),
-        [half, half, shape(2, rows, width), planes, d_shapes[2]],
-        scratch(x4_shape, d_shapes[0], d_shapes[1], x0_shape, total, planes),
-        (gh, gh_a, gh_b, u1, states, pre_acts, m0_a, m0_b, w4, w3, w2, before),
+        [half, half, shape(2, rows, width), d_shapes[2]],
+        scratch(x4_shape, d_shapes[0], d_shapes[1], total, planes),
+        (gh, gh_a, gh_b, u1, x0s, pre_acts, m0_a, m0_b, w4, w3, w2, before),
         {5: pre_spec(0)},
     )
     gh0 = call(functools.partial(input_kernel, rows, ch), part, [], (g, d1, w1))
@@ -580,11 +579,16 @@
     bit = 2
     while bit < count:
         mine = mine.astype(BF16)
-        got = lax.ppermute(mine, axis, [(i, i ^ bit) for i in range(count)])
-        if 2 * bit >= count:
+        steps = (bit, 2 * bit, 3 * bit) if 2 * bit < count else (bit,)
+        got = []
+        for b in steps:
+            got.append(lax.ppermute(mine, axis, [(i, i ^ b) for i in range(count)]))
+        bit *= len(steps) + 1
+        if bit >= count:
             got, adjoint = lax.optimization_barrier((got, adjoint))
-        mine = mine.astype(F32) + got.astype(F32)
-        bit *= 2
+        terms = [t.astype(F32) for t in [mine] + got]
+        sums = [a + b for a, b in zip(terms[::2], terms[1::2])]
+        mine = sums[0] if len(sums) == 1 else sums[0] + sums[1]
     other = lax.ppermute(mine, axis, pair_a)
     factor = 1.0 / math.sqrt(rows * count * width)
     g1, g2, g3, g4 = call(

time: 41.7 us -> 39.8 us (0.954)
  waiting for transfers between devices: 11.8 us -> 6.58 us
  starting transfers between devices: 18.2 us -> 20.7 us
  local copies, waits for them, and re-layouts: 0.04 us -> 0.87 us
    ppermute x3 -> x4, waiting for transfers between devices: 5.03 us -> 2.19 us  [on_device(): got.append(lax.ppermute(mine, axis, [(i, i ^ b) for i in range(count)]))]
    ppermute x3 -> x4, starting transfers between devices: 3.01 us -> 5.21 us  [on_device(): got.append(lax.ppermute(mine, axis, [(i, i ^ b) for i in range(count)]))]
    ppermute x4, waiting for transfers between devices: 4.19 us -> 2.01 us  [swap(): b = lax.ppermute(for_b, axis, pair_b)]
    unnamed x14 -> x16, local copies, waits for them, and re-layouts: 0.04 us -> 0.87 us
    ppermute x4, starting transfers between devices: 13.8 us -> 14.5 us  [swap(): b = lax.ppermute(for_b, axis, pair_b)]
    ppermute x4, starting transfers between devices: 1.23 us -> 0.63 us  [swap(): a = lax.ppermute(for_a, axis, pair_a)]
  transfers between devices with their start and end apart: 13 -> 14, of which waited for: 7 -> 7; matrix products, arithmetic and copies ran while one was open for 0% -> 0% of each run, Pallas kernels for 12% -> 13%
where the time goes in v4:
time: 39.8 us; the launch traced here: 39.6 us
  starting transfers between devices  20.7 us (52%)
  Pallas kernels  10.6 us (27%)
  waiting for transfers between devices  6.58 us (17%)
  local copies, waits for them, and re-layouts  0.87 us (2%)
  between operations  0.78 us (2%)
    ppermute x4, starting transfers between devices, swap(): b = lax.ppermute(for_b, axis, pair_b)  14.5 us
    pallas_call x7, Pallas kernels, call(): pl.pallas_call(kernel, out_shape=outs, grid=(1,) if specs else (), in_spe...  8.17 us
    ppermute x4, starting transfers between devices, on_device(): got.append(lax.ppermute(mine, axis, [(i, i ^ b) for i in range(count)]))  5.21 us
    pallas_call x2, Pallas kernels, borders(): a, b = pack(flat, more)  2.4 us
    ppermute x4, waiting for transfers between devices, on_device(): got.append(lax.ppermute(mine, axis, [(i, i ^ b) for i in range(count)]))  2.19 us
    ppermute x4, waiting for transfers between devices, swap(): b = lax.ppermute(for_b, axis, pair_b)  2.01 us
    ppermute x1, waiting for transfers between devices, on_device(): other = lax.ppermute(mine, axis, pair_a)  1.29 us
    ppermute x1, waiting for transfers between devices, on_device(): mine = keep + lax.ppermute(give, axis, pair_a)  1.08 us
  transfers between devices with their start and end apart: 14, of which 7 were waited for; matrix products, arithmetic and copies ran while one was open for 0% of the time, Pallas kernels for 13%

profile of v4, /device:TPU:0, one launch (start us, length us, event | category | flops | bytes accessed | tf_op | source)
XLA Modules:
  0.0 39.6 jit_solution(11453021941960525063)
XLA Ops:
  0.6 0.0 copy-start
  0.6 0.0 copy-start.6
  0.7 0.0 copy-start.3
  0.7 1.9 %shard_map.110 = (bf16[160,512]{1,0:T(8,128)(2,1)}, bf16[160,512]{1,0:T(8,128)(2,1)}) custom-call(bf16[2,3,384,512]{3,2,1,0:T(8,128)(2,1)} %bitcast.3, f32[2,8,512]{2,1,0:T(8,128)} %cot.1), custom_call_target="tpu_custom_call" | custom-call | tf_op jit(solution)/shard_map/pallas_call | solution.py:505
  2.5 0.6 %collective-permute-start = (bf16[160,512]{1,0:T(8,128)(2,1)}, bf16[160,512]{1,0:T(8,128)(2,1)S(1)}, u32[]{:S(2)}, u32[]{:S(2)}) collective-permute-start(bf16[160,512]{1,0:T(8,128)(2,1)} %get-tuple-element.32), channel_id=1, source_target_pairs={{0,1},{1,0},{2,3},{3,2},{4,5},{5,4},{6,7},{7,6},{8,9},{9,8},{10,11... | collective-permute-start | bytes 491528 | tf_op jit(solution)/shard_map/ppermute | solution.py:478
  3.1 5.6 %collective-permute-start.1 = (bf16[160,512]{1,0:T(8,128)(2,1)}, bf16[160,512]{1,0:T(8,128)(2,1)S(1)}, u32[]{:S(2)}, u32[]{:S(2)}) collective-permute-start(bf16[160,512]{1,0:T(8,128)(2,1)} %get-tuple-element.33), channel_id=1, source_target_pairs={{0,15},{1,2},{2,1},{3,4},{4,3},{5,6},{6,5},{7,8},{8,7},{9,10},{10,... | collective-permute-start | bytes 491528 | tf_op jit(solution)/shard_map/ppermute | solution.py:477
  8.7 0.0 copy-done
  8.7 0.0 copy-start.1
  8.7 0.8 %copy-done.1 = f32[2,2,8,512]{3,2,1,0:T(8,128)S(1)} copy-done((f32[2,2,8,512]{3,2,1,0:T(8,128)S(1)}, f32[2,2,8,512]{3,2,1,0:T(8,128)}, u32[]{:S(2)}) %copy-start.1) | copy-done | bytes 65560
  9.6 0.0 copy-start.4
  9.6 0.0 copy-start.5
  9.6 0.0 copy-start.7
  9.6 0.5 %shard_map.113 = (bf16[208,512]{1,0:T(8,128)(2,1)S(1)}, bf16[208,512]{1,0:T(8,128)(2,1)S(1)}) custom-call(bf16[2,3,384,512]{3,2,1,0:T(8,128)(2,1)S(1)} %bitcast.4, f32[2,2,8,512]{3,2,1,0:T(8,128)S(1)} %copy-done.1), custom_call_target="tpu_custom_call" | custom-call | tf_op jit(solution)/shard_map/pallas_call | solution.py:505
  10.1 0.1 collective-permute-start.4
  10.2 0.6 %collective-permute-start.5 = (bf16[208,512]{1,0:T(8,128)(2,1)S(1)}, bf16[208,512]{1,0:T(8,128)(2,1)S(1)}, u32[]{:S(2)}, u32[]{:S(2)}) collective-permute-start(bf16[208,512]{1,0:T(8,128)(2,1)S(1)} %get-tuple-element.44), channel_id=1, source_target_pairs={{0,15},{1,2},{2,1},{3,4},{4,3},{5,6},{6,5},{7,8},{8,7},{9,10},{10,... | collective-permute-start | bytes 638984 | tf_op jit(solution)/shard_map/ppermute | solution.py:477
  10.8 0.0 copy-done.6
  10.8 0.0 copy-done.4
  10.8 0.0 copy-done.5
  10.8 0.0 copy-done.7
  10.8 0.0 copy-start.2
  10.9 0.4 shard_map.111
  11.2 0.0 collective-permute-done.m_a
  11.2 0.7 %collective-permute-done.1.m_b = bf16[160,512]{1,0:T(8,128)(2,1)S(1)} collective-permute-done((bf16[160,512]{1,0:T(8,128)(2,1)}, bf16[160,512]{1,0:T(8,128)(2,1)S(1)}, u32[]{:S(2)}, u32[]{:S(2)}) %collective-permute-start.1) | collective-permute-done | bytes 163872 | tf_op jit(solution)/shard_map/ppermute | solution.py:477
  11.9 0.0 copy-done.3
  11.9 1.7 %shard_map.112 = (f32[24,512]{1,0:T(8,128)S(1)}, f32[192,512]{1,0:T(8,128)S(1)}, bf16[3,576,512]{2,1,0:T(8,128)(2,1)S(1)}, bf16[3,480,512]{2,1,0:T(8,128)(2,1)S(1)}, bf16[576,512]{1,0:T(8,128)(2,1)S(1)}) custom-call(f32[2,8,512]{2,1,0:T(8,128)S(1)} %copy-done.3, bf16[2,3,8,48,512]{4,3,2,1,0:T(8,128)(2,1)S(1)} %copy-done, ...), custom_call_target="tpu_custom_call" | custom-call | flops 100000000 | bytes 2000000 | tf_op jit(solution)/shard_map/pallas_call | solution.py:452
  13.6 4.6 %collective-permute-start.3 = (f32[24,512]{1,0:T(8,128)S(1)}, f32[24,512]{1,0:T(8,128)S(1)}, u32[]{:S(2)}, u32[]{:S(2)}) collective-permute-start(f32[24,512]{1,0:T(8,128)S(1)} %get-tuple-element.38.gh), channel_id=1, source_target_pairs={{0,15},{1,2},{2,1},{3,4},{4,3},{5,6},{6,5},{7,8},{8,7},{9,10},{10,... | collective-permute-start | bytes 147464 | tf_op jit(solution)/shard_map/ppermute | solution.py:477
  18.2 0.0 collective-permute-start.2
  18.2 0.0 collective-permute-done.4.m_a
  18.2 0.1 collective-permute-done.5.m_b
  18.3 0.0 copy-done.2
  18.3 1.5 %shard_map.114 = (f32[384,128]{1,0:T(8,128)S(1)}, f32[2,24,512]{2,1,0:T(8,128)S(1)}, f32[2,24,512]{2,1,0:T(8,128)S(1)}, f32[80,512]{1,0:T(8,128)S(1)}) custom-call(f32[192,512]{1,0:T(8,128)S(1)} %get-tuple-element.39.x4, bf16[3,576,512]{2,1,0:T(8,128)(2,1)S(1)} %get-tuple-element.40.d3, bf16[3,480,512]{2,1,0:T(8,128)(2,1)S(1)} %get-tuple-element.41.d2, ...), custom_call_target="tpu_custom_call" | custom-call | flops 100000000 | bytes 2000000 | tf_op jit(solution)/shard_map/pallas_call | solution.py:452
  19.8 0.2 collective-permute-done.3.gh_b
  20.0 0.0 collective-permute-done.2.gh_a
  20.0 2.6 %shard_map.115 = (f32[192,128]{1,0:T(8,128)S(1)}, f32[192,128]{1,0:T(8,128)S(1)}, f32[2,8,512]{2,1,0:T(8,128)S(1)}, bf16[576,512]{1,0:T(8,128)(2,1)S(1)}) custom-call(f32[24,512]{1,0:T(8,128)S(1)} %get-tuple-element.38.gh, f32[24,512]{1,0:T(8,128)S(1)} %collective-permute-done.2.gh_a, f32[24,512]{1,0:T(8,128)S(1)} %collective-permute-done.3.gh_b, ...), custom_call_target="tpu_custom_call" | custom-call | flops 100000000 | bytes 2000000 | tf_op jit(solution)/shard_map/pallas_call | solution.py:452
  22.6 0.3 collective-permute-start.6
  22.9 1.1 %collective-permute-done.6 = f32[192,128]{1,0:T(8,128)S(1)} collective-permute-done((f32[192,128]{1,0:T(8,128)S(1)}, f32[192,128]{1,0:T(8,128)S(1)}, u32[]{:S(2)}, u32[]{:S(2)}) %collective-permute-start.6) | collective-permute-done | bytes 98336 | tf_op jit(solution)/shard_map/ppermute | solution.py:578
  24.0 0.1 collective-permute-start.9
  24.1 0.4 collective-permute-start.8
  24.4 3.1 %collective-permute-start.7 = (bf16[192,128]{1,0:T(8,128)(2,1)S(1)}, bf16[192,128]{1,0:T(8,128)(2,1)S(1)}, u32[]{:S(2)}, u32[]{:S(2)}) collective-permute-start(bf16[192,128]{1,0:T(8,128)(2,1)S(1)} %add_convert_fusion.1), channel_id=1, source_target_pairs={{0,2},{1,3},{2,0},{3,1},{4,6},{5,7},{6,4},{7,5},{8,10},{9,11},{10,... | collective-permute-start | bytes 147464 | tf_op jit(solution)/shard_map/ppermute | solution.py:585
  27.5 0.3 shard_map.116.gh
  27.9 3.7 %collective-permute-start.12 = (f32[24,512]{1,0:T(8,128)S(1)}, f32[24,512]{1,0:T(8,128)S(1)}, u32[]{:S(2)}, u32[]{:S(2)}) collective-permute-start(f32[24,512]{1,0:T(8,128)S(1)} %shard_map.116.gh), channel_id=1, source_target_pairs={{0,15},{1,2},{2,1},{3,4},{4,3},{5,6},{6,5},{7,8},{8,7},{9,10},{10,... | collective-permute-start | bytes 147464 | tf_op jit(solution)/shard_map/ppermute | solution.py:477
  31.5 0.0 collective-permute-start.11
  31.5 0.0 collective-permute-done.9
  31.6 0.0 collective-permute-done.8
  31.6 0.0 collective-permute-done.7
  31.6 1.7 %collective-permute-start.10 = (bf16[192,128]{1,0:T(8,128)(2,1)S(1)}, bf16[192,128]{1,0:T(8,128)(2,1)S(1)}, u32[]{:S(2)}, u32[]{:S(2)}) collective-permute-start(bf16[192,128]{1,0:T(8,128)(2,1)S(1)} %add_convert_fusion), channel_id=1, source_target_pairs={{0,8},{1,9},{2,10},{3,11},{4,12},{5,13},{6,14},{7,15},{8,0},{9,1},... | collective-permute-start | bytes 147464 | tf_op jit(solution)/shard_map/ppermute | solution.py:585
  33.3 1.0 %collective-permute-done.12.gh_b = f32[24,512]{1,0:T(8,128)S(1)} collective-permute-done((f32[24,512]{1,0:T(8,128)S(1)}, f32[24,512]{1,0:T(8,128)S(1)}, u32[]{:S(2)}, u32[]{:S(2)}) %collective-permute-start.12) | collective-permute-done | bytes 49184 | tf_op jit(solution)/shard_map/ppermute | solution.py:477
  34.3 0.0 collective-permute-done.11.gh_a
  34.3 0.8 %shard_map.117 = f32[2,8,512]{2,1,0:T(8,128)} custom-call(f32[24,512]{1,0:T(8,128)S(1)} %shard_map.116.gh, f32[24,512]{1,0:T(8,128)S(1)} %collective-permute-done.11.gh_a, f32[24,512]{1,0:T(8,128)S(1)} %collective-permute-done.12.gh_b, f32[2,24,512]{2,1,0:T(8,128)S(1)} %get-tuple-element.52.u), custom_call_target="tpu_custom_call" | custom-call | flops 100000000 | bytes 2000000 | tf_op jit(solution)/shard_map/pallas_call | solution.py:452
  35.1 2.2 %collective-permute-done.10 = bf16[192,128]{1,0:T(8,128)(2,1)S(1)} collective-permute-done((bf16[192,128]{1,0:T(8,128)(2,1)S(1)}, bf16[192,128]{1,0:T(8,128)(2,1)S(1)}, u32[]{:S(2)}, u32[]{:S(2)}) %collective-permute-start.10) | collective-permute-done | bytes 49184 | tf_op jit(solution)/shard_map/ppermute | solution.py:585
  37.3 0.1 collective-permute-start.13
  37.3 1.3 %collective-permute-done.13.other = f32[192,128]{1,0:T(8,128)S(1)} collective-permute-done((f32[192,128]{1,0:T(8,128)S(1)}, f32[192,128]{1,0:T(8,128)S(1)}, u32[]{:S(2)}, u32[]{:S(2)}) %collective-permute-start.13) | collective-permute-done | bytes 98336 | tf_op jit(solution)/shard_map/ppermute | solution.py:592
  38.6 1.0 %shard_map.118 = (f32[9,2,48]{2,1,0:T(2,128)}, f32[9,48,48]{2,1,0:T(8,128)}, f32[9,48,48]{2,1,0:T(8,128)}, f32[9,2,48]{2,1,0:T(2,128)}) custom-call(f32[192,128]{1,0:T(8,128)S(1)} %convert_add_fusion.mine, f32[192,128]{1,0:T(8,128)S(1)} %collective-permute-done.13.other), custom_call_target="tpu_custom_call" | custom-call | flops 100000000 | bytes 2000000 | tf_op jit(solution)/shard_map/pallas_call | solution.py:452
  (3 shorter events, 0.1 us)
Async XLA Ops:
  0.6 8.1 %copy-start = (bf16[2,3,8,48,512]{4,3,2,1,0:T(8,128)(2,1)S(1)}, bf16[2,3,8,48,512]{4,3,2,1,0:T(8,128)(2,1)}, u32[]{:S(2)}) copy-start(bf16[2,3,8,48,512]{4,3,2,1,0:T(8,128)(2,1)} %pre.5) | copy-start | bytes 7077892
  0.6 10.2 %copy-start.6 = (bf16[9,48,2]{1,2,0:T(2,128)(2,1)S(1)}, bf16[9,48,2]{1,2,0:T(2,128)(2,1)}, u32[]{:S(2)}) copy-start(bf16[9,48,2]{1,2,0:T(2,128)(2,1)} %param.10) | copy-start | bytes 5188
  0.7 11.3 %copy-start.3 = (f32[2,8,512]{2,1,0:T(8,128)S(1)}, f32[2,8,512]{2,1,0:T(8,128)}, u32[]{:S(2)}) copy-start(f32[2,8,512]{2,1,0:T(8,128)} %cot.1) | copy-start | bytes 98308
  2.5 8.7 %collective-permute-start = (bf16[160,512]{1,0:T(8,128)(2,1)}, bf16[160,512]{1,0:T(8,128)(2,1)S(1)}, u32[]{:S(2)}, u32[]{:S(2)}) collective-permute-start(bf16[160,512]{1,0:T(8,128)(2,1)} %get-tuple-element.32), channel_id=1, source_target_pairs={{0,1},{1,0},{2,3},{3,2},{4,5},{5,4},{6,7},{7,6},{8,9},{9,8},{10,11... | collective-permute-start | bytes 491528 | tf_op jit(solution)/shard_map/ppermute | solution.py:478
  3.1 8.8 %collective-permute-start.1 = (bf16[160,512]{1,0:T(8,128)(2,1)}, bf16[160,512]{1,0:T(8,128)(2,1)S(1)}, u32[]{:S(2)}, u32[]{:S(2)}) collective-permute-start(bf16[160,512]{1,0:T(8,128)(2,1)} %get-tuple-element.33), channel_id=1, source_target_pairs={{0,15},{1,2},{2,1},{3,4},{4,3},{5,6},{6,5},{7,8},{8,7},{9,10},{10,... | collective-permute-start | bytes 491528 | tf_op jit(solution)/shard_map/ppermute | solution.py:477
  8.7 0.8 %copy-start.1 = (f32[2,2,8,512]{3,2,1,0:T(8,128)S(1)}, f32[2,2,8,512]{3,2,1,0:T(8,128)}, u32[]{:S(2)}) copy-start(f32[2,2,8,512]{3,2,1,0:T(8,128)} %states.1) | copy-start | bytes 196612
  9.6 1.3 %copy-start.4 = (bf16[9,48,48]{2,1,0:T(8,128)(2,1)S(1)}, bf16[9,48,48]{2,1,0:T(8,128)(2,1)}, u32[]{:S(2)}) copy-start(bf16[9,48,48]{2,1,0:T(8,128)(2,1)} %w2.1) | copy-start | bytes 124420
  9.6 1.3 %copy-start.5 = (bf16[9,48,48]{2,1,0:T(8,128)(2,1)S(1)}, bf16[9,48,48]{2,1,0:T(8,128)(2,1)}, u32[]{:S(2)}) copy-start(bf16[9,48,48]{2,1,0:T(8,128)(2,1)} %w3.1) | copy-start | bytes 124420
  9.6 1.3 %copy-start.7 = (bf16[9,2,48]{2,1,0:T(2,128)(2,1)S(1)}, bf16[9,2,48]{2,1,0:T(2,128)(2,1)}, u32[]{:S(2)}) copy-start(bf16[9,2,48]{2,1,0:T(2,128)(2,1)} %w4.1) | copy-start | bytes 5188
  10.1 8.1 %collective-permute-start.4 = (bf16[208,512]{1,0:T(8,128)(2,1)S(1)}, bf16[208,512]{1,0:T(8,128)(2,1)S(1)}, u32[]{:S(2)}, u32[]{:S(2)}) collective-permute-start(bf16[208,512]{1,0:T(8,128)(2,1)S(1)} %get-tuple-element.43), channel_id=1, source_target_pairs={{0,1},{1,0},{2,3},{3,2},{4,5},{5,4},{6,7},{7,6},{8,9},{9,8},{10,11... | collective-permute-start | bytes 638984 | tf_op jit(solution)/shard_map/ppermute | solution.py:478
  10.2 8.1 %collective-permute-start.5 = (bf16[208,512]{1,0:T(8,128)(2,1)S(1)}, bf16[208,512]{1,0:T(8,128)(2,1)S(1)}, u32[]{:S(2)}, u32[]{:S(2)}) collective-permute-start(bf16[208,512]{1,0:T(8,128)(2,1)S(1)} %get-tuple-element.44), channel_id=1, source_target_pairs={{0,15},{1,2},{2,1},{3,4},{4,3},{5,6},{6,5},{7,8},{8,7},{9,10},{10,... | collective-permute-start | bytes 638984 | tf_op jit(solution)/shard_map/ppermute | solution.py:477
  10.8 7.5 %copy-start.2 = (f32[2,2,8,512]{3,2,1,0:T(8,128)S(1)}, f32[2,2,8,512]{3,2,1,0:T(8,128)}, u32[]{:S(2)}) copy-start(f32[2,2,8,512]{3,2,1,0:T(8,128)} %states.1) | copy-start | bytes 196612
  13.6 6.4 %collective-permute-start.3 = (f32[24,512]{1,0:T(8,128)S(1)}, f32[24,512]{1,0:T(8,128)S(1)}, u32[]{:S(2)}, u32[]{:S(2)}) collective-permute-start(f32[24,512]{1,0:T(8,128)S(1)} %get-tuple-element.38.gh), channel_id=1, source_target_pairs={{0,15},{1,2},{2,1},{3,4},{4,3},{5,6},{6,5},{7,8},{8,7},{9,10},{10,... | collective-permute-start | bytes 147464 | tf_op jit(solution)/shard_map/ppermute | solution.py:477
  18.2 1.8 %collective-permute-start.2 = (f32[24,512]{1,0:T(8,128)S(1)}, f32[24,512]{1,0:T(8,128)S(1)}, u32[]{:S(2)}, u32[]{:S(2)}) collective-permute-start(f32[24,512]{1,0:T(8,128)S(1)} %get-tuple-element.38.gh), channel_id=1, source_target_pairs={{0,1},{1,0},{2,3},{3,2},{4,5},{5,4},{6,7},{7,6},{8,9},{9,8},{10,11... | collective-permute-start | bytes 147464 | tf_op jit(solution)/shard_map/ppermute | solution.py:478
  22.6 1.4 %collective-permute-start.6 = (f32[192,128]{1,0:T(8,128)S(1)}, f32[192,128]{1,0:T(8,128)S(1)}, u32[]{:S(2)}, u32[]{:S(2)}) collective-permute-start(f32[192,128]{1,0:T(8,128)S(1)} %get-tuple-element.49), channel_id=1, source_target_pairs={{0,1},{1,0},{2,3},{3,2},{4,5},{5,4},{6,7},{7,6},{8,9},{9,8},{10,11... | collective-permute-start | bytes 294920 | tf_op jit(solution)/shard_map/ppermute | solution.py:578
  24.0 7.6 %collective-permute-start.9 = (bf16[192,128]{1,0:T(8,128)(2,1)S(1)}, bf16[192,128]{1,0:T(8,128)(2,1)S(1)}, u32[]{:S(2)}, u32[]{:S(2)}) collective-permute-start(bf16[192,128]{1,0:T(8,128)(2,1)S(1)} %add_convert_fusion.1), channel_id=1, source_target_pairs={{0,6},{1,7},{2,4},{3,5},{4,2},{5,3},{6,0},{7,1},{8,14},{9,15},{10,... | collective-permute-start | bytes 147464 | tf_op jit(solution)/shard_map/ppermute | solution.py:585
  24.1 7.5 %collective-permute-start.8 = (bf16[192,128]{1,0:T(8,128)(2,1)S(1)}, bf16[192,128]{1,0:T(8,128)(2,1)S(1)}, u32[]{:S(2)}, u32[]{:S(2)}) collective-permute-start(bf16[192,128]{1,0:T(8,128)(2,1)S(1)} %add_convert_fusion.1), channel_id=1, source_target_pairs={{0,4},{1,5},{2,6},{3,7},{4,0},{5,1},{6,2},{7,3},{8,12},{9,13},{10,... | collective-permute-start | bytes 147464 | tf_op jit(solution)/shard_map/ppermute | solution.py:585
  24.4 7.1 %collective-permute-start.7 = (bf16[192,128]{1,0:T(8,128)(2,1)S(1)}, bf16[192,128]{1,0:T(8,128)(2,1)S(1)}, u32[]{:S(2)}, u32[]{:S(2)}) collective-permute-start(bf16[192,128]{1,0:T(8,128)(2,1)S(1)} %add_convert_fusion.1), channel_id=1, source_target_pairs={{0,2},{1,3},{2,0},{3,1},{4,6},{5,7},{6,4},{7,5},{8,10},{9,11},{10,... | collective-permute-start | bytes 147464 | tf_op jit(solution)/shard_map/ppermute | solution.py:585
  27.9 6.4 %collective-permute-start.12 = (f32[24,512]{1,0:T(8,128)S(1)}, f32[24,512]{1,0:T(8,128)S(1)}, u32[]{:S(2)}, u32[]{:S(2)}) collective-permute-start(f32[24,512]{1,0:T(8,128)S(1)} %shard_map.116.gh), channel_id=1, source_target_pairs={{0,15},{1,2},{2,1},{3,4},{4,3},{5,6},{6,5},{7,8},{8,7},{9,10},{10,... | collective-permute-start | bytes 147464 | tf_op jit(solution)/shard_map/ppermute | solution.py:477
  31.5 2.7 %collective-permute-start.11 = (f32[24,512]{1,0:T(8,128)S(1)}, f32[24,512]{1,0:T(8,128)S(1)}, u32[]{:S(2)}, u32[]{:S(2)}) collective-permute-start(f32[24,512]{1,0:T(8,128)S(1)} %shard_map.116.gh), channel_id=1, source_target_pairs={{0,1},{1,0},{2,3},{3,2},{4,5},{5,4},{6,7},{7,6},{8,9},{9,8},{10,11... | collective-permute-start | bytes 147464 | tf_op jit(solution)/shard_map/ppermute | solution.py:478
  31.6 5.6 %collective-permute-start.10 = (bf16[192,128]{1,0:T(8,128)(2,1)S(1)}, bf16[192,128]{1,0:T(8,128)(2,1)S(1)}, u32[]{:S(2)}, u32[]{:S(2)}) collective-permute-start(bf16[192,128]{1,0:T(8,128)(2,1)S(1)} %add_convert_fusion), channel_id=1, source_target_pairs={{0,8},{1,9},{2,10},{3,11},{4,12},{5,13},{6,14},{7,15},{8,0},{9,1},... | collective-permute-start | bytes 147464 | tf_op jit(solution)/shard_map/ppermute | solution.py:585
  37.3 1.4 %collective-permute-start.13 = (f32[192,128]{1,0:T(8,128)S(1)}, f32[192,128]{1,0:T(8,128)S(1)}, u32[]{:S(2)}, u32[]{:S(2)}) collective-permute-start(f32[192,128]{1,0:T(8,128)S(1)} %convert_add_fusion.mine), channel_id=1, source_target_pairs={{0,1},{1,0},{2,3},{3,2},{4,5},{5,4},{6,7},{7,6},{8,9},{9,8},{10,11... | collective-permute-start | bytes 294920 | tf_op jit(solution)/shard_map/ppermute | solution.py:592

commit v5 on v4

--- a/solution.py
+++ b/solution.py
@@ -405,7 +405,7 @@
     half = total.shape[0] // 2
     a, b = total[:half, :], total[half:, :]
     keep[...] = jnp.where(even, a, b)
-    give[...] = jnp.where(even, b, a)
+    give[...] = jnp.where(even, b, a).astype(BF16)
 
 
 def input_kernel(rows, ch, g, d1, w1, gh):
@@ -561,7 +561,7 @@
     )
     keep, give, g, d1 = call(
         functools.partial(front_kernel, axis, rows, ch),
-        [half, half, shape(2, rows, width), d_shapes[2]],
+        [half, shape(*half.shape, dtype=BF16), shape(2, rows, width), d_shapes[2]],
         scratch(x4_shape, d_shapes[0], d_shapes[1], total, planes),
         (gh, gh_a, gh_b, u1, x0s, pre_acts, m0_a, m0_b, w4, w3, w2, before),
         {5: pre_spec(0)},
@@ -575,7 +575,7 @@
         (gh0, gh0_a, gh0_b, u0),
     )
 
-    mine = keep + lax.ppermute(give, axis, pair_a)
+    mine = keep + lax.ppermute(give, axis, pair_a).astype(F32)
     bit = 2
     while bit < count:
         mine = mine.astype(BF16)

time: 39.8 us -> 39.7 us (level)
  no operation moved by 1% of the time
where the time goes in v5:
time: 39.7 us; the launch traced here: 39.5 us
  starting transfers between devices  20.7 us (52%)
  Pallas kernels  10.6 us (27%)
  waiting for transfers between devices  6.5 us (16%)
  local copies, waits for them, and re-layouts  0.87 us (2%)
  between operations  0.78 us (2%)
    ppermute x4, starting transfers between devices, swap(): b = lax.ppermute(for_b, axis, pair_b)  14.5 us
    pallas_call x7, Pallas kernels, call(): pl.pallas_call(kernel, out_shape=outs, grid=(1,) if specs else (), in_spe...  8.17 us
    ppermute x4, starting transfers between devices, on_device(): got.append(lax.ppermute(mine, axis, [(i, i ^ b) for i in range(count)]))  5.22 us
    pallas_call x2, Pallas kernels, borders(): a, b = pack(flat, more)  2.4 us
    ppermute x4, waiting for transfers between devices, on_device(): got.append(lax.ppermute(mine, axis, [(i, i ^ b) for i in range(count)]))  2.18 us
    ppermute x4, waiting for transfers between devices, swap(): b = lax.ppermute(for_b, axis, pair_b)  2.01 us
    ppermute x1, waiting for transfers between devices, on_device(): other = lax.ppermute(mine, axis, pair_a)  1.29 us
    ppermute x1, waiting for transfers between devices, on_device(): mine = keep + lax.ppermute(give, axis, pair_a).astype(F32)  1.01 us
  transfers between devices with their start and end apart: 14, of which 7 were waited for; matrix products, arithmetic and copies ran while one was open for 0% of the time, Pallas kernels for 13%

profile of v5, /device:TPU:0, one launch (start us, length us, event | category | flops | bytes accessed | tf_op | source)
XLA Modules:
  0.0 39.5 jit_solution(938099807151915190)
XLA Ops:
  0.6 0.0 copy-start
  0.6 0.0 copy-start.6
  0.7 0.0 copy-start.3
  0.7 1.9 %shard_map.110 = (bf16[160,512]{1,0:T(8,128)(2,1)}, bf16[160,512]{1,0:T(8,128)(2,1)}) custom-call(bf16[2,3,384,512]{3,2,1,0:T(8,128)(2,1)} %bitcast.3, f32[2,8,512]{2,1,0:T(8,128)} %cot.1), custom_call_target="tpu_custom_call" | custom-call | tf_op jit(solution)/shard_map/pallas_call | solution.py:505
  2.5 0.6 %collective-permute-start = (bf16[160,512]{1,0:T(8,128)(2,1)}, bf16[160,512]{1,0:T(8,128)(2,1)S(1)}, u32[]{:S(2)}, u32[]{:S(2)}) collective-permute-start(bf16[160,512]{1,0:T(8,128)(2,1)} %get-tuple-element.32), channel_id=1, source_target_pairs={{0,1},{1,0},{2,3},{3,2},{4,5},{5,4},{6,7},{7,6},{8,9},{9,8},{10,11... | collective-permute-start | bytes 491528 | tf_op jit(solution)/shard_map/ppermute | solution.py:478
  3.1 5.6 %collective-permute-start.1 = (bf16[160,512]{1,0:T(8,128)(2,1)}, bf16[160,512]{1,0:T(8,128)(2,1)S(1)}, u32[]{:S(2)}, u32[]{:S(2)}) collective-permute-start(bf16[160,512]{1,0:T(8,128)(2,1)} %get-tuple-element.33), channel_id=1, source_target_pairs={{0,15},{1,2},{2,1},{3,4},{4,3},{5,6},{6,5},{7,8},{8,7},{9,10},{10,... | collective-permute-start | bytes 491528 | tf_op jit(solution)/shard_map/ppermute | solution.py:477
  8.7 0.0 copy-done
  8.7 0.0 copy-start.1
  8.7 0.8 %copy-done.1 = f32[2,2,8,512]{3,2,1,0:T(8,128)S(1)} copy-done((f32[2,2,8,512]{3,2,1,0:T(8,128)S(1)}, f32[2,2,8,512]{3,2,1,0:T(8,128)}, u32[]{:S(2)}) %copy-start.1) | copy-done | bytes 65560
  9.6 0.0 copy-start.4
  9.6 0.0 copy-start.5
  9.6 0.0 copy-start.7
  9.6 0.5 %shard_map.113 = (bf16[208,512]{1,0:T(8,128)(2,1)S(1)}, bf16[208,512]{1,0:T(8,128)(2,1)S(1)}) custom-call(bf16[2,3,384,512]{3,2,1,0:T(8,128)(2,1)S(1)} %bitcast.4, f32[2,2,8,512]{3,2,1,0:T(8,128)S(1)} %copy-done.1), custom_call_target="tpu_custom_call" | custom-call | tf_op jit(solution)/shard_map/pallas_call | solution.py:505
  10.1 0.1 collective-permute-start.4
  10.2 0.6 %collective-permute-start.5 = (bf16[208,512]{1,0:T(8,128)(2,1)S(1)}, bf16[208,512]{1,0:T(8,128)(2,1)S(1)}, u32[]{:S(2)}, u32[]{:S(2)}) collective-permute-start(bf16[208,512]{1,0:T(8,128)(2,1)S(1)} %get-tuple-element.44), channel_id=1, source_target_pairs={{0,15},{1,2},{2,1},{3,4},{4,3},{5,6},{6,5},{7,8},{8,7},{9,10},{10,... | collective-permute-start | bytes 638984 | tf_op jit(solution)/shard_map/ppermute | solution.py:477
  10.8 0.0 copy-done.6
  10.8 0.0 copy-done.4
  10.8 0.0 copy-done.5
  10.8 0.0 copy-done.7
  10.8 0.0 copy-start.2
  10.9 0.4 shard_map.111
  11.2 0.0 collective-permute-done.m_a
  11.2 0.7 %collective-permute-done.1.m_b = bf16[160,512]{1,0:T(8,128)(2,1)S(1)} collective-permute-done((bf16[160,512]{1,0:T(8,128)(2,1)}, bf16[160,512]{1,0:T(8,128)(2,1)S(1)}, u32[]{:S(2)}, u32[]{:S(2)}) %collective-permute-start.1) | collective-permute-done | bytes 163872 | tf_op jit(solution)/shard_map/ppermute | solution.py:477
  11.9 0.0 copy-done.3
  11.9 1.7 %shard_map.112 = (f32[24,512]{1,0:T(8,128)S(1)}, f32[192,512]{1,0:T(8,128)S(1)}, bf16[3,576,512]{2,1,0:T(8,128)(2,1)S(1)}, bf16[3,480,512]{2,1,0:T(8,128)(2,1)S(1)}, bf16[576,512]{1,0:T(8,128)(2,1)S(1)}) custom-call(f32[2,8,512]{2,1,0:T(8,128)S(1)} %copy-done.3, bf16[2,3,8,48,512]{4,3,2,1,0:T(8,128)(2,1)S(1)} %copy-done, ...), custom_call_target="tpu_custom_call" | custom-call | flops 100000000 | bytes 2000000 | tf_op jit(solution)/shard_map/pallas_call | solution.py:452
  13.6 4.6 %collective-permute-start.3 = (f32[24,512]{1,0:T(8,128)S(1)}, f32[24,512]{1,0:T(8,128)S(1)}, u32[]{:S(2)}, u32[]{:S(2)}) collective-permute-start(f32[24,512]{1,0:T(8,128)S(1)} %get-tuple-element.38.gh), channel_id=1, source_target_pairs={{0,15},{1,2},{2,1},{3,4},{4,3},{5,6},{6,5},{7,8},{8,7},{9,10},{10,... | collective-permute-start | bytes 147464 | tf_op jit(solution)/shard_map/ppermute | solution.py:477
  18.2 0.0 collective-permute-start.2
  18.2 0.0 collective-permute-done.4.m_a
  18.2 0.1 collective-permute-done.5.m_b
  18.3 0.0 copy-done.2
  18.3 1.5 %shard_map.114 = (f32[384,128]{1,0:T(8,128)S(1)}, f32[2,24,512]{2,1,0:T(8,128)S(1)}, f32[2,24,512]{2,1,0:T(8,128)S(1)}, f32[80,512]{1,0:T(8,128)S(1)}) custom-call(f32[192,512]{1,0:T(8,128)S(1)} %get-tuple-element.39.x4, bf16[3,576,512]{2,1,0:T(8,128)(2,1)S(1)} %get-tuple-element.40.d3, bf16[3,480,512]{2,1,0:T(8,128)(2,1)S(1)} %get-tuple-element.41.d2, ...), custom_call_target="tpu_custom_call" | custom-call | flops 100000000 | bytes 2000000 | tf_op jit(solution)/shard_map/pallas_call | solution.py:452
  19.8 0.2 collective-permute-done.3.gh_b
  20.0 0.0 collective-permute-done.2.gh_a
  20.0 2.6 %shard_map.115 = (f32[192,128]{1,0:T(8,128)S(1)}, bf16[192,128]{1,0:T(8,128)(2,1)S(1)}, f32[2,8,512]{2,1,0:T(8,128)S(1)}, bf16[576,512]{1,0:T(8,128)(2,1)S(1)}) custom-call(f32[24,512]{1,0:T(8,128)S(1)} %get-tuple-element.38.gh, f32[24,512]{1,0:T(8,128)S(1)} %collective-permute-done.2.gh_a, f32[24,512]{1,0:T(8,128)S(1)} %collective-permute-done.3.gh_b, ...), custom_call_target="tpu_custom_call" | custom-call | flops 100000000 | bytes 2000000 | tf_op jit(solution)/shard_map/pallas_call | solution.py:452
  22.6 0.3 collective-permute-start.6
  22.9 1.0 %collective-permute-done.6 = bf16[192,128]{1,0:T(8,128)(2,1)S(1)} collective-permute-done((bf16[192,128]{1,0:T(8,128)(2,1)S(1)}, bf16[192,128]{1,0:T(8,128)(2,1)S(1)}, u32[]{:S(2)}, u32[]{:S(2)}) %collective-permute-start.6) | collective-permute-done | bytes 49184 | tf_op jit(solution)/shard_map/ppermute | solution.py:578
  23.9 0.1 collective-permute-start.9
  24.0 0.4 collective-permute-start.8
  24.4 3.1 %collective-permute-start.7 = (bf16[192,128]{1,0:T(8,128)(2,1)S(1)}, bf16[192,128]{1,0:T(8,128)(2,1)S(1)}, u32[]{:S(2)}, u32[]{:S(2)}) collective-permute-start(bf16[192,128]{1,0:T(8,128)(2,1)S(1)} %add_convert_fusion.1), channel_id=1, source_target_pairs={{0,2},{1,3},{2,0},{3,1},{4,6},{5,7},{6,4},{7,5},{8,10},{9,11},{10,... | collective-permute-start | bytes 147464 | tf_op jit(solution)/shard_map/ppermute | solution.py:585
  27.5 0.3 shard_map.116.gh
  27.8 3.7 %collective-permute-start.12 = (f32[24,512]{1,0:T(8,128)S(1)}, f32[24,512]{1,0:T(8,128)S(1)}, u32[]{:S(2)}, u32[]{:S(2)}) collective-permute-start(f32[24,512]{1,0:T(8,128)S(1)} %shard_map.116.gh), channel_id=1, source_target_pairs={{0,15},{1,2},{2,1},{3,4},{4,3},{5,6},{6,5},{7,8},{8,7},{9,10},{10,... | collective-permute-start | bytes 147464 | tf_op jit(solution)/shard_map/ppermute | solution.py:477
  31.5 0.0 collective-permute-start.11
  31.5 0.0 collective-permute-done.9
  31.5 0.0 collective-permute-done.8
  31.5 0.0 collective-permute-done.7
  31.5 1.7 %collective-permute-start.10 = (bf16[192,128]{1,0:T(8,128)(2,1)S(1)}, bf16[192,128]{1,0:T(8,128)(2,1)S(1)}, u32[]{:S(2)}, u32[]{:S(2)}) collective-permute-start(bf16[192,128]{1,0:T(8,128)(2,1)S(1)} %add_convert_fusion), channel_id=1, source_target_pairs={{0,8},{1,9},{2,10},{3,11},{4,12},{5,13},{6,14},{7,15},{8,0},{9,1},... | collective-permute-start | bytes 147464 | tf_op jit(solution)/shard_map/ppermute | solution.py:585
  33.2 1.0 %collective-permute-done.12.gh_b = f32[24,512]{1,0:T(8,128)S(1)} collective-permute-done((f32[24,512]{1,0:T(8,128)S(1)}, f32[24,512]{1,0:T(8,128)S(1)}, u32[]{:S(2)}, u32[]{:S(2)}) %collective-permute-start.12) | collective-permute-done | bytes 49184 | tf_op jit(solution)/shard_map/ppermute | solution.py:477
  34.2 0.0 collective-permute-done.11.gh_a
  34.2 0.8 %shard_map.117 = f32[2,8,512]{2,1,0:T(8,128)} custom-call(f32[24,512]{1,0:T(8,128)S(1)} %shard_map.116.gh, f32[24,512]{1,0:T(8,128)S(1)} %collective-permute-done.11.gh_a, f32[24,512]{1,0:T(8,128)S(1)} %collective-permute-done.12.gh_b, f32[2,24,512]{2,1,0:T(8,128)S(1)} %get-tuple-element.52.u), custom_call_target="tpu_custom_call" | custom-call | flops 100000000 | bytes 2000000 | tf_op jit(solution)/shard_map/pallas_call | solution.py:452
  35.0 2.2 %collective-permute-done.10 = bf16[192,128]{1,0:T(8,128)(2,1)S(1)} collective-permute-done((bf16[192,128]{1,0:T(8,128)(2,1)S(1)}, bf16[192,128]{1,0:T(8,128)(2,1)S(1)}, u32[]{:S(2)}, u32[]{:S(2)}) %collective-permute-start.10) | collective-permute-done | bytes 49184 | tf_op jit(solution)/shard_map/ppermute | solution.py:585
  37.2 0.1 collective-permute-start.13
  37.3 1.3 %collective-permute-done.13.other = f32[192,128]{1,0:T(8,128)S(1)} collective-permute-done((f32[192,128]{1,0:T(8,128)S(1)}, f32[192,128]{1,0:T(8,128)S(1)}, u32[]{:S(2)}, u32[]{:S(2)}) %collective-permute-start.13) | collective-permute-done | bytes 98336 | tf_op jit(solution)/shard_map/ppermute | solution.py:592
  38.6 1.0 %shard_map.118 = (f32[9,2,48]{2,1,0:T(2,128)}, f32[9,48,48]{2,1,0:T(8,128)}, f32[9,48,48]{2,1,0:T(8,128)}, f32[9,2,48]{2,1,0:T(2,128)}) custom-call(f32[192,128]{1,0:T(8,128)S(1)} %convert_add_fusion.mine, f32[192,128]{1,0:T(8,128)S(1)} %collective-permute-done.13.other), custom_call_target="tpu_custom_call" | custom-call | flops 100000000 | bytes 2000000 | tf_op jit(solution)/shard_map/pallas_call | solution.py:452
  (3 shorter events, 0.1 us)
Async XLA Ops:
  0.6 8.1 %copy-start = (bf16[2,3,8,48,512]{4,3,2,1,0:T(8,128)(2,1)S(1)}, bf16[2,3,8,48,512]{4,3,2,1,0:T(8,128)(2,1)}, u32[]{:S(2)}) copy-start(bf16[2,3,8,48,512]{4,3,2,1,0:T(8,128)(2,1)} %pre.5) | copy-start | bytes 7077892
  0.6 10.2 %copy-start.6 = (bf16[9,48,2]{1,2,0:T(2,128)(2,1)S(1)}, bf16[9,48,2]{1,2,0:T(2,128)(2,1)}, u32[]{:S(2)}) copy-start(bf16[9,48,2]{1,2,0:T(2,128)(2,1)} %param.10) | copy-start | bytes 5188
  0.7 11.3 %copy-start.3 = (f32[2,8,512]{2,1,0:T(8,128)S(1)}, f32[2,8,512]{2,1,0:T(8,128)}, u32[]{:S(2)}) copy-start(f32[2,8,512]{2,1,0:T(8,128)} %cot.1) | copy-start | bytes 98308
  2.5 8.7 %collective-permute-start = (bf16[160,512]{1,0:T(8,128)(2,1)}, bf16[160,512]{1,0:T(8,128)(2,1)S(1)}, u32[]{:S(2)}, u32[]{:S(2)}) collective-permute-start(bf16[160,512]{1,0:T(8,128)(2,1)} %get-tuple-element.32), channel_id=1, source_target_pairs={{0,1},{1,0},{2,3},{3,2},{4,5},{5,4},{6,7},{7,6},{8,9},{9,8},{10,11... | collective-permute-start | bytes 491528 | tf_op jit(solution)/shard_map/ppermute | solution.py:478
  3.1 8.8 %collective-permute-start.1 = (bf16[160,512]{1,0:T(8,128)(2,1)}, bf16[160,512]{1,0:T(8,128)(2,1)S(1)}, u32[]{:S(2)}, u32[]{:S(2)}) collective-permute-start(bf16[160,512]{1,0:T(8,128)(2,1)} %get-tuple-element.33), channel_id=1, source_target_pairs={{0,15},{1,2},{2,1},{3,4},{4,3},{5,6},{6,5},{7,8},{8,7},{9,10},{10,... | collective-permute-start | bytes 491528 | tf_op jit(solution)/shard_map/ppermute | solution.py:477
  8.7 0.8 %copy-start.1 = (f32[2,2,8,512]{3,2,1,0:T(8,128)S(1)}, f32[2,2,8,512]{3,2,1,0:T(8,128)}, u32[]{:S(2)}) copy-start(f32[2,2,8,512]{3,2,1,0:T(8,128)} %states.1) | copy-start | bytes 196612
  9.6 1.3 %copy-start.4 = (bf16[9,48,48]{2,1,0:T(8,128)(2,1)S(1)}, bf16[9,48,48]{2,1,0:T(8,128)(2,1)}, u32[]{:S(2)}) copy-start(bf16[9,48,48]{2,1,0:T(8,128)(2,1)} %w2.1) | copy-start | bytes 124420
  9.6 1.3 %copy-start.5 = (bf16[9,48,48]{2,1,0:T(8,128)(2,1)S(1)}, bf16[9,48,48]{2,1,0:T(8,128)(2,1)}, u32[]{:S(2)}) copy-start(bf16[9,48,48]{2,1,0:T(8,128)(2,1)} %w3.1) | copy-start | bytes 124420
  9.6 1.3 %copy-start.7 = (bf16[9,2,48]{2,1,0:T(2,128)(2,1)S(1)}, bf16[9,2,48]{2,1,0:T(2,128)(2,1)}, u32[]{:S(2)}) copy-start(bf16[9,2,48]{2,1,0:T(2,128)(2,1)} %w4.1) | copy-start | bytes 5188
  10.1 8.1 %collective-permute-start.4 = (bf16[208,512]{1,0:T(8,128)(2,1)S(1)}, bf16[208,512]{1,0:T(8,128)(2,1)S(1)}, u32[]{:S(2)}, u32[]{:S(2)}) collective-permute-start(bf16[208,512]{1,0:T(8,128)(2,1)S(1)} %get-tuple-element.43), channel_id=1, source_target_pairs={{0,1},{1,0},{2,3},{3,2},{4,5},{5,4},{6,7},{7,6},{8,9},{9,8},{10,11... | collective-permute-start | bytes 638984 | tf_op jit(solution)/shard_map/ppermute | solution.py:478
  10.2 8.1 %collective-permute-start.5 = (bf16[208,512]{1,0:T(8,128)(2,1)S(1)}, bf16[208,512]{1,0:T(8,128)(2,1)S(1)}, u32[]{:S(2)}, u32[]{:S(2)}) collective-permute-start(bf16[208,512]{1,0:T(8,128)(2,1)S(1)} %get-tuple-element.44), channel_id=1, source_target_pairs={{0,15},{1,2},{2,1},{3,4},{4,3},{5,6},{6,5},{7,8},{8,7},{9,10},{10,... | collective-permute-start | bytes 638984 | tf_op jit(solution)/shard_map/ppermute | solution.py:477
  10.8 7.5 %copy-start.2 = (f32[2,2,8,512]{3,2,1,0:T(8,128)S(1)}, f32[2,2,8,512]{3,2,1,0:T(8,128)}, u32[]{:S(2)}) copy-start(f32[2,2,8,512]{3,2,1,0:T(8,128)} %states.1) | copy-start | bytes 196612
  13.6 6.4 %collective-permute-start.3 = (f32[24,512]{1,0:T(8,128)S(1)}, f32[24,512]{1,0:T(8,128)S(1)}, u32[]{:S(2)}, u32[]{:S(2)}) collective-permute-start(f32[24,512]{1,0:T(8,128)S(1)} %get-tuple-element.38.gh), channel_id=1, source_target_pairs={{0,15},{1,2},{2,1},{3,4},{4,3},{5,6},{6,5},{7,8},{8,7},{9,10},{10,... | collective-permute-start | bytes 147464 | tf_op jit(solution)/shard_map/ppermute | solution.py:477
  18.2 1.8 %collective-permute-start.2 = (f32[24,512]{1,0:T(8,128)S(1)}, f32[24,512]{1,0:T(8,128)S(1)}, u32[]{:S(2)}, u32[]{:S(2)}) collective-permute-start(f32[24,512]{1,0:T(8,128)S(1)} %get-tuple-element.38.gh), channel_id=1, source_target_pairs={{0,1},{1,0},{2,3},{3,2},{4,5},{5,4},{6,7},{7,6},{8,9},{9,8},{10,11... | collective-permute-start | bytes 147464 | tf_op jit(solution)/shard_map/ppermute | solution.py:478
  22.6 1.3 %collective-permute-start.6 = (bf16[192,128]{1,0:T(8,128)(2,1)S(1)}, bf16[192,128]{1,0:T(8,128)(2,1)S(1)}, u32[]{:S(2)}, u32[]{:S(2)}) collective-permute-start(bf16[192,128]{1,0:T(8,128)(2,1)S(1)} %get-tuple-element.49), channel_id=1, source_target_pairs={{0,1},{1,0},{2,3},{3,2},{4,5},{5,4},{6,7},{7,6},{8,9},{9,8},{10,11... | collective-permute-start | bytes 147464 | tf_op jit(solution)/shard_map/ppermute | solution.py:578
  23.9 7.6 %collective-permute-start.9 = (bf16[192,128]{1,0:T(8,128)(2,1)S(1)}, bf16[192,128]{1,0:T(8,128)(2,1)S(1)}, u32[]{:S(2)}, u32[]{:S(2)}) collective-permute-start(bf16[192,128]{1,0:T(8,128)(2,1)S(1)} %add_convert_fusion.1), channel_id=1, source_target_pairs={{0,6},{1,7},{2,4},{3,5},{4,2},{5,3},{6,0},{7,1},{8,14},{9,15},{10,... | collective-permute-start | bytes 147464 | tf_op jit(solution)/shard_map/ppermute | solution.py:585
  24.0 7.5 %collective-permute-start.8 = (bf16[192,128]{1,0:T(8,128)(2,1)S(1)}, bf16[192,128]{1,0:T(8,128)(2,1)S(1)}, u32[]{:S(2)}, u32[]{:S(2)}) collective-permute-start(bf16[192,128]{1,0:T(8,128)(2,1)S(1)} %add_convert_fusion.1), channel_id=1, source_target_pairs={{0,4},{1,5},{2,6},{3,7},{4,0},{5,1},{6,2},{7,3},{8,12},{9,13},{10,... | collective-permute-start | bytes 147464 | tf_op jit(solution)/shard_map/ppermute | solution.py:585
  24.4 7.1 %collective-permute-start.7 = (bf16[192,128]{1,0:T(8,128)(2,1)S(1)}, bf16[192,128]{1,0:T(8,128)(2,1)S(1)}, u32[]{:S(2)}, u32[]{:S(2)}) collective-permute-start(bf16[192,128]{1,0:T(8,128)(2,1)S(1)} %add_convert_fusion.1), channel_id=1, source_target_pairs={{0,2},{1,3},{2,0},{3,1},{4,6},{5,7},{6,4},{7,5},{8,10},{9,11},{10,... | collective-permute-start | bytes 147464 | tf_op jit(solution)/shard_map/ppermute | solution.py:585
  27.8 6.4 %collective-permute-start.12 = (f32[24,512]{1,0:T(8,128)S(1)}, f32[24,512]{1,0:T(8,128)S(1)}, u32[]{:S(2)}, u32[]{:S(2)}) collective-permute-start(f32[24,512]{1,0:T(8,128)S(1)} %shard_map.116.gh), channel_id=1, source_target_pairs={{0,15},{1,2},{2,1},{3,4},{4,3},{5,6},{6,5},{7,8},{8,7},{9,10},{10,... | collective-permute-start | bytes 147464 | tf_op jit(solution)/shard_map/ppermute | solution.py:477
  31.5 2.7 %collective-permute-start.11 = (f32[24,512]{1,0:T(8,128)S(1)}, f32[24,512]{1,0:T(8,128)S(1)}, u32[]{:S(2)}, u32[]{:S(2)}) collective-permute-start(f32[24,512]{1,0:T(8,128)S(1)} %shard_map.116.gh), channel_id=1, source_target_pairs={{0,1},{1,0},{2,3},{3,2},{4,5},{5,4},{6,7},{7,6},{8,9},{9,8},{10,11... | collective-permute-start | bytes 147464 | tf_op jit(solution)/shard_map/ppermute | solution.py:478
  31.5 5.6 %collective-permute-start.10 = (bf16[192,128]{1,0:T(8,128)(2,1)S(1)}, bf16[192,128]{1,0:T(8,128)(2,1)S(1)}, u32[]{:S(2)}, u32[]{:S(2)}) collective-permute-start(bf16[192,128]{1,0:T(8,128)(2,1)S(1)} %add_convert_fusion), channel_id=1, source_target_pairs={{0,8},{1,9},{2,10},{3,11},{4,12},{5,13},{6,14},{7,15},{8,0},{9,1},... | collective-permute-start | bytes 147464 | tf_op jit(solution)/shard_map/ppermute | solution.py:585
  37.2 1.4 %collective-permute-start.13 = (f32[192,128]{1,0:T(8,128)S(1)}, f32[192,128]{1,0:T(8,128)S(1)}, u32[]{:S(2)}, u32[]{:S(2)}) collective-permute-start(f32[192,128]{1,0:T(8,128)S(1)} %convert_add_fusion.mine), channel_id=1, source_target_pairs={{0,1},{1,0},{2,3},{3,2},{4,5},{5,4},{6,7},{7,6},{8,9},{9,8},{10,11... | collective-permute-start | bytes 294920 | tf_op jit(solution)/shard_map/ppermute | solution.py:592
